TPU v7x, 512 devices: a whole 4x8x8 slice. The times are simulated.
512 devices in a mesh: dp: 16 (over z, core), mp: 8 (over y), expert: 4 (over x).
Axes of the slice: x: 4, y: 8, z: 8, core: 2. Of those that a mesh axis runs over, the one named last changes fastest.
Arguments:
- attn_out: bfloat16 [16384, 2304], P('dp', 'mp'), may hold values from -6 to 6
- residual: float32 [16384, 2304], P(('dp', 'mp', 'expert'))
- proj_weight: bfloat16 [2304, 2304], P('mp'), may hold values from -0.125 to 0.125
- norm_gain: float32 [2304], replicated, may hold values from 0.1 to 1.9
- gate_weight: bfloat16 [8, 2304, 4096], P('mp', None, 'expert'), may hold values from -0.125 to 0.125
- up_weight: bfloat16 [8, 2304, 4096], P('mp', None, 'expert'), may hold values from -0.125 to 0.125
- down_weight: bfloat16 [8, 4096, 2304], P('mp', 'expert'), may hold values from -0.09375 to 0.09375
- routes: int32 [16384, 2], P(('dp', 'mp', 'expert')), may hold values from 0 to 7, as said below
- route_weights: float32 [16384, 2], P(('dp', 'mp', 'expert')), may hold values from 0.2 to 1
Outputs:
- mixed: float32 [16384, 2304], P(('dp', 'mp', 'expert'))
Inputs may be any that keep to these rules, and one draw needn't show every extreme that they name: `routes`: the two ids of a row differ. In the rows of each device (aligned blocks of 32 rows, in order) every expert is named by at most 16 rows; one expert, the same in all blocks, is named by exactly 16 rows in every block, and the other 48 names of a block are spread as evenly as possible over the other experts.
All inputs are finite; a program needn't handle non-finite values.
Results may differ from a plain program's by a relative error of at most 0.0015.
Values may be sent and summed in bfloat16 or wider, within the bound.
No kernel may reach another device: no remote copies, remote signals or barrier semaphores. Data moves between devices by JAX's collectives and lax.ppermute only.
A program may use at most 64 MiB of HBM per device.

v0:
```python
import jax
import jax.numpy as jnp
from jax import lax
from jax.sharding import PartitionSpec as P

EXPERTS = 8
MOST = 16


EPSILON = 1e-06


def body(
    attn_out,
    residual,
    proj_weight,
    norm_gain,
    gate_weight,
    up_weight,
    down_weight,
    routes,
    route_weights,
):
    model_parts = lax.axis_size("mp")
    unit_parts = lax.axis_size("expert")
    row_count = residual.shape[0]
    features = residual.shape[1]
    local_experts = gate_weight.shape[0]
    sources = model_parts * unit_parts
    blocks = attn_out.reshape(model_parts, unit_parts, row_count, attn_out.shape[1])
    picked = lax.dynamic_index_in_dim(blocks, lax.axis_index("expert"), axis=1, keepdims=False)
    picked = picked.reshape(model_parts * row_count, attn_out.shape[1])
    projected = lax.psum_scatter(
        jnp.dot(picked, proj_weight, preferred_element_type=jnp.float32),
        "mp",
        scatter_dimension=0,
        tiled=True,
    )
    hidden_state = residual + projected
    inverse_rms = lax.rsqrt(jnp.mean(hidden_state * hidden_state, axis=1, keepdims=True) + EPSILON)
    normed = (hidden_state * inverse_rms * norm_gain).astype(jnp.bfloat16)
    expert_ids = routes.reshape(-1)
    onehot = (expert_ids[:, None] == jnp.arange(EXPERTS, dtype=jnp.int32)[None, :]).astype(
        jnp.int32
    )
    before = jnp.cumsum(onehot, axis=0) - onehot
    position = jnp.sum(before * onehot, axis=1)
    target = expert_ids * MOST + position
    placement = (jnp.arange(EXPERTS * MOST, dtype=jnp.int32)[:, None] == target[None, :]).astype(
        jnp.bfloat16
    )
    doubled = jnp.repeat(normed, 2, axis=0)
    outgoing = jnp.dot(placement, doubled, preferred_element_type=jnp.float32).astype(jnp.bfloat16)
    outgoing = outgoing.reshape(model_parts, local_experts, MOST, features)
    copies = jnp.broadcast_to(
        outgoing[:, None], (model_parts, unit_parts, local_experts, MOST, features)
    )
    copies = copies.reshape(sources, local_experts, MOST, features)
    arrived = lax.all_to_all(copies, ("mp", "expert"), split_axis=0, concat_axis=0, tiled=True)
    gate_part = jnp.einsum(
        "qemd,edf->qemf", arrived, gate_weight, preferred_element_type=jnp.float32
    )
    up_part = jnp.einsum("qemd,edf->qemf", arrived, up_weight, preferred_element_type=jnp.float32)
    activation = (jax.nn.silu(gate_part) * up_part).astype(jnp.bfloat16)
    partial_value = jnp.einsum(
        "qemf,efd->qemd", activation, down_weight, preferred_element_type=jnp.float32
    ).astype(jnp.bfloat16)
    returned = lax.all_to_all(
        partial_value, ("mp", "expert"), split_axis=0, concat_axis=0, tiled=True
    )
    returned = returned.reshape(model_parts, unit_parts, local_experts, MOST, features)
    outputs = jnp.sum(returned, axis=1, dtype=jnp.float32).astype(jnp.bfloat16)
    expert_out = outputs.reshape(EXPERTS * MOST, features)
    gathered_back = jnp.dot(placement.T, expert_out, preferred_element_type=jnp.float32)
    gathered_back = gathered_back.reshape(row_count, 2, features)
    return (
        hidden_state
        + route_weights[:, 0:1] * gathered_back[:, 0]
        + route_weights[:, 1:2] * gathered_back[:, 1]
    )


def solution(mesh):
    in_specs = (
        P("dp", "mp"),
        P(("dp", "mp", "expert"), None),
        P("mp", None),
        P(),
        P("mp", None, "expert"),
        P("mp", None, "expert"),
        P("mp", "expert", None),
        P(("dp", "mp", "expert"), None),
        P(("dp", "mp", "expert"), None),
    )
    out_specs = P(("dp", "mp", "expert"), None)
    return jax.shard_map(body, mesh=mesh, in_specs=in_specs, out_specs=out_specs, check_vma=False)
```

profile of v0, /device:TPU:4, one launch (start us, length us, event | category | flops | bytes accessed | tf_op | source)
XLA Modules:
  0.0 210.3 jit_solution(8283306659121290336)
XLA Ops:
  6.5 0.0 copy-start
  6.5 0.0 reduce-scatter.2.cloned.1.call-start
  6.5 1.5 copy.14
  8.1 0.0 copy-done
  8.1 0.0 copy-start.4
  8.1 0.0 copy-start.2
  8.1 2.2 %fusion.40 = f32[256,2304]{1,0:T(8,128)} fusion(bf16[256,288]{1,0:T(8,128)(2,1)S(1)} %bitcast.114, bf16[288,2304]{1,0:T(8,128)(2,1)S(1)} %copy-done), kind=kOutput, calls=%fused_computation.42 | convolution fusion | flops 339738624 | bytes 3833856 | tf_op jit(solution)/shard_map/dot_general | solution.py:34
  10.3 0.0 copy-start.3
  10.3 0.0 reduce-scatter.2.cloned.1.call-update
  10.4 0.0 copy-done.4
  10.4 0.1 copy.15
  10.5 0.1 reshape.94
  10.6 0.1 fusion.36
  10.6 0.1 reduce_window_sum.11
  10.7 0.2 select_reduce_fusion
  10.9 49.6 %reduce-scatter.2.cloned.1.call-done = f32[32,2304]{1,0:T(8,128)} async-done(((f32[256,2304]{1,0:T(8,128)}), f32[32,2304]{1,0:T(8,128)}) %reduce-scatter.2.cloned.1.call-update) | async-done | bytes 294928 | tf_op jit(solution)/shard_map/reduce_scatter | solution.py:33
  60.6 0.0 copy-done.2
  60.6 1.1 multiply_reduce_fusion
  61.7 0.0 copy-done.3
  61.7 0.1 multiply_convert_fusion
  61.8 0.2 broadcast_in_dim.8
  61.9 0.1 reshape.95
  62.1 0.3 convolution_convert_fusion
  62.4 0.2 broadcast_in_dim.19
  62.6 60.6 %all_to_all.10 = bf16[32,1,16,2304]{3,2,1,0:T(8,128)(2,1)S(1)} all-to-all(bf16[32,1,16,2304]{3,2,1,0:T(8,128)(2,1)S(1)} %bitcast.110), channel_id=1, replica_groups=mesh['dp'=16,'mp'=8,'expert'=4] {'mp','expert'}, dimensions={0} | all-to-all | bytes 4718592 | tf_op jit(solution)/shard_map/all_to_all | solution.py:59
  123.2 0.0 copy-start.1
  123.2 1.4 copy-done.1
  124.6 6.4 %fusion.4 = f32[32,16,1024]{2,1,0:T(8,128)} fusion(bf16[1,2304,1024]{2,1,0:T(8,128)(2,1)} %param.13, bf16[32,1,16,2304]{3,2,1,0:T(8,128)(2,1)S(1)} %all_to_all.10), kind=kOutput, calls=%fused_computation.4 | convolution fusion | flops 2415919104 | bytes 9175040 | tf_op jit(solution)/shard_map/qemd,edf->qemf/dot_general | solution.py:60
  131.0 11.6 %fusion.9 = bf16[32,1,16,2304]{3,2,1,0:T(8,128)(2,1)} fusion(bf16[1,1024,2304]{2,1,0:T(8,128)(2,1)} %param.15, bf16[1,2304,1024]{2,1,0:T(8,128)(2,1)} %param.14, bf16[32,1,16,2304]{3,2,1,0:T(8,128)(2,1)} %copy-done.1, f32[32,16,1024]{2,1,0:T(8,128)} %fusion.4), kind=kOutput, calls=%fused_computation.7 | convolution fusion | flops 4836163584 | bytes 16252928 | tf_op jit(solution)/shard_map/qemf,efd->qemd/dot_general | solution.py:65
  142.6 0.0 copy-start.5
  142.6 6.5 %all-to-all-start.1 = ((bf16[32,1,16,2304]{3,2,1,0:T(8,128)(2,1)}), bf16[32,1,16,2304]{3,2,1,0:T(8,128)(2,1)}, u32[]{:S(2)}, u32[]{:S(2)}) async-start(bf16[32,1,16,2304]{3,2,1,0:T(8,128)(2,1)} %fusion.9), calls=%async_computation.2 | async-start | bytes 4718592 | tf_op jit(solution)/shard_map/all_to_all | solution.py:68
  149.1 0.1 iota_compare_fusion.3
  149.2 0.0 copy-done.5
  149.2 51.2 %all-to-all-done.1 = bf16[32,1,16,2304]{3,2,1,0:T(8,128)(2,1)} async-done(((bf16[32,1,16,2304]{3,2,1,0:T(8,128)(2,1)}), bf16[32,1,16,2304]{3,2,1,0:T(8,128)(2,1)}, u32[]{:S(2)}, u32[]{:S(2)}) %all-to-all-start.1) | async-done | bytes 2359328 | tf_op jit(solution)/shard_map/all_to_all | solution.py:68
  200.4 2.0 bitcast_reduce_fusion
  202.4 0.2 fusion.37
  202.6 0.8 fusion.32
  (5 shorter events, 0.1 us)
Async XLA Ops:
  6.5 1.6 copy-start
  6.5 54.0 %reduce-scatter.2.cloned.1.call-start = ((), (), s32[]{:S(2)}) async-start(), calls=%async_computation.3 | async-start | bytes 2654208 | tf_op jit(solution)/shard_map/reduce_scatter | solution.py:33
  8.1 2.2 %copy-start.4 = (s32[32,2]{0,1:T(2,128)S(1)}, s32[32,2]{0,1:T(2,128)}, u32[]{:S(2)}) copy-start(s32[32,2]{0,1:T(2,128)} %param.16) | copy-start | bytes 772
  8.1 52.4 %copy-start.2 = (f32[32,2304]{1,0:T(8,128)S(1)}, f32[32,2304]{1,0:T(8,128)}, u32[]{:S(2)}) copy-start(f32[32,2304]{1,0:T(8,128)} %param.10) | copy-start | bytes 884740
  10.3 51.3 %copy-start.3 = (f32[2304]{0:T(1024)S(1)}, f32[2304]{0:T(1024)}, u32[]{:S(2)}) copy-start(f32[2304]{0:T(1024)} %param.12) | copy-start | bytes 27652
  123.2 1.4 copy-start.1
  142.6 6.6 %copy-start.5 = (f32[32,2]{0,1:T(2,128)S(1)}, f32[32,2]{0,1:T(2,128)}, u32[]{:S(2)}) copy-start(f32[32,2]{0,1:T(2,128)} %param.17) | copy-start | bytes 772
  142.6 57.8 %all-to-all-start.1 = ((bf16[32,1,16,2304]{3,2,1,0:T(8,128)(2,1)}), bf16[32,1,16,2304]{3,2,1,0:T(8,128)(2,1)}, u32[]{:S(2)}, u32[]{:S(2)}) async-start(bf16[32,1,16,2304]{3,2,1,0:T(8,128)(2,1)} %fusion.9), calls=%async_computation.2 | async-start | bytes 4718592 | tf_op jit(solution)/shard_map/all_to_all | solution.py:68
Sparse Core Ops, SparseCore 0:
  10.5 50.0 reduce-scatter.1
where the time goes:
time: 211 us; the launch traced here: 210 us
  waiting for transfers between devices  101 us (48%)
  blocking collectives  60.6 us (29%)
  matrix products  20.7 us (10%)
  between operations  13.5 us (6%)
  starting transfers between devices  6.48 us (3%)
  other arithmetic  4.47 us (2%)
  local copies, waits for them, and re-layouts  3.62 us (2%)
    all_to_all x1, blocking collectives, body(): lax.all_to_all(copies, ('mp', 'expert'), split_axis=0, concat_axis=0, til...  60.6 us
    all_to_all x1, waiting for transfers between devices, body(): lax.all_to_all(partial_value, ('mp', 'expert'), split_axis=0, concat_axis...  51.2 us
    reduce_scatter x1, waiting for transfers between devices, body(): lax.psum_scatter(jnp.dot(picked, proj_weight, preferred_element_type=jnp....  49.6 us
    dot_general x1, matrix products, body(): jnp.einsum('qemf,efd->qemd', activation, down_weight, preferred_element_t...  11.6 us
    all_to_all x1, starting transfers between devices, body(): lax.all_to_all(partial_value, ('mp', 'expert'), split_axis=0, concat_axis...  6.48 us
    dot_general x1, matrix products, body(): jnp.einsum('qemd,edf->qemf', arrived, gate_weight, preferred_element_type...  6.37 us
  transfers between devices with their start and end apart: 2, of which 2 were waited for; matrix products, arithmetic and copies ran while one was open for 0% of the time, Pallas kernels for 0%

commit v1 on v0

v1 whole, which is shorter than its diff:
```python
import jax
import jax.numpy as jnp
from jax import lax
from jax.experimental import pallas as pl
from jax.experimental.pallas import tpu as pltpu
from jax.sharding import PartitionSpec as P

EXPERTS = 8
MOST = 16
EPSILON = 1e-06

UP_CHUNK = 256
DOWN_CHUNK = 768


def ffn_kernel(x_ref, gate_ref, up_ref, down_ref, out_ref, act_ref):
    step = pl.program_id(0)
    up_steps = act_ref.shape[0]

    @pl.when(step < up_steps)
    def _():
        rows = x_ref[...]
        gate = jnp.dot(rows, gate_ref[...], preferred_element_type=jnp.float32)
        up = jnp.dot(rows, up_ref[...], preferred_element_type=jnp.float32)
        act_ref[step] = (gate / (1.0 + jnp.exp(-gate)) * up).astype(jnp.bfloat16)

    @pl.when(step >= up_steps)
    def _():
        total = jnp.dot(act_ref[0], down_ref[0], preferred_element_type=jnp.float32)
        for part in range(1, up_steps):
            total += jnp.dot(act_ref[part], down_ref[part], preferred_element_type=jnp.float32)
        out_ref[...] = total.astype(jnp.bfloat16)


def ffn(rows, gate_weight, up_weight, down_weight):
    count, features = rows.shape
    units = gate_weight.shape[1]
    up_steps = units // UP_CHUNK
    down_steps = features // DOWN_CHUNK
    return pl.pallas_call(
        ffn_kernel,
        out_shape=jax.ShapeDtypeStruct((count, features), jnp.bfloat16),
        grid=(up_steps + down_steps,),
        in_specs=[
            pl.BlockSpec((count, features), lambda i: (0, 0)),
            pl.BlockSpec((features, UP_CHUNK), lambda i: (0, jnp.minimum(i, up_steps - 1))),
            pl.BlockSpec((features, UP_CHUNK), lambda i: (0, jnp.minimum(i, up_steps - 1))),
            pl.BlockSpec(
                (up_steps, UP_CHUNK, DOWN_CHUNK), lambda i: (0, 0, jnp.maximum(i - up_steps, 0))
            ),
        ],
        out_specs=pl.BlockSpec((count, DOWN_CHUNK), lambda i: (0, jnp.maximum(i - up_steps, 0))),
        scratch_shapes=[pltpu.VMEM((up_steps, count, UP_CHUNK), jnp.bfloat16)],
        compiler_params=pltpu.CompilerParams(vmem_limit_bytes=40 << 20),
    )(rows, gate_weight, up_weight, down_weight.reshape(up_steps, UP_CHUNK, features))


def body(
    attn_out,
    residual,
    proj_weight,
    norm_gain,
    gate_weight,
    up_weight,
    down_weight,
    routes,
    route_weights,
):
    model_parts = lax.axis_size("mp")
    unit_parts = lax.axis_size("expert")
    row_count = residual.shape[0]
    features = residual.shape[1]
    blocks = attn_out.reshape(model_parts, unit_parts, row_count, attn_out.shape[1])
    picked = lax.dynamic_index_in_dim(blocks, lax.axis_index("expert"), axis=1, keepdims=False)
    picked = picked.reshape(model_parts * row_count, attn_out.shape[1])
    parts = jnp.dot(picked, proj_weight, preferred_element_type=jnp.float32).astype(jnp.bfloat16)
    parts = parts.reshape(model_parts, row_count, features)
    parts = lax.all_to_all(parts, "mp", split_axis=0, concat_axis=0, tiled=True)
    hidden_state = residual + jnp.sum(parts, axis=0, dtype=jnp.float32)
    inverse_rms = lax.rsqrt(jnp.mean(hidden_state * hidden_state, axis=1, keepdims=True) + EPSILON)
    normed = (hidden_state * inverse_rms * norm_gain).astype(jnp.bfloat16)
    expert_ids = routes.reshape(-1)
    onehot = (expert_ids[:, None] == jnp.arange(EXPERTS, dtype=jnp.int32)[None, :]).astype(
        jnp.int32
    )
    before = jnp.cumsum(onehot, axis=0) - onehot
    position = jnp.sum(before * onehot, axis=1)
    target = (expert_ids * MOST + position).reshape(row_count, 2)
    slots = jnp.arange(EXPERTS * MOST, dtype=jnp.int32)
    first = target[:, 0][:, None] == slots[None, :]
    second = target[:, 1][:, None] == slots[None, :]
    placement = (first | second).astype(jnp.bfloat16)
    outgoing = lax.dot_general(
        placement, normed, (((0,), (0,)), ((), ())), preferred_element_type=jnp.float32
    ).astype(jnp.bfloat16)
    outgoing = outgoing.reshape(model_parts, MOST, features)
    arrived = lax.all_to_all(outgoing, "mp", split_axis=0, concat_axis=0, tiled=True)
    copies = jnp.broadcast_to(arrived[None], (unit_parts, model_parts, MOST, features))
    copies = lax.all_to_all(copies, "expert", split_axis=0, concat_axis=0, tiled=True)
    rows = copies.reshape(unit_parts * model_parts * MOST, features)
    partial_value = ffn(rows, gate_weight[0], up_weight[0], down_weight[0])
    partial_value = partial_value.reshape(unit_parts, model_parts, MOST, features)
    returned = lax.all_to_all(partial_value, "expert", split_axis=0, concat_axis=0, tiled=True)
    outputs = jnp.sum(returned, axis=0, dtype=jnp.float32).astype(jnp.bfloat16)
    outputs = lax.all_to_all(outputs, "mp", split_axis=0, concat_axis=0, tiled=True)
    expert_out = outputs.reshape(EXPERTS * MOST, features)
    one = jnp.dot(first.astype(jnp.bfloat16), expert_out, preferred_element_type=jnp.float32)
    two = jnp.dot(second.astype(jnp.bfloat16), expert_out, preferred_element_type=jnp.float32)
    return hidden_state + route_weights[:, 0:1] * one + route_weights[:, 1:2] * two


def solution(mesh):
    in_specs = (
        P("dp", "mp"),
        P(("dp", "mp", "expert"), None),
        P("mp", None),
        P(),
        P("mp", None, "expert"),
        P("mp", None, "expert"),
        P("mp", "expert", None),
        P(("dp", "mp", "expert"), None),
        P(("dp", "mp", "expert"), None),
    )
    out_specs = P(("dp", "mp", "expert"), None)
    return jax.shard_map(body, mesh=mesh, in_specs=in_specs, out_specs=out_specs, check_vma=False)
```

time: 211 us -> 165 us (0.78)
  the two profiles are of different devices: /device:TPU:4 before, /device:TPU:448 now
where the time goes in v1:
time: 165 us; the launch traced here: 164 us
  blocking collectives  85.7 us (52%)
  waiting for transfers between devices  46.7 us (28%)
  Pallas kernels  11.7 us (7%)
  starting transfers between devices  10.8 us (7%)
  other arithmetic  3.65 us (2%)
  matrix products  3.47 us (2%)
  local copies, waits for them, and re-layouts  2.16 us (1%)
    all_to_all x1, blocking collectives, body(): lax.all_to_all(copies, 'expert', split_axis=0, concat_axis=0, tiled=True)  33 us
    all_to_all x1, waiting for transfers between devices, body(): parts = lax.all_to_all(parts, 'mp', split_axis=0, concat_axis=0, tiled=True)  30.8 us
    all_to_all x1, blocking collectives, body(): lax.all_to_all(partial_value, 'expert', split_axis=0, concat_axis=0, tile...  30.7 us
    all_to_all x1, blocking collectives, body(): lax.all_to_all(outgoing, 'mp', split_axis=0, concat_axis=0, tiled=True)  22 us
    all_to_all x1, waiting for transfers between devices, body(): lax.all_to_all(outputs, 'mp', split_axis=0, concat_axis=0, tiled=True)  15.9 us
    pallas_call x1, Pallas kernels, ffn(): pl.pallas_call(ffn_kernel, out_shape=jax.ShapeDtypeStruct((count, feature...  11.7 us
    all_to_all x1, starting transfers between devices, body(): parts = lax.all_to_all(parts, 'mp', split_axis=0, concat_axis=0, tiled=True)  7.23 us
    all_to_all x1, starting transfers between devices, body(): lax.all_to_all(outputs, 'mp', split_axis=0, concat_axis=0, tiled=True)  3.54 us
  transfers between devices with their start and end apart: 2, of which 2 were waited for; matrix products, arithmetic and copies ran while one was open for 0% of the time, Pallas kernels for 0%

profile of v1, /device:TPU:448, one launch (start us, length us, event | category | flops | bytes accessed | tf_op | source)
XLA Modules:
  0.0 164.4 jit_solution(3935390419740043103)
XLA Ops:
  0.0 0.0 copy-start
  0.0 1.5 copy.17
  1.6 0.0 copy-done
  1.6 0.0 copy-start.4
  1.6 1.8 %convolution_convert_fusion = bf16[256,2304]{1,0:T(8,128)(2,1)} fusion(bf16[256,288]{1,0:T(8,128)(2,1)S(1)} %bitcast.34, bf16[288,2304]{1,0:T(8,128)(2,1)S(1)} %copy-done), kind=kOutput, calls=%fused_computation | convolution fusion | flops 340328448 | bytes 2654208 | tf_op jit(solution)/shard_map/dot_general | solution.py:76
  3.4 0.0 copy-start.2
  3.4 0.0 copy-start.3
  3.4 7.2 %all-to-all-start = ((bf16[8,32,2304]{2,1,0:T(8,128)(2,1)}), bf16[8,32,2304]{2,1,0:T(8,128)(2,1)S(1)}, u32[]{:S(2)}, u32[]{:S(2)}) async-start(bf16[8,32,2304]{2,1,0:T(8,128)(2,1)} %bitcast.30), calls=%async_computation | async-start | bytes 2359296 | tf_op jit(solution)/shard_map/all_to_all | solution.py:78
  10.6 0.0 copy-done.4
  10.6 0.1 copy.18
  10.7 0.1 eq.45
  10.8 0.1 fusion.4
  10.9 0.1 reduce_window_sum.11
  11.0 0.2 select_reduce_fusion
  11.2 0.1 reduce_sum.43
  11.3 0.1 copy.19
  11.4 30.8 %all-to-all-done = bf16[8,32,2304]{2,1,0:T(8,128)(2,1)S(1)} async-done(((bf16[8,32,2304]{2,1,0:T(8,128)(2,1)}), bf16[8,32,2304]{2,1,0:T(8,128)(2,1)S(1)}, u32[]{:S(2)}, u32[]{:S(2)}) %all-to-all-start) | async-done | bytes 1179680 | tf_op jit(solution)/shard_map/all_to_all | solution.py:78
  42.2 0.1 convert_reduce_fusion
  42.4 0.0 copy-done.2
  42.4 0.1 multiply_reduce_fusion
  42.5 0.0 copy-done.3
  42.5 0.0 slice-start
  42.6 0.4 convolution_convert_fusion.1
  43.0 22.0 %all_to_all.25 = bf16[8,16,2304]{2,1,0:T(8,128)(2,1)S(1)} all-to-all(bf16[8,16,2304]{2,1,0:T(8,128)(2,1)S(1)} %bitcast.32), channel_id=1, replica_groups=mesh['dp'=16,'mp'=8,'expert'=4] {'mp'}, dimensions={0} | all-to-all | bytes 1179648 | tf_op jit(solution)/shard_map/all_to_all | solution.py:97
  65.0 0.0 slice-start.1
  65.0 0.2 broadcast_in_dim.2
  65.2 0.0 copy-start.1
  65.2 33.0 %all_to_all.26 = bf16[4,8,16,2304]{3,2,1,0:T(8,128)(2,1)S(1)} all-to-all(bf16[4,8,16,2304]{3,2,1,0:T(8,128)(2,1)S(1)} %broadcast_in_dim.2), channel_id=1, replica_groups=mesh['dp'=16,'mp'=8,'expert'=4] {'expert'}, dimensions={0} | all-to-all | bytes 4718592 | tf_op jit(solution)/shard_map/all_to_all | solution.py:99
  98.2 0.0 slice-done
  98.2 0.0 slice-done.1
  98.2 0.0 copy-done.1
  98.2 11.7 %shard_map.91 = bf16[512,2304]{1,0:T(8,128)(2,1)S(1)} custom-call(bf16[512,2304]{1,0:T(8,128)(2,1)S(1)} %bitcast.22, bf16[2304,1024]{1,0:T(8,128)(2,1)S(1)} %bitcast.26, bf16[2304,1024]{1,0:T(8,128)(2,1)S(1)} %bitcast.27, bf16[4,256,2304]{2,1,0:T(8,128)(2,1)} %bitcast.31), custom_call_target="tpu_custom_call" | custom-call | tf_op jit(solution)/shard_map/pallas_call | solution.py:40
  109.9 30.7 %all_to_all.27 = bf16[4,8,16,2304]{3,2,1,0:T(8,128)(2,1)} all-to-all(bf16[4,8,16,2304]{3,2,1,0:T(8,128)(2,1)S(1)} %bitcast.23), channel_id=1, replica_groups=mesh['dp'=16,'mp'=8,'expert'=4] {'expert'}, dimensions={0} | all-to-all | bytes 4718592 | tf_op jit(solution)/shard_map/all_to_all | solution.py:103
  140.7 0.0 copy-start.5
  140.7 3.0 %reduce_sum.45 = bf16[8,16,2304]{2,1,0:T(8,128)(2,1)} reduce(bf16[4,8,16,2304]{3,2,1,0:T(8,128)(2,1)} %all_to_all.27, bf16[]{:T(256)} %constant.25.clone.1), dimensions={0}, to_apply=%region_4.5 | reduce | flops 884736 | bytes 2949122 | tf_op jit(solution)/shard_map/reduce_sum | solution.py:104
  143.6 3.5 %all-to-all-start.4 = ((bf16[8,16,2304]{2,1,0:T(8,128)(2,1)}), bf16[8,16,2304]{2,1,0:T(8,128)(2,1)S(1)}, u32[]{:S(2)}, u32[]{:S(2)}) async-start(bf16[8,16,2304]{2,1,0:T(8,128)(2,1)} %reduce_sum.45), calls=%async_computation.4 | async-start | bytes 1179648 | tf_op jit(solution)/shard_map/all_to_all | solution.py:105
  147.2 0.0 copy-done.5
  147.2 15.9 %all-to-all-done.4 = bf16[8,16,2304]{2,1,0:T(8,128)(2,1)S(1)} async-done(((bf16[8,16,2304]{2,1,0:T(8,128)(2,1)}), bf16[8,16,2304]{2,1,0:T(8,128)(2,1)S(1)}, u32[]{:S(2)}, u32[]{:S(2)}) %all-to-all-start.4) | async-done | bytes 589856 | tf_op jit(solution)/shard_map/all_to_all | solution.py:105
  163.1 0.3 convolution_multiply_fusion
  163.4 1.0 fusion.1
  (6 shorter events, 0.1 us)
Async XLA Ops:
  0.0 1.6 copy-start
  1.6 9.0 %copy-start.4 = (s32[32,2]{0,1:T(2,128)S(1)}, s32[32,2]{0,1:T(2,128)}, u32[]{:S(2)}) copy-start(s32[32,2]{0,1:T(2,128)} %param.16) | copy-start | bytes 772
  3.4 39.0 %copy-start.2 = (f32[32,2304]{1,0:T(8,128)S(1)}, f32[32,2304]{1,0:T(8,128)}, u32[]{:S(2)}) copy-start(f32[32,2304]{1,0:T(8,128)} %param.10) | copy-start | bytes 884740
  3.4 39.1 %copy-start.3 = (f32[2304]{0:T(1024)S(1)}, f32[2304]{0:T(1024)}, u32[]{:S(2)}) copy-start(f32[2304]{0:T(1024)} %param.12) | copy-start | bytes 27652
  3.4 38.8 %all-to-all-start = ((bf16[8,32,2304]{2,1,0:T(8,128)(2,1)}), bf16[8,32,2304]{2,1,0:T(8,128)(2,1)S(1)}, u32[]{:S(2)}, u32[]{:S(2)}) async-start(bf16[8,32,2304]{2,1,0:T(8,128)(2,1)} %bitcast.30), calls=%async_computation | async-start | bytes 2359296 | tf_op jit(solution)/shard_map/all_to_all | solution.py:78
  42.5 55.7 %slice-start = ((s8[4718592]{0:T(1024)(128)(4,1)}), s8[4194304]{0:T(1024)(128)(4,1)S(1)}, s32[]{:S(2)}) async-start(s8[4718592]{0:T(1024)(128)(4,1)} %bitcast.24), calls=%async_computation.5 | async-start | bytes 8388608
  65.0 33.2 %slice-start.1 = ((s8[4718592]{0:T(1024)(128)(4,1)}), s8[524288]{0:T(1024)(128)(4,1)S(1)}, s32[]{:S(2)}) async-start(s8[4718592]{0:T(1024)(128)(4,1)} %bitcast.24), calls=%async_computation.6 | async-start | bytes 1048576
  65.2 33.0 %copy-start.1 = (bf16[1,2304,1024]{2,1,0:T(8,128)(2,1)S(1)}, bf16[1,2304,1024]{2,1,0:T(8,128)(2,1)}, u32[]{:S(2)}) copy-start(bf16[1,2304,1024]{2,1,0:T(8,128)(2,1)} %param.14) | copy-start | bytes 14155780
  140.7 6.5 %copy-start.5 = (f32[32,2]{0,1:T(2,128)S(1)}, f32[32,2]{0,1:T(2,128)}, u32[]{:S(2)}) copy-start(f32[32,2]{0,1:T(2,128)} %param.17) | copy-start | bytes 772
  143.6 19.5 %all-to-all-start.4 = ((bf16[8,16,2304]{2,1,0:T(8,128)(2,1)}), bf16[8,16,2304]{2,1,0:T(8,128)(2,1)S(1)}, u32[]{:S(2)}, u32[]{:S(2)}) async-start(bf16[8,16,2304]{2,1,0:T(8,128)(2,1)} %reduce_sum.45), calls=%async_computation.4 | async-start | bytes 1179648 | tf_op jit(solution)/shard_map/all_to_all | solution.py:105

commit v2 on v1

--- a/solution.py
+++ b/solution.py
@@ -7,6 +7,7 @@
 
 EXPERTS = 8
 MOST = 16
+PIECES = 2
 EPSILON = 1e-06
 
 UP_CHUNK = 256
@@ -52,7 +53,14 @@
         out_specs=pl.BlockSpec((count, DOWN_CHUNK), lambda i: (0, jnp.maximum(i - up_steps, 0))),
         scratch_shapes=[pltpu.VMEM((up_steps, count, UP_CHUNK), jnp.bfloat16)],
         compiler_params=pltpu.CompilerParams(vmem_limit_bytes=40 << 20),
-    )(rows, gate_weight, up_weight, down_weight.reshape(up_steps, UP_CHUNK, features))
+    )(
+        rows,
+        pltpu.with_memory_space_constraint(gate_weight, pltpu.HBM),
+        pltpu.with_memory_space_constraint(up_weight, pltpu.HBM),
+        pltpu.with_memory_space_constraint(
+            down_weight.reshape(up_steps, UP_CHUNK, features), pltpu.HBM
+        ),
+    )
 
 
 def body(
@@ -73,7 +81,7 @@
     blocks = attn_out.reshape(model_parts, unit_parts, row_count, attn_out.shape[1])
     picked = lax.dynamic_index_in_dim(blocks, lax.axis_index("expert"), axis=1, keepdims=False)
     picked = picked.reshape(model_parts * row_count, attn_out.shape[1])
-    parts = jnp.dot(picked, proj_weight, preferred_element_type=jnp.float32).astype(jnp.bfloat16)
+    parts = jnp.dot(picked, proj_weight, preferred_element_type=jnp.float32).astype(jnp.float16)
     parts = parts.reshape(model_parts, row_count, features)
     parts = lax.all_to_all(parts, "mp", split_axis=0, concat_axis=0, tiled=True)
     hidden_state = residual + jnp.sum(parts, axis=0, dtype=jnp.float32)
@@ -95,13 +103,18 @@
     ).astype(jnp.bfloat16)
     outgoing = outgoing.reshape(model_parts, MOST, features)
     arrived = lax.all_to_all(outgoing, "mp", split_axis=0, concat_axis=0, tiled=True)
-    copies = jnp.broadcast_to(arrived[None], (unit_parts, model_parts, MOST, features))
-    copies = lax.all_to_all(copies, "expert", split_axis=0, concat_axis=0, tiled=True)
-    rows = copies.reshape(unit_parts * model_parts * MOST, features)
-    partial_value = ffn(rows, gate_weight[0], up_weight[0], down_weight[0])
-    partial_value = partial_value.reshape(unit_parts, model_parts, MOST, features)
-    returned = lax.all_to_all(partial_value, "expert", split_axis=0, concat_axis=0, tiled=True)
-    outputs = jnp.sum(returned, axis=0, dtype=jnp.float32).astype(jnp.bfloat16)
+    depth = MOST // PIECES
+    sums = []
+    for piece in range(PIECES):
+        part = arrived[:, piece * depth : (piece + 1) * depth]
+        copies = jnp.broadcast_to(part[None], (unit_parts,) + part.shape)
+        copies = lax.all_to_all(copies, "expert", split_axis=0, concat_axis=0, tiled=True)
+        rows = copies.reshape(-1, features)
+        partial_value = ffn(rows, gate_weight[0], up_weight[0], down_weight[0])
+        partial_value = partial_value.reshape(copies.shape)
+        returned = lax.all_to_all(partial_value, "expert", split_axis=0, concat_axis=0, tiled=True)
+        sums.append(jnp.sum(returned, axis=0, dtype=jnp.float32).astype(jnp.bfloat16))
+    outputs = jnp.concatenate(sums, axis=1)
     outputs = lax.all_to_all(outputs, "mp", split_axis=0, concat_axis=0, tiled=True)
     expert_out = outputs.reshape(EXPERTS * MOST, features)
     one = jnp.dot(first.astype(jnp.bfloat16), expert_out, preferred_element_type=jnp.float32)

time: 165 us -> 160 us (0.970)
  blocking collectives: 85.7 us -> 41.9 us
  waiting for transfers between devices: 46.7 us -> 62.4 us
  starting transfers between devices: 10.8 us -> 23 us
  Pallas kernels: 11.7 us -> 18.5 us
  local copies, waits for them, and re-layouts: 2.16 us -> 6.48 us
    all_to_all x1 -> x0, blocking collectives: 30.7 us -> none  [body(): lax.all_to_all(partial_value, 'expert', split_axis=0, concat_axis=0, tile...]
    all_to_all x0 -> x3, waiting for transfers between devices: none -> 17.4 us  [the longest x2 14.2 us: body(): lax.all_to_all(partial_value, 'expert', split_axis=0, concat_axis=0, tile...]
    all_to_all x1, blocking collectives: 33 us -> 20.2 us  [body(): lax.all_to_all(copies, 'expert', split_axis=0, concat_axis=0, tiled=True)]
    all_to_all x0 -> x3, starting transfers between devices: none -> 11.3 us  [the longest x2 7.81 us: body(): lax.all_to_all(partial_value, 'expert', split_axis=0, concat_axis=0, tile...]
    pallas_call x1 -> x2, Pallas kernels: 11.7 us -> 18.5 us  [ffn(): pl.pallas_call(ffn_kernel, out_shape=jax.ShapeDtypeStruct((count, feature...]
    unnamed x18, local copies, waits for them, and re-layouts: 1.65 us -> 4.93 us
    all_to_all x1, waiting for transfers between devices: 15.9 us -> 14.2 us  [body(): lax.all_to_all(outputs, 'mp', split_axis=0, concat_axis=0, tiled=True)]
  transfers between devices with their start and end apart: 2 -> 5, of which waited for: 2 -> 5; matrix products, arithmetic and copies ran while one was open for 0% -> 1% of each run, Pallas kernels for 0% -> 12%
where the time goes in v2:
time: 160 us; the launch traced here: 159 us
  waiting for transfers between devices  62.4 us (39%)
  blocking collectives  41.9 us (26%)
  starting transfers between devices  23 us (14%)
  Pallas kernels  18.5 us (12%)
  local copies, waits for them, and re-layouts  6.48 us (4%)
  matrix products  3.47 us (2%)
  other arithmetic  3.2 us (2%)
    all_to_all x1, waiting for transfers between devices, body(): parts = lax.all_to_all(parts, 'mp', split_axis=0, concat_axis=0, tiled=True)  30.8 us
    all_to_all x1, blocking collectives, body(): lax.all_to_all(outgoing, 'mp', split_axis=0, concat_axis=0, tiled=True)  21.7 us
    all_to_all x1, blocking collectives, body(): lax.all_to_all(copies, 'expert', split_axis=0, concat_axis=0, tiled=True)  20.2 us
    pallas_call x2, Pallas kernels, ffn(): pl.pallas_call(ffn_kernel, out_shape=jax.ShapeDtypeStruct((count, feature...  18.5 us
    all_to_all x2, waiting for transfers between devices, body(): lax.all_to_all(partial_value, 'expert', split_axis=0, concat_axis=0, tile...  14.2 us
    all_to_all x1, waiting for transfers between devices, body(): lax.all_to_all(outputs, 'mp', split_axis=0, concat_axis=0, tiled=True)  14.2 us
    all_to_all x2, starting transfers between devices, body(): lax.all_to_all(partial_value, 'expert', split_axis=0, concat_axis=0, tile...  7.81 us
    all_to_all x1, starting transfers between devices, body(): parts = lax.all_to_all(parts, 'mp', split_axis=0, concat_axis=0, tiled=True)  7.23 us
  transfers between devices with their start and end apart: 5, of which 5 were waited for; matrix products, arithmetic and copies ran while one was open for 1% of the time, Pallas kernels for 12%

profile of v2, /device:TPU:448, one launch (start us, length us, event | category | flops | bytes accessed | tf_op | source)
XLA Modules:
  0.0 159.3 jit_solution(16501665186588261265)
XLA Ops:
  0.0 0.0 copy-start
  0.0 1.5 copy.17
  1.6 0.0 copy-done
  1.6 1.8 %convolution_convert_fusion = f16[256,2304]{1,0:T(8,128)(2,1)} fusion(bf16[256,288]{1,0:T(8,128)(2,1)S(1)} %bitcast.39, bf16[288,2304]{1,0:T(8,128)(2,1)S(1)} %copy-done), kind=kOutput, calls=%fused_computation | convolution fusion | flops 340328448 | bytes 2654208 | tf_op jit(solution)/shard_map/dot_general | solution.py:84
  3.4 0.0 copy-start.6
  3.4 7.2 %all-to-all-start = ((f16[8,32,2304]{2,1,0:T(8,128)(2,1)}), f16[8,32,2304]{2,1,0:T(8,128)(2,1)S(1)}, u32[]{:S(2)}, u32[]{:S(2)}) async-start(f16[8,32,2304]{2,1,0:T(8,128)(2,1)} %bitcast.36), calls=%async_computation | async-start | bytes 2359296 | tf_op jit(solution)/shard_map/all_to_all | solution.py:86
  10.6 0.0 copy-done.6
  10.6 0.0 copy-start.4
  10.6 0.1 copy.18
  10.7 0.1 eq.45
  10.8 0.1 fusion.4
  10.9 0.1 reduce_window_sum.11
  11.0 0.2 select_reduce_fusion
  11.2 0.1 reduce_sum.55
  11.3 0.1 copy.19
  11.4 0.0 copy-start.5
  11.4 30.8 %all-to-all-done = f16[8,32,2304]{2,1,0:T(8,128)(2,1)S(1)} async-done(((f16[8,32,2304]{2,1,0:T(8,128)(2,1)}), f16[8,32,2304]{2,1,0:T(8,128)(2,1)S(1)}, u32[]{:S(2)}, u32[]{:S(2)}) %all-to-all-start) | async-done | bytes 1179680 | tf_op jit(solution)/shard_map/all_to_all | solution.py:86
  42.2 0.2 convert_reduce_fusion
  42.4 0.0 copy-done.4
  42.4 0.1 multiply_reduce_fusion
  42.5 0.0 copy-done.5
  42.5 0.4 convolution_convert_fusion.1
  43.0 21.7 %all_to_all.35 = bf16[8,16,2304]{2,1,0:T(8,128)(2,1)S(1)} all-to-all(bf16[8,16,2304]{2,1,0:T(8,128)(2,1)S(1)} %bitcast.37), channel_id=1, replica_groups=mesh['dp'=16,'mp'=8,'expert'=4] {'mp'}, dimensions={0} | all-to-all | bytes 1179648 | tf_op jit(solution)/shard_map/all_to_all | solution.py:105
  64.8 0.1 broadcast_in_dim.4
  64.8 20.2 %all_to_all.36 = bf16[4,8,8,2304]{3,2,1,0:T(8,128)(2,1)} all-to-all(bf16[4,8,8,2304]{3,2,1,0:T(8,128)(2,1)S(1)} %broadcast_in_dim.4), channel_id=1, replica_groups=mesh['dp'=16,'mp'=8,'expert'=4] {'expert'}, dimensions={0} | all-to-all | bytes 2359296 | tf_op jit(solution)/shard_map/all_to_all | solution.py:111
  85.0 1.1 broadcast_in_dim.5
  86.2 3.5 %all-to-all-start.4 = ((bf16[4,8,8,2304]{3,2,1,0:T(8,128)(2,1)}), bf16[4,8,8,2304]{3,2,1,0:T(8,128)(2,1)S(1)}, u32[]{:S(2)}, u32[]{:S(2)}) async-start(bf16[4,8,8,2304]{3,2,1,0:T(8,128)(2,1)} %broadcast_in_dim.5), calls=%async_computation.4 | async-start | bytes 2359296 | tf_op jit(solution)/shard_map/all_to_all | solution.py:111
  89.7 0.0 copy-start.3
  89.7 1.3 copy-done.3
  91.0 9.3 %shard_map.91 = bf16[256,2304]{1,0:T(8,128)(2,1)S(1)} custom-call(bf16[256,2304]{1,0:T(8,128)(2,1)S(1)} %bitcast.27, bf16[2304,1024]{1,0:T(8,128)(2,1)} %bitcast.28, bf16[2304,1024]{1,0:T(8,128)(2,1)} %bitcast.30, bf16[4,256,2304]{2,1,0:T(8,128)(2,1)} %bitcast.32), custom_call_target="tpu_custom_call" | custom-call | tf_op jit(solution)/shard_map/pallas_call | solution.py:41
  100.2 0.0 copy-start.1
  100.2 1.0 copy-done.1
  101.2 3.2 %all-to-all-done.4 = bf16[4,8,8,2304]{3,2,1,0:T(8,128)(2,1)S(1)} async-done(((bf16[4,8,8,2304]{3,2,1,0:T(8,128)(2,1)}), bf16[4,8,8,2304]{3,2,1,0:T(8,128)(2,1)S(1)}, u32[]{:S(2)}, u32[]{:S(2)}) %all-to-all-start.4) | async-done | bytes 1179680 | tf_op jit(solution)/shard_map/all_to_all | solution.py:111
  104.5 4.3 %all-to-all-start.3 = ((bf16[4,8,8,2304]{3,2,1,0:T(8,128)(2,1)}), bf16[4,8,8,2304]{3,2,1,0:T(8,128)(2,1)}, u32[]{:S(2)}, u32[]{:S(2)}) async-start(bf16[4,8,8,2304]{3,2,1,0:T(8,128)(2,1)} %bitcast.25), calls=%async_computation.3 | async-start | bytes 2359296 | tf_op jit(solution)/shard_map/all_to_all | solution.py:115
  108.8 9.3 %shard_map.92 = bf16[256,2304]{1,0:T(8,128)(2,1)S(1)} custom-call(bf16[256,2304]{1,0:T(8,128)(2,1)S(1)} %bitcast.24, bf16[2304,1024]{1,0:T(8,128)(2,1)} %bitcast.29, bf16[2304,1024]{1,0:T(8,128)(2,1)} %bitcast.31, bf16[4,256,2304]{2,1,0:T(8,128)(2,1)} %bitcast.33), custom_call_target="tpu_custom_call" | custom-call | tf_op jit(solution)/shard_map/pallas_call | solution.py:41
  118.0 0.0 copy-start.2
  118.1 1.0 copy-done.2
  119.1 3.3 %all-to-all-done.3 = bf16[4,8,8,2304]{3,2,1,0:T(8,128)(2,1)} async-done(((bf16[4,8,8,2304]{3,2,1,0:T(8,128)(2,1)}), bf16[4,8,8,2304]{3,2,1,0:T(8,128)(2,1)}, u32[]{:S(2)}, u32[]{:S(2)}) %all-to-all-start.3) | async-done | bytes 1179680 | tf_op jit(solution)/shard_map/all_to_all | solution.py:115
  122.4 3.5 %all-to-all-start.5 = ((bf16[4,8,8,2304]{3,2,1,0:T(8,128)(2,1)}), bf16[4,8,8,2304]{3,2,1,0:T(8,128)(2,1)S(1)}, u32[]{:S(2)}, u32[]{:S(2)}) async-start(bf16[4,8,8,2304]{3,2,1,0:T(8,128)(2,1)} %bitcast.26), calls=%async_computation.5 | async-start | bytes 2359296 | tf_op jit(solution)/shard_map/all_to_all | solution.py:115
  126.0 1.5 reduce_sum.57
  127.4 10.9 %all-to-all-done.5 = bf16[4,8,8,2304]{3,2,1,0:T(8,128)(2,1)S(1)} async-done(((bf16[4,8,8,2304]{3,2,1,0:T(8,128)(2,1)}), bf16[4,8,8,2304]{3,2,1,0:T(8,128)(2,1)S(1)}, u32[]{:S(2)}, u32[]{:S(2)}) %all-to-all-start.5) | async-done | bytes 1179680 | tf_op jit(solution)/shard_map/all_to_all | solution.py:115
  138.3 0.2 reduce_sum.58
  138.5 0.0 copy-start.7
  138.5 0.9 pad_maximum_fusion
  139.4 4.4 %all-to-all-start.6 = ((bf16[8,16,2304]{2,1,0:T(8,128)(2,1)}), bf16[8,16,2304]{2,1,0:T(8,128)(2,1)S(1)}, u32[]{:S(2)}, u32[]{:S(2)}) async-start(bf16[8,16,2304]{2,1,0:T(8,128)(2,1)} %pad_maximum_fusion), calls=%async_computation.6 | async-start | bytes 1179648 | tf_op jit(solution)/shard_map/all_to_all | solution.py:118
  143.8 0.0 copy-done.7
  143.8 14.2 %all-to-all-done.6 = bf16[8,16,2304]{2,1,0:T(8,128)(2,1)S(1)} async-done(((bf16[8,16,2304]{2,1,0:T(8,128)(2,1)}), bf16[8,16,2304]{2,1,0:T(8,128)(2,1)S(1)}, u32[]{:S(2)}, u32[]{:S(2)}) %all-to-all-start.6) | async-done | bytes 589856 | tf_op jit(solution)/shard_map/all_to_all | solution.py:118
  158.0 0.3 convolution_multiply_fusion
  158.3 1.0 fusion.1
  (6 shorter events, 0.1 us)
Async XLA Ops:
  0.0 1.6 copy-start
  3.4 7.2 %copy-start.6 = (s32[32,2]{0,1:T(2,128)S(1)}, s32[32,2]{0,1:T(2,128)}, u32[]{:S(2)}) copy-start(s32[32,2]{0,1:T(2,128)} %param.16) | copy-start | bytes 772
  3.4 38.8 %all-to-all-start = ((f16[8,32,2304]{2,1,0:T(8,128)(2,1)}), f16[8,32,2304]{2,1,0:T(8,128)(2,1)S(1)}, u32[]{:S(2)}, u32[]{:S(2)}) async-start(f16[8,32,2304]{2,1,0:T(8,128)(2,1)} %bitcast.36), calls=%async_computation | async-start | bytes 2359296 | tf_op jit(solution)/shard_map/all_to_all | solution.py:86
  10.6 31.7 %copy-start.4 = (f32[32,2304]{1,0:T(8,128)S(1)}, f32[32,2304]{1,0:T(8,128)}, u32[]{:S(2)}) copy-start(f32[32,2304]{1,0:T(8,128)} %param.10) | copy-start | bytes 884740
  11.4 31.1 %copy-start.5 = (f32[2304]{0:T(1024)S(1)}, f32[2304]{0:T(1024)}, u32[]{:S(2)}) copy-start(f32[2304]{0:T(1024)} %param.12) | copy-start | bytes 27652
  86.2 18.3 %all-to-all-start.4 = ((bf16[4,8,8,2304]{3,2,1,0:T(8,128)(2,1)}), bf16[4,8,8,2304]{3,2,1,0:T(8,128)(2,1)S(1)}, u32[]{:S(2)}, u32[]{:S(2)}) async-start(bf16[4,8,8,2304]{3,2,1,0:T(8,128)(2,1)} %broadcast_in_dim.5), calls=%async_computation.4 | async-start | bytes 2359296 | tf_op jit(solution)/shard_map/all_to_all | solution.py:111
  89.7 1.3 copy-start.3
  100.2 1.0 copy-start.1
  104.5 18.0 %all-to-all-start.3 = ((bf16[4,8,8,2304]{3,2,1,0:T(8,128)(2,1)}), bf16[4,8,8,2304]{3,2,1,0:T(8,128)(2,1)}, u32[]{:S(2)}, u32[]{:S(2)}) async-start(bf16[4,8,8,2304]{3,2,1,0:T(8,128)(2,1)} %bitcast.25), calls=%async_computation.3 | async-start | bytes 2359296 | tf_op jit(solution)/shard_map/all_to_all | solution.py:115
  118.0 1.0 copy-start.2
  122.4 15.9 %all-to-all-start.5 = ((bf16[4,8,8,2304]{3,2,1,0:T(8,128)(2,1)}), bf16[4,8,8,2304]{3,2,1,0:T(8,128)(2,1)S(1)}, u32[]{:S(2)}, u32[]{:S(2)}) async-start(bf16[4,8,8,2304]{3,2,1,0:T(8,128)(2,1)} %bitcast.26), calls=%async_computation.5 | async-start | bytes 2359296 | tf_op jit(solution)/shard_map/all_to_all | solution.py:115
  138.5 5.3 %copy-start.7 = (f32[32,2]{0,1:T(2,128)S(1)}, f32[32,2]{0,1:T(2,128)}, u32[]{:S(2)}) copy-start(f32[32,2]{0,1:T(2,128)} %param.17) | copy-start | bytes 772
  139.4 18.6 %all-to-all-start.6 = ((bf16[8,16,2304]{2,1,0:T(8,128)(2,1)}), bf16[8,16,2304]{2,1,0:T(8,128)(2,1)S(1)}, u32[]{:S(2)}, u32[]{:S(2)}) async-start(bf16[8,16,2304]{2,1,0:T(8,128)(2,1)} %pad_maximum_fusion), calls=%async_computation.6 | async-start | bytes 1179648 | tf_op jit(solution)/shard_map/all_to_all | solution.py:118

commit v3 on v1

v3 whole, which is shorter than its diff:
```python
import functools

import jax
import jax.numpy as jnp
from jax import lax
from jax.experimental import pallas as pl
from jax.experimental.pallas import tpu as pltpu
from jax.sharding import PartitionSpec as P

EXPERTS = 8
MOST = 16
EPSILON = 1e-06

UNIT_CHUNK = 512
OUT_CHUNK = 1152


def ffn_kernel(count, *refs):
    row_refs, refs = refs[:count], refs[count:]
    (gate_hbm, up_hbm, down_hbm), refs = refs[:3], refs[3:]
    out_refs, refs = refs[:count], refs[count:]
    rows_ref, act_ref, gate_ref, up_ref, down_ref, gate_sem, up_sem, down_sem = refs
    depth = row_refs[0].shape[0]
    unit_steps = gate_sem.shape[0]
    out_steps = down_sem.shape[0]

    def columns(step, width):
        return pl.ds(step * width, width)

    gate_copies, up_copies, down_copies = [], [], []
    for step in range(unit_steps):
        at = columns(step, UNIT_CHUNK)
        gate_copies.append(
            pltpu.make_async_copy(gate_hbm.at[:, at], gate_ref.at[:, at], gate_sem.at[step])
        )
        up_copies.append(pltpu.make_async_copy(up_hbm.at[:, at], up_ref.at[:, at], up_sem.at[step]))
    for step in range(out_steps):
        at = columns(step, OUT_CHUNK)
        down_copies.append(
            pltpu.make_async_copy(down_hbm.at[:, at], down_ref.at[:, at], down_sem.at[step])
        )
    for step in range(unit_steps):
        gate_copies[step].start()
        up_copies[step].start()
    for step in range(out_steps):
        down_copies[step].start()
    for piece in range(count):
        rows_ref[pl.ds(piece * depth, depth), :] = row_refs[piece][...]
    for step in range(unit_steps):
        at = columns(step, UNIT_CHUNK)
        gate_copies[step].wait()
        up_copies[step].wait()
        gate = jnp.dot(rows_ref[...], gate_ref[:, at], preferred_element_type=jnp.float32)
        up = jnp.dot(rows_ref[...], up_ref[:, at], preferred_element_type=jnp.float32)
        act_ref[:, at] = (gate / (1.0 + jnp.exp(-gate)) * up).astype(jnp.bfloat16)
    for step in range(out_steps):
        at = columns(step, OUT_CHUNK)
        down_copies[step].wait()
        out = jnp.dot(act_ref[...], down_ref[:, at], preferred_element_type=jnp.float32)
        for piece in range(count):
            out_refs[piece][:, at] = out[piece * depth : (piece + 1) * depth].astype(jnp.bfloat16)


def ffn(pieces, *weights):
    count = len(pieces)
    depth, features = pieces[0].shape
    units = weights[0].shape[1]
    vmem = pl.BlockSpec(memory_space=pltpu.VMEM)
    hbm = pl.BlockSpec(memory_space=pltpu.HBM)
    return pl.pallas_call(
        functools.partial(ffn_kernel, count),
        out_shape=[jax.ShapeDtypeStruct((depth, features), jnp.bfloat16)] * count,
        in_specs=[vmem] * count + [hbm] * 3,
        out_specs=[vmem] * count,
        scratch_shapes=[
            pltpu.VMEM((count * depth, features), jnp.bfloat16),
            pltpu.VMEM((count * depth, units), jnp.bfloat16),
            pltpu.VMEM((features, units), jnp.bfloat16),
            pltpu.VMEM((features, units), jnp.bfloat16),
            pltpu.VMEM((units, features), jnp.bfloat16),
            pltpu.SemaphoreType.DMA((units // UNIT_CHUNK,)),
            pltpu.SemaphoreType.DMA((units // UNIT_CHUNK,)),
            pltpu.SemaphoreType.DMA((features // OUT_CHUNK,)),
        ],
        compiler_params=pltpu.CompilerParams(vmem_limit_bytes=40 << 20),
        cost_estimate=pl.CostEstimate(
            flops=6 * count * depth * features * units,
            transcendentals=count * depth * units,
            bytes_accessed=6 * features * units + 4 * count * depth * features,
        ),
    )(*pieces, *(pltpu.with_memory_space_constraint(w, pltpu.HBM) for w in weights))


def body(
    attn_out,
    residual,
    proj_weight,
    norm_gain,
    gate_weight,
    up_weight,
    down_weight,
    routes,
    route_weights,
):
    model_parts = lax.axis_size("mp")
    unit_parts = lax.axis_size("expert")
    row_count = residual.shape[0]
    features = residual.shape[1]
    blocks = attn_out.reshape(model_parts, unit_parts, row_count, attn_out.shape[1])
    picked = lax.dynamic_index_in_dim(blocks, lax.axis_index("expert"), axis=1, keepdims=False)
    picked = picked.reshape(model_parts * row_count, attn_out.shape[1])
    parts = jnp.dot(picked, proj_weight, preferred_element_type=jnp.float32).astype(jnp.float16)
    parts = parts.reshape(model_parts, row_count, features)
    parts = lax.all_to_all(parts, "mp", split_axis=0, concat_axis=0, tiled=True)
    hidden_state = residual + jnp.sum(parts, axis=0, dtype=jnp.float32)
    inverse_rms = lax.rsqrt(jnp.mean(hidden_state * hidden_state, axis=1, keepdims=True) + EPSILON)
    normed = (hidden_state * inverse_rms * norm_gain).astype(jnp.bfloat16)
    expert_ids = routes.reshape(-1)
    onehot = (expert_ids[:, None] == jnp.arange(EXPERTS, dtype=jnp.int32)[None, :]).astype(
        jnp.int32
    )
    before = jnp.cumsum(onehot, axis=0) - onehot
    position = jnp.sum(before * onehot, axis=1)
    target = (expert_ids * MOST + position).reshape(row_count, 2)
    slots = jnp.arange(EXPERTS * MOST, dtype=jnp.int32)
    first = target[:, 0][:, None] == slots[None, :]
    second = target[:, 1][:, None] == slots[None, :]
    placement = (first | second).astype(jnp.bfloat16)
    outgoing = lax.dot_general(
        placement, normed, (((0,), (0,)), ((), ())), preferred_element_type=jnp.float32
    ).astype(jnp.bfloat16)
    outgoing = outgoing.reshape(model_parts, MOST, features)
    arrived = lax.all_to_all(outgoing, "mp", split_axis=0, concat_axis=0, tiled=True)
    own = arrived.reshape(model_parts * MOST, features)
    weights = (gate_weight[0], up_weight[0], down_weight[0])

    def shift(value, by):
        return lax.ppermute(
            value, "expert", [(i, (i + by) % unit_parts) for i in range(unit_parts)]
        )

    before_rows = shift(own, 1)
    after_rows = shift(own, -1)
    (own_sum,) = ffn([own], *weights)
    far_rows = shift(lax.optimization_barrier((own, own_sum))[0], 2)
    before_sum, after_sum = ffn([before_rows, after_rows], *weights)
    back_after = shift(before_sum, -1)
    back_before = shift(after_sum, 1)
    far_rows = lax.optimization_barrier((far_rows, before_sum))[0]
    (far_sum,) = ffn([far_rows], *weights)
    back_far = shift(far_sum, 2)
    outputs = own_sum.astype(jnp.float32)
    for value in (back_after, back_before, back_far):
        outputs += value.astype(jnp.float32)
    outputs = outputs.astype(jnp.bfloat16).reshape(model_parts, MOST, features)
    outputs = lax.all_to_all(outputs, "mp", split_axis=0, concat_axis=0, tiled=True)
    expert_out = outputs.reshape(EXPERTS * MOST, features)
    one = jnp.dot(first.astype(jnp.bfloat16), expert_out, preferred_element_type=jnp.float32)
    two = jnp.dot(second.astype(jnp.bfloat16), expert_out, preferred_element_type=jnp.float32)
    return hidden_state + route_weights[:, 0:1] * one + route_weights[:, 1:2] * two


def solution(mesh):
    in_specs = (
        P("dp", "mp"),
        P(("dp", "mp", "expert"), None),
        P("mp", None),
        P(),
        P("mp", None, "expert"),
        P("mp", None, "expert"),
        P("mp", "expert", None),
        P(("dp", "mp", "expert"), None),
        P(("dp", "mp", "expert"), None),
    )
    out_specs = P(("dp", "mp", "expert"), None)
    return jax.shard_map(body, mesh=mesh, in_specs=in_specs, out_specs=out_specs, check_vma=False)
```

time: 165 us -> 160 us (0.970)
  the two profiles are of different devices: /device:TPU:448 before, /device:TPU:1 now
where the time goes in v3:
time: 160 us; the launch traced here: 159 us
  waiting for transfers between devices  75.3 us (47%)
  starting transfers between devices  38 us (24%)
  Pallas kernels  20.2 us (13%)
  blocking collectives  18 us (11%)
  matrix products  3.47 us (2%)
  local copies, waits for them, and re-layouts  1.96 us (1%)
  other arithmetic  1.77 us (1%)
    all_to_all x1, waiting for transfers between devices, body(): parts = lax.all_to_all(parts, 'mp', split_axis=0, concat_axis=0, tiled=True)  29.5 us
    ppermute x6, waiting for transfers between devices, shift(): lax.ppermute(value, 'expert', [(i, (i + by) % unit_parts) for i in range(...  26.6 us
    ppermute x6, starting transfers between devices, shift(): lax.ppermute(value, 'expert', [(i, (i + by) % unit_parts) for i in range(...  26.6 us
    pallas_call x3, Pallas kernels, ffn(): pl.pallas_call(functools.partial(ffn_kernel, count), out_shape=[jax.Shape...  20.2 us
    all_to_all x1, waiting for transfers between devices, body(): lax.all_to_all(outputs, 'mp', split_axis=0, concat_axis=0, tiled=True)  19.3 us
    all_to_all x1, blocking collectives, body(): lax.all_to_all(outgoing, 'mp', split_axis=0, concat_axis=0, tiled=True)  18 us
    all_to_all x1, starting transfers between devices, body(): parts = lax.all_to_all(parts, 'mp', split_axis=0, concat_axis=0, tiled=True)  7.78 us
    all_to_all x1, starting transfers between devices, body(): lax.all_to_all(outputs, 'mp', split_axis=0, concat_axis=0, tiled=True)  3.67 us
  transfers between devices with their start and end apart: 8, of which 6 were waited for; matrix products, arithmetic and copies ran while one was open for 0% of the time, Pallas kernels for 13%

profile of v3, /device:TPU:1, one launch (start us, length us, event | category | flops | bytes accessed | tf_op | source)
XLA Modules:
  0.0 159.0 jit_solution(4931183801075040252)
XLA Ops:
  0.0 0.0 copy-start
  0.0 1.5 copy.17
  1.6 0.0 copy-done
  1.6 1.8 %convolution_convert_fusion = f16[256,2304]{1,0:T(8,128)(2,1)} fusion(bf16[256,288]{1,0:T(8,128)(2,1)S(1)} %bitcast.40, bf16[288,2304]{1,0:T(8,128)(2,1)S(1)} %copy-done), kind=kOutput, calls=%fused_computation | convolution fusion | flops 340328448 | bytes 2654208 | tf_op jit(solution)/shard_map/dot_general | solution.py:112
  3.4 0.0 copy-start.3
  3.4 7.8 %all-to-all-start = ((f16[8,32,2304]{2,1,0:T(8,128)(2,1)}), f16[8,32,2304]{2,1,0:T(8,128)(2,1)S(1)}, u32[]{:S(2)}, u32[]{:S(2)}) async-start(f16[8,32,2304]{2,1,0:T(8,128)(2,1)} %bitcast.37), calls=%async_computation | async-start | bytes 2359296 | tf_op jit(solution)/shard_map/all_to_all | solution.py:114
  11.2 0.0 copy-done.3
  11.2 0.0 copy-start.1
  11.2 0.1 copy.18
  11.3 0.1 eq.45
  11.4 0.1 fusion.4
  11.4 0.1 reduce_window_sum.11
  11.5 0.2 select_reduce_fusion
  11.7 0.1 reduce_sum.31
  11.8 0.1 copy.19
  11.9 0.0 copy-start.2
  11.9 29.5 %all-to-all-done = f16[8,32,2304]{2,1,0:T(8,128)(2,1)S(1)} async-done(((f16[8,32,2304]{2,1,0:T(8,128)(2,1)}), f16[8,32,2304]{2,1,0:T(8,128)(2,1)S(1)}, u32[]{:S(2)}, u32[]{:S(2)}) %all-to-all-start) | async-done | bytes 1179680 | tf_op jit(solution)/shard_map/all_to_all | solution.py:114
  41.4 0.2 convert_reduce_fusion
  41.6 0.0 copy-done.1
  41.6 0.1 multiply_reduce_fusion
  41.8 0.0 copy-done.2
  41.8 0.4 convolution_convert_fusion.1
  42.2 18.0 %all_to_all.15 = bf16[8,16,2304]{2,1,0:T(8,128)(2,1)S(1)} all-to-all(bf16[8,16,2304]{2,1,0:T(8,128)(2,1)S(1)} %bitcast.38), channel_id=1, replica_groups=mesh['dp'=16,'mp'=8,'expert'=4] {'mp'}, dimensions={0} | all-to-all | bytes 1179648 | tf_op jit(solution)/shard_map/all_to_all | solution.py:133
  60.2 7.9 %collective-permute-start = (bf16[128,2304]{1,0:T(8,128)(2,1)S(1)}, bf16[128,2304]{1,0:T(8,128)(2,1)S(1)}, u32[]{:S(2)}, u32[]{:S(2)}) collective-permute-start(bf16[128,2304]{1,0:T(8,128)(2,1)S(1)} %bitcast.22), channel_id=1, source_target_pairs={{0,1},{1,2},{2,3},{3,0},{4,5},{5,6},{6,7},{7,4},{8,9},{9,10},{10,1... | collective-permute-start | bytes 1769480 | tf_op jit(solution)/shard_map/ppermute | solution.py:138
  68.2 3.2 %collective-permute-start.1 = (bf16[128,2304]{1,0:T(8,128)(2,1)S(1)}, bf16[128,2304]{1,0:T(8,128)(2,1)S(1)}, u32[]{:S(2)}, u32[]{:S(2)}) collective-permute-start(bf16[128,2304]{1,0:T(8,128)(2,1)S(1)} %bitcast.23), channel_id=1, source_target_pairs={{0,3},{1,0},{2,1},{3,2},{4,7},{5,4},{6,5},{7,6},{8,11},{9,8},{10,9... | collective-permute-start | bytes 1769480 | tf_op jit(solution)/shard_map/ppermute | solution.py:138
  71.4 6.3 %shard_map.91 = bf16[128,2304]{1,0:T(8,128)(2,1)S(1)} custom-call(bf16[128,2304]{1,0:T(8,128)(2,1)S(1)} %bitcast.24, bf16[2304,1024]{1,0:T(8,128)(2,1)} %bitcast.26, bf16[2304,1024]{1,0:T(8,128)(2,1)} %bitcast.29, bf16[1024,2304]{1,0:T(8,128)(2,1)} %bitcast.32), custom_call_target="tpu_custom_call" | custom-call | flops 1811939328 | bytes 15335424 | tf_op jit(solution)/shard_map/pallas_call | solution.py:70
  77.7 3.6 %collective-permute-start.4 = (bf16[128,2304]{1,0:T(8,128)(2,1)S(1)}, bf16[128,2304]{1,0:T(8,128)(2,1)S(1)}, u32[]{:S(2)}, u32[]{:S(2)}) collective-permute-start(bf16[128,2304]{1,0:T(8,128)(2,1)S(1)} %bitcast.25), channel_id=1, source_target_pairs={{0,2},{1,3},{2,0},{3,1},{4,6},{5,7},{6,4},{7,5},{8,10},{9,11},{10,... | collective-permute-start | bytes 1769480 | tf_op jit(solution)/shard_map/ppermute | solution.py:138
  81.3 0.6 collective-permute-done.refs_0_
  81.9 1.5 collective-permute-done.1.refs_1_
  83.4 7.6 %shard_map.92 = (bf16[128,2304]{1,0:T(8,128)(2,1)S(1)}, bf16[128,2304]{1,0:T(8,128)(2,1)S(1)}) custom-call(bf16[128,2304]{1,0:T(8,128)(2,1)S(1)} %collective-permute-done.refs_0_, bf16[128,2304]{1,0:T(8,128)(2,1)S(1)} %collective-permute-done.1.refs_1_, bf16[2304,1024]{1,0:T(8,128)(2,1)} %bitcast.27, bf16[2304,1024]{1,0:T(8,128)(2,1)} %bitcast.30, ...), custom_call_target="tpu_custom_call" | custom-call | flops 3623878656 | bytes 16515072 | tf_op jit(solution)/shard_map/pallas_call | solution.py:70
  91.0 5.0 %collective-permute-start.2 = (bf16[128,2304]{1,0:T(8,128)(2,1)S(1)}, bf16[128,2304]{1,0:T(8,128)(2,1)S(1)}, u32[]{:S(2)}, u32[]{:S(2)}) collective-permute-start(bf16[128,2304]{1,0:T(8,128)(2,1)S(1)} %get-tuple-element.9), channel_id=1, source_target_pairs={{0,3},{1,0},{2,1},{3,2},{4,7},{5,4},{6,5},{7,6},{8,11},{9,8},{10,9... | collective-permute-start | bytes 1769480 | tf_op jit(solution)/shard_map/ppermute | solution.py:138
  96.1 0.0 collective-permute-done.4.refs_0_
  96.1 6.3 %shard_map.93 = bf16[128,2304]{1,0:T(8,128)(2,1)S(1)} custom-call(bf16[128,2304]{1,0:T(8,128)(2,1)S(1)} %collective-permute-done.4.refs_0_, bf16[2304,1024]{1,0:T(8,128)(2,1)} %bitcast.28, bf16[2304,1024]{1,0:T(8,128)(2,1)} %bitcast.31, bf16[1024,2304]{1,0:T(8,128)(2,1)} %bitcast.34), custom_call_target="tpu_custom_call" | custom-call | flops 1811939328 | bytes 15335424 | tf_op jit(solution)/shard_map/pallas_call | solution.py:70
  102.4 1.9 %collective-permute-start.5 = (bf16[128,2304]{1,0:T(8,128)(2,1)S(1)}, bf16[128,2304]{1,0:T(8,128)(2,1)S(1)}, u32[]{:S(2)}, u32[]{:S(2)}) collective-permute-start(bf16[128,2304]{1,0:T(8,128)(2,1)S(1)} %shard_map.93), channel_id=1, source_target_pairs={{0,2},{1,3},{2,0},{3,1},{4,6},{5,7},{6,4},{7,5},{8,10},{9,11},{10,... | collective-permute-start | bytes 1769480 | tf_op jit(solution)/shard_map/ppermute | solution.py:138
  104.3 4.9 %collective-permute-start.3 = (bf16[128,2304]{1,0:T(8,128)(2,1)S(1)}, bf16[128,2304]{1,0:T(8,128)(2,1)S(1)}, u32[]{:S(2)}, u32[]{:S(2)}) collective-permute-start(bf16[128,2304]{1,0:T(8,128)(2,1)S(1)} %get-tuple-element.10), channel_id=1, source_target_pairs={{0,1},{1,2},{2,3},{3,0},{4,5},{5,6},{6,7},{7,4},{8,9},{9,10},{10,1... | collective-permute-start | bytes 1769480 | tf_op jit(solution)/shard_map/ppermute | solution.py:138
  109.2 7.5 %collective-permute-done.5 = bf16[128,2304]{1,0:T(8,128)(2,1)S(1)} collective-permute-done((bf16[128,2304]{1,0:T(8,128)(2,1)S(1)}, bf16[128,2304]{1,0:T(8,128)(2,1)S(1)}, u32[]{:S(2)}, u32[]{:S(2)}) %collective-permute-start.5) | collective-permute-done | bytes 589856 | tf_op jit(solution)/shard_map/ppermute | solution.py:138
  116.7 0.0 collective-permute-done.2
  116.7 17.0 %collective-permute-done.3 = bf16[128,2304]{1,0:T(8,128)(2,1)S(1)} collective-permute-done((bf16[128,2304]{1,0:T(8,128)(2,1)S(1)}, bf16[128,2304]{1,0:T(8,128)(2,1)S(1)}, u32[]{:S(2)}, u32[]{:S(2)}) %collective-permute-start.3) | collective-permute-done | bytes 589856 | tf_op jit(solution)/shard_map/ppermute | solution.py:138
  133.7 1.1 add_convert_fusion
  134.8 0.0 copy-start.4
  134.8 3.7 %all-to-all-start.2 = ((bf16[8,16,2304]{2,1,0:T(8,128)(2,1)}), bf16[8,16,2304]{2,1,0:T(8,128)(2,1)S(1)}, u32[]{:S(2)}, u32[]{:S(2)}) async-start(bf16[8,16,2304]{2,1,0:T(8,128)(2,1)} %bitcast.11), calls=%async_computation.2 | async-start | bytes 1179648 | tf_op jit(solution)/shard_map/all_to_all | solution.py:156
  138.5 0.0 copy-done.4
  138.5 19.3 %all-to-all-done.2 = bf16[8,16,2304]{2,1,0:T(8,128)(2,1)S(1)} async-done(((bf16[8,16,2304]{2,1,0:T(8,128)(2,1)}), bf16[8,16,2304]{2,1,0:T(8,128)(2,1)S(1)}, u32[]{:S(2)}, u32[]{:S(2)}) %all-to-all-start.2) | async-done | bytes 589856 | tf_op jit(solution)/shard_map/all_to_all | solution.py:156
  157.8 0.3 convolution_multiply_fusion
  158.1 1.0 fusion.1
  (5 shorter events, 0.1 us)
Async XLA Ops:
  0.0 1.6 copy-start
  3.4 7.8 %copy-start.3 = (s32[32,2]{0,1:T(2,128)S(1)}, s32[32,2]{0,1:T(2,128)}, u32[]{:S(2)}) copy-start(s32[32,2]{0,1:T(2,128)} %param.16) | copy-start | bytes 772
  3.4 38.0 %all-to-all-start = ((f16[8,32,2304]{2,1,0:T(8,128)(2,1)}), f16[8,32,2304]{2,1,0:T(8,128)(2,1)S(1)}, u32[]{:S(2)}, u32[]{:S(2)}) async-start(f16[8,32,2304]{2,1,0:T(8,128)(2,1)} %bitcast.37), calls=%async_computation | async-start | bytes 2359296 | tf_op jit(solution)/shard_map/all_to_all | solution.py:114
  11.2 30.4 %copy-start.1 = (f32[32,2304]{1,0:T(8,128)S(1)}, f32[32,2304]{1,0:T(8,128)}, u32[]{:S(2)}) copy-start(f32[32,2304]{1,0:T(8,128)} %param.10) | copy-start | bytes 884740
  11.9 29.8 %copy-start.2 = (f32[2304]{0:T(1024)S(1)}, f32[2304]{0:T(1024)}, u32[]{:S(2)}) copy-start(f32[2304]{0:T(1024)} %param.12) | copy-start | bytes 27652
  60.2 21.7 %collective-permute-start = (bf16[128,2304]{1,0:T(8,128)(2,1)S(1)}, bf16[128,2304]{1,0:T(8,128)(2,1)S(1)}, u32[]{:S(2)}, u32[]{:S(2)}) collective-permute-start(bf16[128,2304]{1,0:T(8,128)(2,1)S(1)} %bitcast.22), channel_id=1, source_target_pairs={{0,1},{1,2},{2,3},{3,0},{4,5},{5,6},{6,7},{7,4},{8,9},{9,10},{10,1... | collective-permute-start | bytes 1769480 | tf_op jit(solution)/shard_map/ppermute | solution.py:138
  68.2 15.3 %collective-permute-start.1 = (bf16[128,2304]{1,0:T(8,128)(2,1)S(1)}, bf16[128,2304]{1,0:T(8,128)(2,1)S(1)}, u32[]{:S(2)}, u32[]{:S(2)}) collective-permute-start(bf16[128,2304]{1,0:T(8,128)(2,1)S(1)} %bitcast.23), channel_id=1, source_target_pairs={{0,3},{1,0},{2,1},{3,2},{4,7},{5,4},{6,5},{7,6},{8,11},{9,8},{10,9... | collective-permute-start | bytes 1769480 | tf_op jit(solution)/shard_map/ppermute | solution.py:138
  77.7 18.4 %collective-permute-start.4 = (bf16[128,2304]{1,0:T(8,128)(2,1)S(1)}, bf16[128,2304]{1,0:T(8,128)(2,1)S(1)}, u32[]{:S(2)}, u32[]{:S(2)}) collective-permute-start(bf16[128,2304]{1,0:T(8,128)(2,1)S(1)} %bitcast.25), channel_id=1, source_target_pairs={{0,2},{1,3},{2,0},{3,1},{4,6},{5,7},{6,4},{7,5},{8,10},{9,11},{10,... | collective-permute-start | bytes 1769480 | tf_op jit(solution)/shard_map/ppermute | solution.py:138
  91.0 25.7 %collective-permute-start.2 = (bf16[128,2304]{1,0:T(8,128)(2,1)S(1)}, bf16[128,2304]{1,0:T(8,128)(2,1)S(1)}, u32[]{:S(2)}, u32[]{:S(2)}) collective-permute-start(bf16[128,2304]{1,0:T(8,128)(2,1)S(1)} %get-tuple-element.9), channel_id=1, source_target_pairs={{0,3},{1,0},{2,1},{3,2},{4,7},{5,4},{6,5},{7,6},{8,11},{9,8},{10,9... | collective-permute-start | bytes 1769480 | tf_op jit(solution)/shard_map/ppermute | solution.py:138
  102.4 14.3 %collective-permute-start.5 = (bf16[128,2304]{1,0:T(8,128)(2,1)S(1)}, bf16[128,2304]{1,0:T(8,128)(2,1)S(1)}, u32[]{:S(2)}, u32[]{:S(2)}) collective-permute-start(bf16[128,2304]{1,0:T(8,128)(2,1)S(1)} %shard_map.93), channel_id=1, source_target_pairs={{0,2},{1,3},{2,0},{3,1},{4,6},{5,7},{6,4},{7,5},{8,10},{9,11},{10,... | collective-permute-start | bytes 1769480 | tf_op jit(solution)/shard_map/ppermute | solution.py:138
  104.3 29.4 %collective-permute-start.3 = (bf16[128,2304]{1,0:T(8,128)(2,1)S(1)}, bf16[128,2304]{1,0:T(8,128)(2,1)S(1)}, u32[]{:S(2)}, u32[]{:S(2)}) collective-permute-start(bf16[128,2304]{1,0:T(8,128)(2,1)S(1)} %get-tuple-element.10), channel_id=1, source_target_pairs={{0,1},{1,2},{2,3},{3,0},{4,5},{5,6},{6,7},{7,4},{8,9},{9,10},{10,1... | collective-permute-start | bytes 1769480 | tf_op jit(solution)/shard_map/ppermute | solution.py:138
  134.8 3.7 %copy-start.4 = (f32[32,2]{0,1:T(2,128)S(1)}, f32[32,2]{0,1:T(2,128)}, u32[]{:S(2)}) copy-start(f32[32,2]{0,1:T(2,128)} %param.17) | copy-start | bytes 772
  134.8 23.0 %all-to-all-start.2 = ((bf16[8,16,2304]{2,1,0:T(8,128)(2,1)}), bf16[8,16,2304]{2,1,0:T(8,128)(2,1)S(1)}, u32[]{:S(2)}, u32[]{:S(2)}) async-start(bf16[8,16,2304]{2,1,0:T(8,128)(2,1)} %bitcast.11), calls=%async_computation.2 | async-start | bytes 1179648 | tf_op jit(solution)/shard_map/all_to_all | solution.py:156

commit v4 on v3

--- a/solution.py
+++ b/solution.py
@@ -106,9 +106,14 @@
     unit_parts = lax.axis_size("expert")
     row_count = residual.shape[0]
     features = residual.shape[1]
-    blocks = attn_out.reshape(model_parts, unit_parts, row_count, attn_out.shape[1])
-    picked = lax.dynamic_index_in_dim(blocks, lax.axis_index("expert"), axis=1, keepdims=False)
-    picked = picked.reshape(model_parts * row_count, attn_out.shape[1])
+    picked_rows = jnp.arange(model_parts * row_count, dtype=jnp.int32)
+    picked_rows = (
+        picked_rows // row_count * unit_parts + lax.axis_index("expert")
+    ) * row_count + picked_rows % row_count
+    pick = (picked_rows[:, None] == jnp.arange(attn_out.shape[0], dtype=jnp.int32)[None, :]).astype(
+        jnp.bfloat16
+    )
+    picked = jnp.dot(pick, attn_out, preferred_element_type=jnp.float32).astype(jnp.bfloat16)
     parts = jnp.dot(picked, proj_weight, preferred_element_type=jnp.float32).astype(jnp.float16)
     parts = parts.reshape(model_parts, row_count, features)
     parts = lax.all_to_all(parts, "mp", split_axis=0, concat_axis=0, tiled=True)
@@ -139,16 +144,18 @@
             value, "expert", [(i, (i + by) % unit_parts) for i in range(unit_parts)]
         )
 
-    before_rows = shift(own, 1)
-    after_rows = shift(own, -1)
+    far_rows = shift(own, 2)
     (own_sum,) = ffn([own], *weights)
-    far_rows = shift(lax.optimization_barrier((own, own_sum))[0], 2)
+    later = lax.optimization_barrier((own, own_sum))[0]
+    before_rows = shift(later, 1)
+    after_rows = shift(later, -1)
+    (far_sum,) = ffn([far_rows], *weights)
+    back_far = shift(far_sum, 2)
+    before_rows, after_rows, far_sum = lax.optimization_barrier((before_rows, after_rows, far_sum))
     before_sum, after_sum = ffn([before_rows, after_rows], *weights)
     back_after = shift(before_sum, -1)
+    after_sum, back_far = lax.optimization_barrier((after_sum, back_far))
     back_before = shift(after_sum, 1)
-    far_rows = lax.optimization_barrier((far_rows, before_sum))[0]
-    (far_sum,) = ffn([far_rows], *weights)
-    back_far = shift(far_sum, 2)
     outputs = own_sum.astype(jnp.float32)
     for value in (back_after, back_before, back_far):
         outputs += value.astype(jnp.float32)

time: 160 us -> 156 us (0.975)
  the two profiles are of different devices: /device:TPU:1 before, /device:TPU:448 now
where the time goes in v4:
time: 156 us
  waiting for transfers between devices  69.2 us (44%)
  starting transfers between devices  35.5 us (23%)
  blocking collectives  21.7 us (14%)
  Pallas kernels  20.2 us (13%)
  matrix products  5.27 us (3%)
  other arithmetic  1.78 us (1%)
  local copies, waits for them, and re-layouts  1.72 us (1%)
    all_to_all x1, waiting for transfers between devices, body(): parts = lax.all_to_all(parts, 'mp', split_axis=0, concat_axis=0, tiled=True)  30.8 us
    ppermute x6, starting transfers between devices, shift(): lax.ppermute(value, 'expert', [(i, (i + by) % unit_parts) for i in range(...  24.6 us
    ppermute x6, waiting for transfers between devices, shift(): lax.ppermute(value, 'expert', [(i, (i + by) % unit_parts) for i in range(...  24.6 us
    all_to_all x1, blocking collectives, body(): lax.all_to_all(outgoing, 'mp', split_axis=0, concat_axis=0, tiled=True)  21.7 us
    pallas_call x3, Pallas kernels, ffn(): pl.pallas_call(functools.partial(ffn_kernel, count), out_shape=[jax.Shape...  20.2 us
    all_to_all x1, waiting for transfers between devices, body(): lax.all_to_all(outputs, 'mp', split_axis=0, concat_axis=0, tiled=True)  13.9 us
    all_to_all x1, starting transfers between devices, body(): parts = lax.all_to_all(parts, 'mp', split_axis=0, concat_axis=0, tiled=True)  7.23 us
    all_to_all x1, starting transfers between devices, body(): lax.all_to_all(outputs, 'mp', split_axis=0, concat_axis=0, tiled=True)  3.67 us
  transfers between devices with their start and end apart: 8, of which 7 were waited for; matrix products, arithmetic and copies ran while one was open for 0% of the time, Pallas kernels for 13%

profile of v4, /device:TPU:448, one launch (start us, length us, event | category | flops | bytes accessed | tf_op | source)
XLA Modules:
  0.0 155.6 jit_solution(15717541210970101536)
XLA Ops:
  0.0 0.0 copy-start
  0.0 1.3 copy-done
  1.3 3.6 %convolution_convert_fusion = f16[256,2304]{1,0:T(8,128)(2,1)} fusion(bf16[288,2304]{1,0:T(8,128)(2,1)S(1)} %copy-done, bf16[1024,288]{0,1:T(8,128)(2,1)} %param.9, s32[256]{0:T(256)S(1)} %fusion.15), kind=kOutput, calls=%fused_computation | convolution fusion | flops 491659264 | bytes 3097600 | tf_op jit(solution)/shard_map/dot_general | solution.py:117
  4.9 0.0 copy-start.3
  4.9 7.2 %all-to-all-start = ((f16[8,32,2304]{2,1,0:T(8,128)(2,1)}), f16[8,32,2304]{2,1,0:T(8,128)(2,1)S(1)}, u32[]{:S(2)}, u32[]{:S(2)}) async-start(f16[8,32,2304]{2,1,0:T(8,128)(2,1)} %bitcast.36), calls=%async_computation | async-start | bytes 2359296 | tf_op jit(solution)/shard_map/all_to_all | solution.py:119
  12.2 0.0 copy-done.3
  12.2 0.0 copy-start.1
  12.2 0.1 copy.16
  12.3 0.1 eq.63
  12.4 0.1 fusion.6
  12.4 0.1 reduce_window_sum.11
  12.5 0.2 select_reduce_fusion
  12.7 0.1 reduce_sum.31
  12.8 0.1 copy.17
  12.9 0.0 copy-start.2
  12.9 30.8 %all-to-all-done = f16[8,32,2304]{2,1,0:T(8,128)(2,1)S(1)} async-done(((f16[8,32,2304]{2,1,0:T(8,128)(2,1)}), f16[8,32,2304]{2,1,0:T(8,128)(2,1)S(1)}, u32[]{:S(2)}, u32[]{:S(2)}) %all-to-all-start) | async-done | bytes 1179680 | tf_op jit(solution)/shard_map/all_to_all | solution.py:119
  43.7 0.2 convert_reduce_fusion
  43.9 0.0 copy-done.1
  43.9 0.1 multiply_reduce_fusion
  44.1 0.0 copy-done.2
  44.1 0.4 convolution_convert_fusion.1
  44.5 21.7 %all_to_all.15 = bf16[8,16,2304]{2,1,0:T(8,128)(2,1)S(1)} all-to-all(bf16[8,16,2304]{2,1,0:T(8,128)(2,1)S(1)} %bitcast.35), channel_id=1, replica_groups=mesh['dp'=16,'mp'=8,'expert'=4] {'mp'}, dimensions={0} | all-to-all | bytes 1179648 | tf_op jit(solution)/shard_map/all_to_all | solution.py:138
  66.2 4.9 %collective-permute-start.2 = (bf16[128,2304]{1,0:T(8,128)(2,1)S(1)}, bf16[128,2304]{1,0:T(8,128)(2,1)S(1)}, u32[]{:S(2)}, u32[]{:S(2)}) collective-permute-start(bf16[128,2304]{1,0:T(8,128)(2,1)S(1)} %bitcast.20), channel_id=1, source_target_pairs={{0,2},{1,3},{2,0},{3,1},{4,6},{5,7},{6,4},{7,5},{8,10},{9,11},{10,... | collective-permute-start | bytes 1769480 | tf_op jit(solution)/shard_map/ppermute | solution.py:143
  71.2 6.3 %shard_map.91 = bf16[128,2304]{1,0:T(8,128)(2,1)S(1)} custom-call(bf16[128,2304]{1,0:T(8,128)(2,1)S(1)} %bitcast.21, bf16[2304,1024]{1,0:T(8,128)(2,1)} %bitcast.24, bf16[2304,1024]{1,0:T(8,128)(2,1)} %bitcast.27, bf16[1024,2304]{1,0:T(8,128)(2,1)} %bitcast.30), custom_call_target="tpu_custom_call" | custom-call | flops 1811939328 | bytes 15335424 | tf_op jit(solution)/shard_map/pallas_call | solution.py:70
  77.5 2.5 %collective-permute-start = (bf16[128,2304]{1,0:T(8,128)(2,1)S(1)}, bf16[128,2304]{1,0:T(8,128)(2,1)S(1)}, u32[]{:S(2)}, u32[]{:S(2)}) collective-permute-start(bf16[128,2304]{1,0:T(8,128)(2,1)S(1)} %bitcast.22), channel_id=1, source_target_pairs={{0,1},{1,2},{2,3},{3,0},{4,5},{5,6},{6,7},{7,4},{8,9},{9,10},{10,1... | collective-permute-start | bytes 1769480 | tf_op jit(solution)/shard_map/ppermute | solution.py:143
  80.0 4.5 %collective-permute-start.1 = (bf16[128,2304]{1,0:T(8,128)(2,1)S(1)}, bf16[128,2304]{1,0:T(8,128)(2,1)S(1)}, u32[]{:S(2)}, u32[]{:S(2)}) collective-permute-start(bf16[128,2304]{1,0:T(8,128)(2,1)S(1)} %bitcast.23), channel_id=1, source_target_pairs={{0,3},{1,0},{2,1},{3,2},{4,7},{5,4},{6,5},{7,6},{8,11},{9,8},{10,9... | collective-permute-start | bytes 1769480 | tf_op jit(solution)/shard_map/ppermute | solution.py:143
  84.6 1.3 collective-permute-done.2.refs_0_
  85.9 6.3 %shard_map.92 = bf16[128,2304]{1,0:T(8,128)(2,1)S(1)} custom-call(bf16[128,2304]{1,0:T(8,128)(2,1)S(1)} %collective-permute-done.2.refs_0_, bf16[2304,1024]{1,0:T(8,128)(2,1)} %bitcast.25, bf16[2304,1024]{1,0:T(8,128)(2,1)} %bitcast.28, bf16[1024,2304]{1,0:T(8,128)(2,1)} %bitcast.31), custom_call_target="tpu_custom_call" | custom-call | flops 1811939328 | bytes 15335424 | tf_op jit(solution)/shard_map/pallas_call | solution.py:70
  92.2 5.0 %collective-permute-start.4 = (bf16[128,2304]{1,0:T(8,128)(2,1)S(1)}, bf16[128,2304]{1,0:T(8,128)(2,1)S(1)}, u32[]{:S(2)}, u32[]{:S(2)}) collective-permute-start(bf16[128,2304]{1,0:T(8,128)(2,1)S(1)} %shard_map.92), channel_id=1, source_target_pairs={{0,2},{1,3},{2,0},{3,1},{4,6},{5,7},{6,4},{7,5},{8,10},{9,11},{10,... | collective-permute-start | bytes 1769480 | tf_op jit(solution)/shard_map/ppermute | solution.py:143
  97.2 1.0 collective-permute-done.refs_0_
  98.2 11.1 %collective-permute-done.1.refs_1_ = bf16[128,2304]{1,0:T(8,128)(2,1)S(1)} collective-permute-done((bf16[128,2304]{1,0:T(8,128)(2,1)S(1)}, bf16[128,2304]{1,0:T(8,128)(2,1)S(1)}, u32[]{:S(2)}, u32[]{:S(2)}) %collective-permute-start.1) | collective-permute-done | bytes 589856 | tf_op jit(solution)/shard_map/ppermute | solution.py:143
  109.4 7.6 %shard_map.93 = (bf16[128,2304]{1,0:T(8,128)(2,1)S(1)}, bf16[128,2304]{1,0:T(8,128)(2,1)S(1)}) custom-call(bf16[128,2304]{1,0:T(8,128)(2,1)S(1)} %collective-permute-done.refs_0_, bf16[128,2304]{1,0:T(8,128)(2,1)S(1)} %collective-permute-done.1.refs_1_, bf16[2304,1024]{1,0:T(8,128)(2,1)} %bitcast.26, bf16[2304,1024]{1,0:T(8,128)(2,1)} %bitcast.29, ...), custom_call_target="tpu_custom_call" | custom-call | flops 3623878656 | bytes 16515072 | tf_op jit(solution)/shard_map/pallas_call | solution.py:70
  117.0 5.7 %collective-permute-start.3 = (bf16[128,2304]{1,0:T(8,128)(2,1)S(1)}, bf16[128,2304]{1,0:T(8,128)(2,1)S(1)}, u32[]{:S(2)}, u32[]{:S(2)}) collective-permute-start(bf16[128,2304]{1,0:T(8,128)(2,1)S(1)} %get-tuple-element.15), channel_id=1, source_target_pairs={{0,3},{1,0},{2,1},{3,2},{4,7},{5,4},{6,5},{7,6},{8,11},{9,8},{10,9... | collective-permute-start | bytes 1769480 | tf_op jit(solution)/shard_map/ppermute | solution.py:143
  122.7 0.0 collective-permute-done.4
  122.7 1.9 %collective-permute-start.5 = (bf16[128,2304]{1,0:T(8,128)(2,1)S(1)}, bf16[128,2304]{1,0:T(8,128)(2,1)S(1)}, u32[]{:S(2)}, u32[]{:S(2)}) collective-permute-start(bf16[128,2304]{1,0:T(8,128)(2,1)S(1)} %get-tuple-element.17), channel_id=1, source_target_pairs={{0,1},{1,2},{2,3},{3,0},{4,5},{5,6},{6,7},{7,4},{8,9},{9,10},{10,1... | collective-permute-start | bytes 1769480 | tf_op jit(solution)/shard_map/ppermute | solution.py:143
  124.7 5.4 %collective-permute-done.3 = bf16[128,2304]{1,0:T(8,128)(2,1)S(1)} collective-permute-done((bf16[128,2304]{1,0:T(8,128)(2,1)S(1)}, bf16[128,2304]{1,0:T(8,128)(2,1)S(1)}, u32[]{:S(2)}, u32[]{:S(2)}) %collective-permute-start.3) | collective-permute-done | bytes 589856 | tf_op jit(solution)/shard_map/ppermute | solution.py:143
  130.1 5.6 %collective-permute-done.5 = bf16[128,2304]{1,0:T(8,128)(2,1)S(1)} collective-permute-done((bf16[128,2304]{1,0:T(8,128)(2,1)S(1)}, bf16[128,2304]{1,0:T(8,128)(2,1)S(1)}, u32[]{:S(2)}, u32[]{:S(2)}) %collective-permute-start.5) | collective-permute-done | bytes 589856 | tf_op jit(solution)/shard_map/ppermute | solution.py:143
  135.7 1.1 add_convert_fusion
  136.8 0.0 copy-start.4
  136.8 3.7 %all-to-all-start.2 = ((bf16[8,16,2304]{2,1,0:T(8,128)(2,1)}), bf16[8,16,2304]{2,1,0:T(8,128)(2,1)S(1)}, u32[]{:S(2)}, u32[]{:S(2)}) async-start(bf16[8,16,2304]{2,1,0:T(8,128)(2,1)} %bitcast.9), calls=%async_computation.2 | async-start | bytes 1179648 | tf_op jit(solution)/shard_map/all_to_all | solution.py:163
  140.5 0.0 copy-done.4
  140.5 13.9 %all-to-all-done.2 = bf16[8,16,2304]{2,1,0:T(8,128)(2,1)S(1)} async-done(((bf16[8,16,2304]{2,1,0:T(8,128)(2,1)}), bf16[8,16,2304]{2,1,0:T(8,128)(2,1)S(1)}, u32[]{:S(2)}, u32[]{:S(2)}) %all-to-all-start.2) | async-done | bytes 589856 | tf_op jit(solution)/shard_map/all_to_all | solution.py:163
  154.4 0.3 convolution_multiply_fusion
  154.7 1.0 fusion.1
  (5 shorter events, 0.0 us)
Async XLA Ops:
  0.0 1.3 copy-start
  4.9 7.2 %copy-start.3 = (s32[32,2]{0,1:T(2,128)S(1)}, s32[32,2]{0,1:T(2,128)}, u32[]{:S(2)}) copy-start(s32[32,2]{0,1:T(2,128)} %param.16) | copy-start | bytes 772
  4.9 38.8 %all-to-all-start = ((f16[8,32,2304]{2,1,0:T(8,128)(2,1)}), f16[8,32,2304]{2,1,0:T(8,128)(2,1)S(1)}, u32[]{:S(2)}, u32[]{:S(2)}) async-start(f16[8,32,2304]{2,1,0:T(8,128)(2,1)} %bitcast.36), calls=%async_computation | async-start | bytes 2359296 | tf_op jit(solution)/shard_map/all_to_all | solution.py:119
  12.2 31.7 %copy-start.1 = (f32[32,2304]{1,0:T(8,128)S(1)}, f32[32,2304]{1,0:T(8,128)}, u32[]{:S(2)}) copy-start(f32[32,2304]{1,0:T(8,128)} %param.10) | copy-start | bytes 884740
  12.9 31.1 %copy-start.2 = (f32[2304]{0:T(1024)S(1)}, f32[2304]{0:T(1024)}, u32[]{:S(2)}) copy-start(f32[2304]{0:T(1024)} %param.12) | copy-start | bytes 27652
  66.2 19.7 %collective-permute-start.2 = (bf16[128,2304]{1,0:T(8,128)(2,1)S(1)}, bf16[128,2304]{1,0:T(8,128)(2,1)S(1)}, u32[]{:S(2)}, u32[]{:S(2)}) collective-permute-start(bf16[128,2304]{1,0:T(8,128)(2,1)S(1)} %bitcast.20), channel_id=1, source_target_pairs={{0,2},{1,3},{2,0},{3,1},{4,6},{5,7},{6,4},{7,5},{8,10},{9,11},{10,... | collective-permute-start | bytes 1769480 | tf_op jit(solution)/shard_map/ppermute | solution.py:143
  77.5 20.7 %collective-permute-start = (bf16[128,2304]{1,0:T(8,128)(2,1)S(1)}, bf16[128,2304]{1,0:T(8,128)(2,1)S(1)}, u32[]{:S(2)}, u32[]{:S(2)}) collective-permute-start(bf16[128,2304]{1,0:T(8,128)(2,1)S(1)} %bitcast.22), channel_id=1, source_target_pairs={{0,1},{1,2},{2,3},{3,0},{4,5},{5,6},{6,7},{7,4},{8,9},{9,10},{10,1... | collective-permute-start | bytes 1769480 | tf_op jit(solution)/shard_map/ppermute | solution.py:143
  80.0 29.4 %collective-permute-start.1 = (bf16[128,2304]{1,0:T(8,128)(2,1)S(1)}, bf16[128,2304]{1,0:T(8,128)(2,1)S(1)}, u32[]{:S(2)}, u32[]{:S(2)}) collective-permute-start(bf16[128,2304]{1,0:T(8,128)(2,1)S(1)} %bitcast.23), channel_id=1, source_target_pairs={{0,3},{1,0},{2,1},{3,2},{4,7},{5,4},{6,5},{7,6},{8,11},{9,8},{10,9... | collective-permute-start | bytes 1769480 | tf_op jit(solution)/shard_map/ppermute | solution.py:143
  92.2 30.5 %collective-permute-start.4 = (bf16[128,2304]{1,0:T(8,128)(2,1)S(1)}, bf16[128,2304]{1,0:T(8,128)(2,1)S(1)}, u32[]{:S(2)}, u32[]{:S(2)}) collective-permute-start(bf16[128,2304]{1,0:T(8,128)(2,1)S(1)} %shard_map.92), channel_id=1, source_target_pairs={{0,2},{1,3},{2,0},{3,1},{4,6},{5,7},{6,4},{7,5},{8,10},{9,11},{10,... | collective-permute-start | bytes 1769480 | tf_op jit(solution)/shard_map/ppermute | solution.py:143
  117.0 13.1 %collective-permute-start.3 = (bf16[128,2304]{1,0:T(8,128)(2,1)S(1)}, bf16[128,2304]{1,0:T(8,128)(2,1)S(1)}, u32[]{:S(2)}, u32[]{:S(2)}) collective-permute-start(bf16[128,2304]{1,0:T(8,128)(2,1)S(1)} %get-tuple-element.15), channel_id=1, source_target_pairs={{0,3},{1,0},{2,1},{3,2},{4,7},{5,4},{6,5},{7,6},{8,11},{9,8},{10,9... | collective-permute-start | bytes 1769480 | tf_op jit(solution)/shard_map/ppermute | solution.py:143
  122.7 13.0 %collective-permute-start.5 = (bf16[128,2304]{1,0:T(8,128)(2,1)S(1)}, bf16[128,2304]{1,0:T(8,128)(2,1)S(1)}, u32[]{:S(2)}, u32[]{:S(2)}) collective-permute-start(bf16[128,2304]{1,0:T(8,128)(2,1)S(1)} %get-tuple-element.17), channel_id=1, source_target_pairs={{0,1},{1,2},{2,3},{3,0},{4,5},{5,6},{6,7},{7,4},{8,9},{9,10},{10,1... | collective-permute-start | bytes 1769480 | tf_op jit(solution)/shard_map/ppermute | solution.py:143
  136.8 3.7 %copy-start.4 = (f32[32,2]{0,1:T(2,128)S(1)}, f32[32,2]{0,1:T(2,128)}, u32[]{:S(2)}) copy-start(f32[32,2]{0,1:T(2,128)} %param.17) | copy-start | bytes 772
  136.8 17.6 %all-to-all-start.2 = ((bf16[8,16,2304]{2,1,0:T(8,128)(2,1)}), bf16[8,16,2304]{2,1,0:T(8,128)(2,1)S(1)}, u32[]{:S(2)}, u32[]{:S(2)}) async-start(bf16[8,16,2304]{2,1,0:T(8,128)(2,1)} %bitcast.9), calls=%async_computation.2 | async-start | bytes 1179648 | tf_op jit(solution)/shard_map/all_to_all | solution.py:163

commit v5 on v3

--- a/solution.py
+++ b/solution.py
@@ -15,47 +15,52 @@
 OUT_CHUNK = 1152
 
 
+def load_kernel(*refs):
+    count = (len(refs) - 1) // 2
+    sems = refs[-1]
+    copies = [
+        pltpu.make_async_copy(refs[i], refs[count + i], sems.at[i]) for i in range(count)
+    ]
+    for copy in copies:
+        copy.start()
+    for copy in copies:
+        copy.wait()
+
+
+def load(*weights):
+    hbm = pl.BlockSpec(memory_space=pltpu.HBM)
+    vmem = pl.BlockSpec(memory_space=pltpu.VMEM)
+    total = sum(w.size * w.dtype.itemsize for w in weights)
+    return pl.pallas_call(
+        load_kernel,
+        out_shape=[pltpu.VMEM(w.shape, w.dtype) for w in weights],
+        in_specs=[hbm] * len(weights),
+        out_specs=[vmem] * len(weights),
+        scratch_shapes=[pltpu.SemaphoreType.DMA((len(weights),))],
+        compiler_params=pltpu.CompilerParams(vmem_limit_bytes=20 << 20),
+        cost_estimate=pl.CostEstimate(flops=0, transcendentals=0, bytes_accessed=2 * total),
+    )(*(pltpu.with_memory_space_constraint(w, pltpu.HBM) for w in weights))
+
+
 def ffn_kernel(count, *refs):
     row_refs, refs = refs[:count], refs[count:]
-    (gate_hbm, up_hbm, down_hbm), refs = refs[:3], refs[3:]
+    (gate_ref, up_ref, down_ref), refs = refs[:3], refs[3:]
     out_refs, refs = refs[:count], refs[count:]
-    rows_ref, act_ref, gate_ref, up_ref, down_ref, gate_sem, up_sem, down_sem = refs
+    act_ref = refs[0]
     depth = row_refs[0].shape[0]
-    unit_steps = gate_sem.shape[0]
-    out_steps = down_sem.shape[0]
-
-    def columns(step, width):
-        return pl.ds(step * width, width)
-
-    gate_copies, up_copies, down_copies = [], [], []
-    for step in range(unit_steps):
-        at = columns(step, UNIT_CHUNK)
-        gate_copies.append(
-            pltpu.make_async_copy(gate_hbm.at[:, at], gate_ref.at[:, at], gate_sem.at[step])
-        )
-        up_copies.append(pltpu.make_async_copy(up_hbm.at[:, at], up_ref.at[:, at], up_sem.at[step]))
-    for step in range(out_steps):
-        at = columns(step, OUT_CHUNK)
-        down_copies.append(
-            pltpu.make_async_copy(down_hbm.at[:, at], down_ref.at[:, at], down_sem.at[step])
-        )
-    for step in range(unit_steps):
-        gate_copies[step].start()
-        up_copies[step].start()
-    for step in range(out_steps):
-        down_copies[step].start()
-    for piece in range(count):
-        rows_ref[pl.ds(piece * depth, depth), :] = row_refs[piece][...]
-    for step in range(unit_steps):
-        at = columns(step, UNIT_CHUNK)
-        gate_copies[step].wait()
-        up_copies[step].wait()
+    if count == 1:
+        rows_ref = row_refs[0]
+    else:
+        rows_ref = refs[1]
+        for piece in range(count):
+            rows_ref[pl.ds(piece * depth, depth), :] = row_refs[piece][...]
+    for start in range(0, act_ref.shape[1], UNIT_CHUNK):
+        at = pl.ds(start, UNIT_CHUNK)
         gate = jnp.dot(rows_ref[...], gate_ref[:, at], preferred_element_type=jnp.float32)
         up = jnp.dot(rows_ref[...], up_ref[:, at], preferred_element_type=jnp.float32)
         act_ref[:, at] = (gate / (1.0 + jnp.exp(-gate)) * up).astype(jnp.bfloat16)
-    for step in range(out_steps):
-        at = columns(step, OUT_CHUNK)
-        down_copies[step].wait()
+    for start in range(0, down_ref.shape[1], OUT_CHUNK):
+        at = pl.ds(start, OUT_CHUNK)
         out = jnp.dot(act_ref[...], down_ref[:, at], preferred_element_type=jnp.float32)
         for piece in range(count):
             out_refs[piece][:, at] = out[piece * depth : (piece + 1) * depth].astype(jnp.bfloat16)
@@ -66,29 +71,22 @@
     depth, features = pieces[0].shape
     units = weights[0].shape[1]
     vmem = pl.BlockSpec(memory_space=pltpu.VMEM)
-    hbm = pl.BlockSpec(memory_space=pltpu.HBM)
+    scratch = [pltpu.VMEM((count * depth, units), jnp.bfloat16)]
+    if count > 1:
+        scratch.append(pltpu.VMEM((count * depth, features), jnp.bfloat16))
     return pl.pallas_call(
         functools.partial(ffn_kernel, count),
         out_shape=[jax.ShapeDtypeStruct((depth, features), jnp.bfloat16)] * count,
-        in_specs=[vmem] * count + [hbm] * 3,
+        in_specs=[vmem] * (count + 3),
         out_specs=[vmem] * count,
-        scratch_shapes=[
-            pltpu.VMEM((count * depth, features), jnp.bfloat16),
-            pltpu.VMEM((count * depth, units), jnp.bfloat16),
-            pltpu.VMEM((features, units), jnp.bfloat16),
-            pltpu.VMEM((features, units), jnp.bfloat16),
-            pltpu.VMEM((units, features), jnp.bfloat16),
-            pltpu.SemaphoreType.DMA((units // UNIT_CHUNK,)),
-            pltpu.SemaphoreType.DMA((units // UNIT_CHUNK,)),
-            pltpu.SemaphoreType.DMA((features // OUT_CHUNK,)),
-        ],
-        compiler_params=pltpu.CompilerParams(vmem_limit_bytes=40 << 20),
+        scratch_shapes=scratch,
+        compiler_params=pltpu.CompilerParams(vmem_limit_bytes=24 << 20),
         cost_estimate=pl.CostEstimate(
             flops=6 * count * depth * features * units,
             transcendentals=count * depth * units,
             bytes_accessed=6 * features * units + 4 * count * depth * features,
         ),
-    )(*pieces, *(pltpu.with_memory_space_constraint(w, pltpu.HBM) for w in weights))
+    )(*pieces, *weights)
 
 
 def body(
@@ -132,7 +130,8 @@
     outgoing = outgoing.reshape(model_parts, MOST, features)
     arrived = lax.all_to_all(outgoing, "mp", split_axis=0, concat_axis=0, tiled=True)
     own = arrived.reshape(model_parts * MOST, features)
-    weights = (gate_weight[0], up_weight[0], down_weight[0])
+
+    weights = load(gate_weight[0], up_weight[0], down_weight[0])
 
     def shift(value, by):
         return lax.ppermute(
@@ -149,9 +148,9 @@
     far_rows = lax.optimization_barrier((far_rows, before_sum))[0]
     (far_sum,) = ffn([far_rows], *weights)
     back_far = shift(far_sum, 2)
-    outputs = own_sum.astype(jnp.float32)
-    for value in (back_after, back_before, back_far):
-        outputs += value.astype(jnp.float32)
+    near = own_sum.astype(jnp.float32)
+    near = near + back_after.astype(jnp.float32) + back_before.astype(jnp.float32)
+    outputs = lax.optimization_barrier(near) + back_far.astype(jnp.float32)
     outputs = outputs.astype(jnp.bfloat16).reshape(model_parts, MOST, features)
     outputs = lax.all_to_all(outputs, "mp", split_axis=0, concat_axis=0, tiled=True)
     expert_out = outputs.reshape(EXPERTS * MOST, features)

time: 160 us -> 147 us (0.919)
  the two profiles are of different devices: /device:TPU:1 before, /device:TPU:448 now
where the time goes in v5:
time: 147 us; the launch traced here: 144 us
  waiting for transfers between devices  68.5 us (47%)
  starting transfers between devices  33 us (22%)
  blocking collectives  21.7 us (15%)
  Pallas kernels  13.4 us (9%)
  matrix products  3.49 us (2%)
  local copies, waits for them, and re-layouts  1.96 us (1%)
  other arithmetic  1.79 us (1%)
    all_to_all x1, waiting for transfers between devices, body(): parts = lax.all_to_all(parts, 'mp', split_axis=0, concat_axis=0, tiled=True)  30.8 us
    ppermute x6, waiting for transfers between devices, shift(): lax.ppermute(value, 'expert', [(i, (i + by) % unit_parts) for i in range(...  23.8 us
    ppermute x6, starting transfers between devices, shift(): lax.ppermute(value, 'expert', [(i, (i + by) % unit_parts) for i in range(...  22.1 us
    all_to_all x1, blocking collectives, body(): lax.all_to_all(outgoing, 'mp', split_axis=0, concat_axis=0, tiled=True)  21.7 us
    all_to_all x1, waiting for transfers between devices, body(): lax.all_to_all(outputs, 'mp', split_axis=0, concat_axis=0, tiled=True)  13.9 us
    pallas_call x3, Pallas kernels, ffn(): pl.pallas_call(functools.partial(ffn_kernel, count), out_shape=[jax.Shape...  8.24 us
    all_to_all x1, starting transfers between devices, body(): parts = lax.all_to_all(parts, 'mp', split_axis=0, concat_axis=0, tiled=True)  7.23 us
    pallas_call x1, Pallas kernels, load(): pl.pallas_call(load_kernel, out_shape=[pltpu.VMEM(w.shape, w.dtype) for w...  5.15 us
  transfers between devices with their start and end apart: 8, of which 5 were waited for; matrix products, arithmetic and copies ran while one was open for 1% of the time, Pallas kernels for 9%

profile of v5, /device:TPU:448, one launch (start us, length us, event | category | flops | bytes accessed | tf_op | source)
XLA Modules:
  0.0 144.0 jit_solution(7396812272206679546)
XLA Ops:
  0.0 0.0 copy-start
  0.0 1.5 %copy.17 = bf16[1024,288]{1,0:T(8,128)(2,1)S(1)} copy(bf16[1024,288]{0,1:T(8,128)(2,1)} %param.9) | data formatting | bytes 1179648 | tf_op args[0]
  1.6 0.0 copy-done
  1.6 1.8 %convolution_convert_fusion = f16[256,2304]{1,0:T(8,128)(2,1)} fusion(bf16[256,288]{1,0:T(8,128)(2,1)S(1)} %bitcast.34, bf16[288,2304]{1,0:T(8,128)(2,1)S(1)} %copy-done), kind=kOutput, calls=%fused_computation | convolution fusion | flops 340328448 | bytes 2654208 | tf_op jit(solution)/shard_map/dot_general | solution.py:110
  3.4 0.0 copy-start.3
  3.4 7.2 %all-to-all-start = ((f16[8,32,2304]{2,1,0:T(8,128)(2,1)}), f16[8,32,2304]{2,1,0:T(8,128)(2,1)S(1)}, u32[]{:S(2)}, u32[]{:S(2)}) async-start(f16[8,32,2304]{2,1,0:T(8,128)(2,1)} %bitcast.31), calls=%async_computation | async-start | bytes 2359296 | tf_op jit(solution)/shard_map/all_to_all | solution.py:112
  10.6 0.0 copy-done.3
  10.6 0.0 copy-start.1
  10.6 0.1 copy.18
  10.7 0.1 eq.45
  10.8 0.1 fusion.4
  10.9 0.1 reduce_window_sum.11
  11.0 0.2 select_reduce_fusion
  11.2 0.1 reduce_sum.31
  11.3 0.1 copy.19
  11.4 0.0 copy-start.2
  11.4 30.8 %all-to-all-done = f16[8,32,2304]{2,1,0:T(8,128)(2,1)S(1)} async-done(((f16[8,32,2304]{2,1,0:T(8,128)(2,1)}), f16[8,32,2304]{2,1,0:T(8,128)(2,1)S(1)}, u32[]{:S(2)}, u32[]{:S(2)}) %all-to-all-start) | async-done | bytes 1179680 | tf_op jit(solution)/shard_map/all_to_all | solution.py:112
  42.2 0.2 convert_reduce_fusion
  42.4 0.0 copy-done.1
  42.4 0.1 multiply_reduce_fusion
  42.5 0.0 copy-done.2
  42.5 0.4 convolution_convert_fusion.1
  43.0 21.7 %all_to_all.15 = bf16[8,16,2304]{2,1,0:T(8,128)(2,1)S(1)} all-to-all(bf16[8,16,2304]{2,1,0:T(8,128)(2,1)S(1)} %bitcast.32), channel_id=1, replica_groups=mesh['dp'=16,'mp'=8,'expert'=4] {'mp'}, dimensions={0} | all-to-all | bytes 1179648 | tf_op jit(solution)/shard_map/all_to_all | solution.py:131
  64.7 3.4 %collective-permute-start = (bf16[128,2304]{1,0:T(8,128)(2,1)S(1)}, bf16[128,2304]{1,0:T(8,128)(2,1)S(1)}, u32[]{:S(2)}, u32[]{:S(2)}) collective-permute-start(bf16[128,2304]{1,0:T(8,128)(2,1)S(1)} %bitcast.22), channel_id=1, source_target_pairs={{0,1},{1,2},{2,3},{3,0},{4,5},{5,6},{6,7},{7,4},{8,9},{9,10},{10,1... | collective-permute-start | bytes 1769480 | tf_op jit(solution)/shard_map/ppermute | solution.py:137
  68.1 3.7 %collective-permute-start.1 = (bf16[128,2304]{1,0:T(8,128)(2,1)S(1)}, bf16[128,2304]{1,0:T(8,128)(2,1)S(1)}, u32[]{:S(2)}, u32[]{:S(2)}) collective-permute-start(bf16[128,2304]{1,0:T(8,128)(2,1)S(1)} %bitcast.23), channel_id=1, source_target_pairs={{0,3},{1,0},{2,1},{3,2},{4,7},{5,4},{6,5},{7,6},{8,11},{9,8},{10,9... | collective-permute-start | bytes 1769480 | tf_op jit(solution)/shard_map/ppermute | solution.py:137
  71.8 5.1 %shard_map.91 = (bf16[2304,1024]{1,0:T(8,128)(2,1)S(1)}, bf16[2304,1024]{1,0:T(8,128)(2,1)S(1)}, bf16[1024,2304]{1,0:T(8,128)(2,1)S(1)}) custom-call(bf16[2304,1024]{1,0:T(8,128)(2,1)} %bitcast.28, bf16[2304,1024]{1,0:T(8,128)(2,1)} %bitcast.29, bf16[1024,2304]{1,0:T(8,128)(2,1)} %bitcast.30), custom_call_target="tpu_custom_call" | custom-call | bytes 28311552 | tf_op jit(solution)/shard_map/pallas_call | solution.py:34
  76.9 2.1 %shard_map.92 = bf16[128,2304]{1,0:T(8,128)(2,1)S(1)} custom-call(bf16[128,2304]{1,0:T(8,128)(2,1)S(1)} %bitcast.24, bf16[2304,1024]{1,0:T(8,128)(2,1)S(1)} %get-tuple-element.12.refs_1_.refs_2_, bf16[2304,1024]{1,0:T(8,128)(2,1)S(1)} %get-tuple-element.13.refs_2_.refs_3_, bf16[1024,2304]{1,0:T(8,128)(2,1)S(1)} %get-tuple-element.14.refs_3_.refs_4_), custom_call_target="tpu_custom_call" | custom-call | flops 1811939328 | bytes 15335424 | tf_op jit(solution)/shard_map/pallas_call | solution.py:77
  79.1 3.7 %collective-permute-start.4 = (bf16[128,2304]{1,0:T(8,128)(2,1)S(1)}, bf16[128,2304]{1,0:T(8,128)(2,1)S(1)}, u32[]{:S(2)}, u32[]{:S(2)}) collective-permute-start(bf16[128,2304]{1,0:T(8,128)(2,1)S(1)} %bitcast.25), channel_id=1, source_target_pairs={{0,2},{1,3},{2,0},{3,1},{4,6},{5,7},{6,4},{7,5},{8,10},{9,11},{10,... | collective-permute-start | bytes 1769480 | tf_op jit(solution)/shard_map/ppermute | solution.py:137
  82.8 0.0 collective-permute-done.refs_0_
  82.8 11.9 %collective-permute-done.1.refs_1_ = bf16[128,2304]{1,0:T(8,128)(2,1)S(1)} collective-permute-done((bf16[128,2304]{1,0:T(8,128)(2,1)S(1)}, bf16[128,2304]{1,0:T(8,128)(2,1)S(1)}, u32[]{:S(2)}, u32[]{:S(2)}) %collective-permute-start.1) | collective-permute-done | bytes 589856 | tf_op jit(solution)/shard_map/ppermute | solution.py:137
  94.7 4.0 %shard_map.93 = (bf16[128,2304]{1,0:T(8,128)(2,1)S(1)}, bf16[128,2304]{1,0:T(8,128)(2,1)S(1)}) custom-call(bf16[128,2304]{1,0:T(8,128)(2,1)S(1)} %collective-permute-done.refs_0_, bf16[128,2304]{1,0:T(8,128)(2,1)S(1)} %collective-permute-done.1.refs_1_, bf16[2304,1024]{1,0:T(8,128)(2,1)S(1)} %get-tuple-element.12.refs_1_.refs_2_, ...), custom_call_target="tpu_custom_call" | custom-call | flops 3623878656 | bytes 16515072 | tf_op jit(solution)/shard_map/pallas_call | solution.py:77
  98.7 6.0 %collective-permute-start.2 = (bf16[128,2304]{1,0:T(8,128)(2,1)S(1)}, bf16[128,2304]{1,0:T(8,128)(2,1)S(1)}, u32[]{:S(2)}, u32[]{:S(2)}) collective-permute-start(bf16[128,2304]{1,0:T(8,128)(2,1)S(1)} %get-tuple-element.15), channel_id=1, source_target_pairs={{0,3},{1,0},{2,1},{3,2},{4,7},{5,4},{6,5},{7,6},{8,11},{9,8},{10,9... | collective-permute-start | bytes 1769480 | tf_op jit(solution)/shard_map/ppermute | solution.py:137
  104.7 1.9 %collective-permute-start.3 = (bf16[128,2304]{1,0:T(8,128)(2,1)S(1)}, bf16[128,2304]{1,0:T(8,128)(2,1)S(1)}, u32[]{:S(2)}, u32[]{:S(2)}) collective-permute-start(bf16[128,2304]{1,0:T(8,128)(2,1)S(1)} %get-tuple-element.16), channel_id=1, source_target_pairs={{0,1},{1,2},{2,3},{3,0},{4,5},{5,6},{6,7},{7,4},{8,9},{9,10},{10,1... | collective-permute-start | bytes 1769480 | tf_op jit(solution)/shard_map/ppermute | solution.py:137
  106.7 0.0 collective-permute-done.4.refs_0_
  106.7 2.1 %shard_map.94 = bf16[128,2304]{1,0:T(8,128)(2,1)S(1)} custom-call(bf16[128,2304]{1,0:T(8,128)(2,1)S(1)} %collective-permute-done.4.refs_0_, bf16[2304,1024]{1,0:T(8,128)(2,1)S(1)} %get-tuple-element.12.refs_1_.refs_2_, bf16[2304,1024]{1,0:T(8,128)(2,1)S(1)} %get-tuple-element.13.refs_2_.refs_3_, bf16[1024,2304]{1,0:T(8,128)(2,1)S(1)} %get-tuple-element.14.refs_3_.refs_4_), custom_call_target="tpu_custom_call" | custom-call | flops 1811939328 | bytes 15335424 | tf_op jit(solution)/shard_map/pallas_call | solution.py:77
  108.8 3.4 %collective-permute-start.5 = (bf16[128,2304]{1,0:T(8,128)(2,1)S(1)}, bf16[128,2304]{1,0:T(8,128)(2,1)S(1)}, u32[]{:S(2)}, u32[]{:S(2)}) collective-permute-start(bf16[128,2304]{1,0:T(8,128)(2,1)S(1)} %shard_map.94), channel_id=1, source_target_pairs={{0,2},{1,3},{2,0},{3,1},{4,6},{5,7},{6,4},{7,5},{8,10},{9,11},{10,... | collective-permute-start | bytes 1769480 | tf_op jit(solution)/shard_map/ppermute | solution.py:137
  112.2 10.8 %collective-permute-done.2 = bf16[128,2304]{1,0:T(8,128)(2,1)S(1)} collective-permute-done((bf16[128,2304]{1,0:T(8,128)(2,1)S(1)}, bf16[128,2304]{1,0:T(8,128)(2,1)S(1)}, u32[]{:S(2)}, u32[]{:S(2)}) %collective-permute-start.2) | collective-permute-done | bytes 589856 | tf_op jit(solution)/shard_map/ppermute | solution.py:137
  123.0 1.0 collective-permute-done.3
  124.1 0.2 convert_add_fusion
  124.2 0.0 collective-permute-done.5
  124.3 0.9 add_convert_fusion
  125.2 0.0 copy-start.4
  125.2 3.7 %all-to-all-start.2 = ((bf16[8,16,2304]{2,1,0:T(8,128)(2,1)}), bf16[8,16,2304]{2,1,0:T(8,128)(2,1)S(1)}, u32[]{:S(2)}, u32[]{:S(2)}) async-start(bf16[8,16,2304]{2,1,0:T(8,128)(2,1)} %bitcast.11), calls=%async_computation.2 | async-start | bytes 1179648 | tf_op jit(solution)/shard_map/all_to_all | solution.py:155
  128.9 0.0 copy-done.4
  128.9 13.9 %all-to-all-done.2 = bf16[8,16,2304]{2,1,0:T(8,128)(2,1)S(1)} async-done(((bf16[8,16,2304]{2,1,0:T(8,128)(2,1)}), bf16[8,16,2304]{2,1,0:T(8,128)(2,1)S(1)}, u32[]{:S(2)}, u32[]{:S(2)}) %all-to-all-start.2) | async-done | bytes 589856 | tf_op jit(solution)/shard_map/all_to_all | solution.py:155
  142.8 0.3 convolution_multiply_fusion
  143.0 1.0 fusion.1
  (5 shorter events, 0.1 us)
Async XLA Ops:
  0.0 1.6 %copy-start = (bf16[288,2304]{1,0:T(8,128)(2,1)S(1)}, bf16[288,2304]{1,0:T(8,128)(2,1)}, u32[]{:S(2)}) copy-start(bf16[288,2304]{1,0:T(8,128)(2,1)} %param.11) | copy-start | bytes 3981316
  3.4 7.2 %copy-start.3 = (s32[32,2]{0,1:T(2,128)S(1)}, s32[32,2]{0,1:T(2,128)}, u32[]{:S(2)}) copy-start(s32[32,2]{0,1:T(2,128)} %param.16) | copy-start | bytes 772
  3.4 38.8 %all-to-all-start = ((f16[8,32,2304]{2,1,0:T(8,128)(2,1)}), f16[8,32,2304]{2,1,0:T(8,128)(2,1)S(1)}, u32[]{:S(2)}, u32[]{:S(2)}) async-start(f16[8,32,2304]{2,1,0:T(8,128)(2,1)} %bitcast.31), calls=%async_computation | async-start | bytes 2359296 | tf_op jit(solution)/shard_map/all_to_all | solution.py:112
  10.6 31.7 %copy-start.1 = (f32[32,2304]{1,0:T(8,128)S(1)}, f32[32,2304]{1,0:T(8,128)}, u32[]{:S(2)}) copy-start(f32[32,2304]{1,0:T(8,128)} %param.10) | copy-start | bytes 884740
  11.4 31.1 %copy-start.2 = (f32[2304]{0:T(1024)S(1)}, f32[2304]{0:T(1024)}, u32[]{:S(2)}) copy-start(f32[2304]{0:T(1024)} %param.12) | copy-start | bytes 27652
  64.7 18.1 %collective-permute-start = (bf16[128,2304]{1,0:T(8,128)(2,1)S(1)}, bf16[128,2304]{1,0:T(8,128)(2,1)S(1)}, u32[]{:S(2)}, u32[]{:S(2)}) collective-permute-start(bf16[128,2304]{1,0:T(8,128)(2,1)S(1)} %bitcast.22), channel_id=1, source_target_pairs={{0,1},{1,2},{2,3},{3,0},{4,5},{5,6},{6,7},{7,4},{8,9},{9,10},{10,1... | collective-permute-start | bytes 1769480 | tf_op jit(solution)/shard_map/ppermute | solution.py:137
  68.1 26.6 %collective-permute-start.1 = (bf16[128,2304]{1,0:T(8,128)(2,1)S(1)}, bf16[128,2304]{1,0:T(8,128)(2,1)S(1)}, u32[]{:S(2)}, u32[]{:S(2)}) collective-permute-start(bf16[128,2304]{1,0:T(8,128)(2,1)S(1)} %bitcast.23), channel_id=1, source_target_pairs={{0,3},{1,0},{2,1},{3,2},{4,7},{5,4},{6,5},{7,6},{8,11},{9,8},{10,9... | collective-permute-start | bytes 1769480 | tf_op jit(solution)/shard_map/ppermute | solution.py:137
  79.1 27.6 %collective-permute-start.4 = (bf16[128,2304]{1,0:T(8,128)(2,1)S(1)}, bf16[128,2304]{1,0:T(8,128)(2,1)S(1)}, u32[]{:S(2)}, u32[]{:S(2)}) collective-permute-start(bf16[128,2304]{1,0:T(8,128)(2,1)S(1)} %bitcast.25), channel_id=1, source_target_pairs={{0,2},{1,3},{2,0},{3,1},{4,6},{5,7},{6,4},{7,5},{8,10},{9,11},{10,... | collective-permute-start | bytes 1769480 | tf_op jit(solution)/shard_map/ppermute | solution.py:137
  98.7 24.3 %collective-permute-start.2 = (bf16[128,2304]{1,0:T(8,128)(2,1)S(1)}, bf16[128,2304]{1,0:T(8,128)(2,1)S(1)}, u32[]{:S(2)}, u32[]{:S(2)}) collective-permute-start(bf16[128,2304]{1,0:T(8,128)(2,1)S(1)} %get-tuple-element.15), channel_id=1, source_target_pairs={{0,3},{1,0},{2,1},{3,2},{4,7},{5,4},{6,5},{7,6},{8,11},{9,8},{10,9... | collective-permute-start | bytes 1769480 | tf_op jit(solution)/shard_map/ppermute | solution.py:137
  104.7 19.3 %collective-permute-start.3 = (bf16[128,2304]{1,0:T(8,128)(2,1)S(1)}, bf16[128,2304]{1,0:T(8,128)(2,1)S(1)}, u32[]{:S(2)}, u32[]{:S(2)}) collective-permute-start(bf16[128,2304]{1,0:T(8,128)(2,1)S(1)} %get-tuple-element.16), channel_id=1, source_target_pairs={{0,1},{1,2},{2,3},{3,0},{4,5},{5,6},{6,7},{7,4},{8,9},{9,10},{10,1... | collective-permute-start | bytes 1769480 | tf_op jit(solution)/shard_map/ppermute | solution.py:137
  108.8 15.4 %collective-permute-start.5 = (bf16[128,2304]{1,0:T(8,128)(2,1)S(1)}, bf16[128,2304]{1,0:T(8,128)(2,1)S(1)}, u32[]{:S(2)}, u32[]{:S(2)}) collective-permute-start(bf16[128,2304]{1,0:T(8,128)(2,1)S(1)} %shard_map.94), channel_id=1, source_target_pairs={{0,2},{1,3},{2,0},{3,1},{4,6},{5,7},{6,4},{7,5},{8,10},{9,11},{10,... | collective-permute-start | bytes 1769480 | tf_op jit(solution)/shard_map/ppermute | solution.py:137
  125.2 3.7 %copy-start.4 = (f32[32,2]{0,1:T(2,128)S(1)}, f32[32,2]{0,1:T(2,128)}, u32[]{:S(2)}) copy-start(f32[32,2]{0,1:T(2,128)} %param.17) | copy-start | bytes 772
  125.2 17.6 %all-to-all-start.2 = ((bf16[8,16,2304]{2,1,0:T(8,128)(2,1)}), bf16[8,16,2304]{2,1,0:T(8,128)(2,1)S(1)}, u32[]{:S(2)}, u32[]{:S(2)}) async-start(bf16[8,16,2304]{2,1,0:T(8,128)(2,1)} %bitcast.11), calls=%async_computation.2 | async-start | bytes 1179648 | tf_op jit(solution)/shard_map/all_to_all | solution.py:155

commit v6 on v5

--- a/solution.py
+++ b/solution.py
@@ -89,6 +89,82 @@
     )(*pieces, *weights)
 
 
+def stream_ffn_kernel(count, *refs):
+    row_refs, refs = refs[:count], refs[count:]
+    (gate_hbm, up_hbm, down_hbm), refs = refs[:3], refs[3:]
+    out_refs, refs = refs[:count], refs[count:]
+    rows_ref, act_ref, gate_ref, up_ref, down_ref, gate_sem, up_sem, down_sem = refs
+    depth = row_refs[0].shape[0]
+    unit_steps = gate_sem.shape[0]
+    out_steps = down_sem.shape[0]
+
+    def columns(step, width):
+        return pl.ds(step * width, width)
+
+    gate_copies, up_copies, down_copies = [], [], []
+    for step in range(unit_steps):
+        at = columns(step, UNIT_CHUNK)
+        gate_copies.append(
+            pltpu.make_async_copy(gate_hbm.at[:, at], gate_ref.at[:, at], gate_sem.at[step])
+        )
+        up_copies.append(pltpu.make_async_copy(up_hbm.at[:, at], up_ref.at[:, at], up_sem.at[step]))
+    for step in range(out_steps):
+        at = columns(step, OUT_CHUNK)
+        down_copies.append(
+            pltpu.make_async_copy(down_hbm.at[:, at], down_ref.at[:, at], down_sem.at[step])
+        )
+    for step in range(unit_steps):
+        gate_copies[step].start()
+        up_copies[step].start()
+    for step in range(out_steps):
+        down_copies[step].start()
+    for piece in range(count):
+        rows_ref[pl.ds(piece * depth, depth), :] = row_refs[piece][...]
+    for step in range(unit_steps):
+        at = columns(step, UNIT_CHUNK)
+        gate_copies[step].wait()
+        up_copies[step].wait()
+        gate = jnp.dot(rows_ref[...], gate_ref[:, at], preferred_element_type=jnp.float32)
+        up = jnp.dot(rows_ref[...], up_ref[:, at], preferred_element_type=jnp.float32)
+        act_ref[:, at] = (gate / (1.0 + jnp.exp(-gate)) * up).astype(jnp.bfloat16)
+    for step in range(out_steps):
+        at = columns(step, OUT_CHUNK)
+        down_copies[step].wait()
+        out = jnp.dot(act_ref[...], down_ref[:, at], preferred_element_type=jnp.float32)
+        for piece in range(count):
+            out_refs[piece][:, at] = out[piece * depth : (piece + 1) * depth].astype(jnp.bfloat16)
+
+
+def stream_ffn(pieces, *weights):
+    count = len(pieces)
+    depth, features = pieces[0].shape
+    units = weights[0].shape[1]
+    vmem = pl.BlockSpec(memory_space=pltpu.VMEM)
+    hbm = pl.BlockSpec(memory_space=pltpu.HBM)
+    return pl.pallas_call(
+        functools.partial(stream_ffn_kernel, count),
+        out_shape=[jax.ShapeDtypeStruct((depth, features), jnp.bfloat16)] * count,
+        in_specs=[vmem] * count + [hbm] * 3,
+        out_specs=[vmem] * count,
+        scratch_shapes=[
+            pltpu.VMEM((count * depth, features), jnp.bfloat16),
+            pltpu.VMEM((count * depth, units), jnp.bfloat16),
+            pltpu.VMEM((features, units), jnp.bfloat16),
+            pltpu.VMEM((features, units), jnp.bfloat16),
+            pltpu.VMEM((units, features), jnp.bfloat16),
+            pltpu.SemaphoreType.DMA((units // UNIT_CHUNK,)),
+            pltpu.SemaphoreType.DMA((units // UNIT_CHUNK,)),
+            pltpu.SemaphoreType.DMA((features // OUT_CHUNK,)),
+        ],
+        compiler_params=pltpu.CompilerParams(vmem_limit_bytes=40 << 20),
+        cost_estimate=pl.CostEstimate(
+            flops=6 * count * depth * features * units,
+            transcendentals=count * depth * units,
+            bytes_accessed=6 * features * units + 4 * count * depth * features,
+        ),
+    )(*pieces, *(pltpu.with_memory_space_constraint(w, pltpu.HBM) for w in weights))
+
+
 def body(
     attn_out,
     residual,
@@ -104,6 +180,20 @@
     unit_parts = lax.axis_size("expert")
     row_count = residual.shape[0]
     features = residual.shape[1]
+    def shift(value, by):
+        return lax.ppermute(
+            value, "expert", [(i, (i + by) % unit_parts) for i in range(unit_parts)]
+        )
+
+    expert_ids = routes.reshape(-1)
+    onehot = (expert_ids[:, None] == jnp.arange(EXPERTS, dtype=jnp.int32)[None, :]).astype(
+        jnp.int32
+    )
+    before = jnp.cumsum(onehot, axis=0) - onehot
+    position = jnp.sum(before * onehot, axis=1)
+    target = (expert_ids * MOST + position).reshape(row_count, 2)
+    far_target = shift(target, 2)
+    residual, far_target = lax.optimization_barrier((residual, far_target))
     blocks = attn_out.reshape(model_parts, unit_parts, row_count, attn_out.shape[1])
     picked = lax.dynamic_index_in_dim(blocks, lax.axis_index("expert"), axis=1, keepdims=False)
     picked = picked.reshape(model_parts * row_count, attn_out.shape[1])
@@ -113,40 +203,37 @@
     hidden_state = residual + jnp.sum(parts, axis=0, dtype=jnp.float32)
     inverse_rms = lax.rsqrt(jnp.mean(hidden_state * hidden_state, axis=1, keepdims=True) + EPSILON)
     normed = (hidden_state * inverse_rms * norm_gain).astype(jnp.bfloat16)
-    expert_ids = routes.reshape(-1)
-    onehot = (expert_ids[:, None] == jnp.arange(EXPERTS, dtype=jnp.int32)[None, :]).astype(
-        jnp.int32
-    )
-    before = jnp.cumsum(onehot, axis=0) - onehot
-    position = jnp.sum(before * onehot, axis=1)
-    target = (expert_ids * MOST + position).reshape(row_count, 2)
     slots = jnp.arange(EXPERTS * MOST, dtype=jnp.int32)
-    first = target[:, 0][:, None] == slots[None, :]
-    second = target[:, 1][:, None] == slots[None, :]
-    placement = (first | second).astype(jnp.bfloat16)
-    outgoing = lax.dot_general(
-        placement, normed, (((0,), (0,)), ((), ())), preferred_element_type=jnp.float32
-    ).astype(jnp.bfloat16)
-    outgoing = outgoing.reshape(model_parts, MOST, features)
-    arrived = lax.all_to_all(outgoing, "mp", split_axis=0, concat_axis=0, tiled=True)
-    own = arrived.reshape(model_parts * MOST, features)
-
-    weights = load(gate_weight[0], up_weight[0], down_weight[0])
-
-    def shift(value, by):
-        return lax.ppermute(
-            value, "expert", [(i, (i + by) % unit_parts) for i in range(unit_parts)]
-        )
-
+
+    def chosen(slot_of):
+        return slot_of[:, 0][:, None] == slots[None, :], slot_of[:, 1][:, None] == slots[None, :]
+
+    def pack(pair, rows):
+        placement = (pair[0] | pair[1]).astype(jnp.bfloat16)
+        packed = lax.dot_general(
+            placement, rows, (((0,), (0,)), ((), ())), preferred_element_type=jnp.float32
+        ).astype(jnp.bfloat16)
+        return packed.reshape(model_parts, MOST, features)
+
+    def to_experts(packed):
+        packed = lax.all_to_all(packed, "mp", split_axis=0, concat_axis=0, tiled=True)
+        return packed.reshape(model_parts * MOST, features)
+
+    first, second = chosen(target)
+    far_normed = shift(normed, 2)
+    own = to_experts(pack((first, second), normed))
+    far_rows = to_experts(pack(chosen(far_target), far_normed))
+    stored = (gate_weight[0], up_weight[0], down_weight[0])
+    weights = load(*stored)
     before_rows = shift(own, 1)
     after_rows = shift(own, -1)
     (own_sum,) = ffn([own], *weights)
-    far_rows = shift(lax.optimization_barrier((own, own_sum))[0], 2)
+    before_rows, own_sum = lax.optimization_barrier((before_rows, own_sum))
     before_sum, after_sum = ffn([before_rows, after_rows], *weights)
     back_after = shift(before_sum, -1)
     back_before = shift(after_sum, 1)
     far_rows = lax.optimization_barrier((far_rows, before_sum))[0]
-    (far_sum,) = ffn([far_rows], *weights)
+    (far_sum,) = stream_ffn([far_rows], *stored)
     back_far = shift(far_sum, 2)
     near = own_sum.astype(jnp.float32)
     near = near + back_after.astype(jnp.float32) + back_before.astype(jnp.float32)

time: 147 us -> 152 us (1.034); the launches traced: 144 us -> 151 us
  blocking collectives: 21.7 us -> 0 us
  starting transfers between devices: 33 us -> 46.7 us
  Pallas kernels: 13.4 us -> 19.8 us
  waiting for transfers between devices: 68.5 us -> 74 us
  matrix products: 3.49 us -> 5.6 us
    all_to_all x1 -> x0, blocking collectives: 21.7 us -> none  [body(): lax.all_to_all(outgoing, 'mp', split_axis=0, concat_axis=0, tiled=True)]
    all_to_all x0 -> x2, waiting for transfers between devices: none -> 14.4 us  [to_experts(): lax.all_to_all(packed, 'mp', split_axis=0, concat_axis=0, tiled=True)]
    all_to_all x0 -> x2, starting transfers between devices: none -> 7.07 us  [to_experts(): lax.all_to_all(packed, 'mp', split_axis=0, concat_axis=0, tiled=True)]
    all_to_all x1, waiting for transfers between devices: 30.8 us -> 23.8 us  [body(): parts = lax.all_to_all(parts, 'mp', split_axis=0, concat_axis=0, tiled=True)]
    pallas_call x0 -> x1, Pallas kernels: none -> 6.31 us  [stream_ffn(): pl.pallas_call(functools.partial(stream_ffn_kernel, count), out_shape=[ja...]
    ppermute x6 -> x7, starting transfers between devices: 22.1 us -> 27.4 us  [shift(): lax.ppermute(value, 'expert', [(i, (i + by) % unit_parts) for i in range(...]
    ppermute x6 -> x7, waiting for transfers between devices: 23.8 us -> 21.1 us  [shift(): lax.ppermute(value, 'expert', [(i, (i + by) % unit_parts) for i in range(...]
    dot_general x1 -> x2, matrix products: 0.43 us -> 2.53 us  [pack(): lax.dot_general(placement, rows, (((0,), (0,)), ((), ())), preferred_elem...]
  transfers between devices with their start and end apart: 8 -> 11, of which waited for: 5 -> 6; matrix products, arithmetic and copies ran while one was open for 1% -> 2% of each run, Pallas kernels for 9% -> 13%
where the time goes in v6:
time: 152 us; the launch traced here: 151 us
  waiting for transfers between devices  74 us (49%)
  starting transfers between devices  46.7 us (31%)
  Pallas kernels  19.8 us (13%)
  matrix products  5.6 us (4%)
  other arithmetic  2.95 us (2%)
  local copies, waits for them, and re-layouts  1.96 us (1%)
    ppermute x7, starting transfers between devices, shift(): lax.ppermute(value, 'expert', [(i, (i + by) % unit_parts) for i in range(...  27.4 us
    all_to_all x1, waiting for transfers between devices, body(): parts = lax.all_to_all(parts, 'mp', split_axis=0, concat_axis=0, tiled=True)  23.8 us
    ppermute x7, waiting for transfers between devices, shift(): lax.ppermute(value, 'expert', [(i, (i + by) % unit_parts) for i in range(...  21.1 us
    all_to_all x1, waiting for transfers between devices, body(): lax.all_to_all(outputs, 'mp', split_axis=0, concat_axis=0, tiled=True)  14.8 us
    all_to_all x2, waiting for transfers between devices, to_experts(): lax.all_to_all(packed, 'mp', split_axis=0, concat_axis=0, tiled=True)  14.4 us
    pallas_call x2, Pallas kernels, ffn(): pl.pallas_call(functools.partial(ffn_kernel, count), out_shape=[jax.Shape...  8.37 us
    all_to_all x1, starting transfers between devices, body(): parts = lax.all_to_all(parts, 'mp', split_axis=0, concat_axis=0, tiled=True)  7.23 us
    all_to_all x2, starting transfers between devices, to_experts(): lax.all_to_all(packed, 'mp', split_axis=0, concat_axis=0, tiled=True)  7.07 us
  transfers between devices with their start and end apart: 11, of which 6 were waited for; matrix products, arithmetic and copies ran while one was open for 2% of the time, Pallas kernels for 13%

profile of v6, /device:TPU:448, one launch (start us, length us, event | category | flops | bytes accessed | tf_op | source)
XLA Modules:
  0.0 151.3 jit_solution(4434517695657723228)
XLA Ops:
  0.0 0.0 copy-start
  0.0 1.5 %copy.19 = bf16[1024,288]{1,0:T(8,128)(2,1)S(1)} copy(bf16[1024,288]{0,1:T(8,128)(2,1)} %param.9) | data formatting | bytes 1179648 | tf_op args[0]
  1.6 0.0 copy-done
  1.6 1.8 %convolution_convert_fusion = f16[256,2304]{1,0:T(8,128)(2,1)} fusion(bf16[256,288]{1,0:T(8,128)(2,1)S(1)} %bitcast.44, bf16[288,2304]{1,0:T(8,128)(2,1)S(1)} %copy-done), kind=kOutput, calls=%fused_computation | convolution fusion | flops 340328448 | bytes 2654208 | tf_op jit(solution)/shard_map/dot_general | solution.py:200
  3.4 0.0 copy-start.3
  3.4 7.2 %all-to-all-start = ((f16[8,32,2304]{2,1,0:T(8,128)(2,1)}), f16[8,32,2304]{2,1,0:T(8,128)(2,1)S(1)}, u32[]{:S(2)}, u32[]{:S(2)}) async-start(f16[8,32,2304]{2,1,0:T(8,128)(2,1)} %bitcast.42), calls=%async_computation | async-start | bytes 2359296 | tf_op jit(solution)/shard_map/all_to_all | solution.py:202
  10.6 0.0 copy-done.3
  10.6 0.0 copy-start.1
  10.6 0.1 copy.17
  10.7 0.1 eq.75
  10.8 0.1 fusion.2
  10.9 0.1 reduce_window_sum.11
  11.0 0.2 select_reduce_fusion
  11.2 0.1 reduce_sum.30
  11.3 0.1 copy.18
  11.4 4.9 %collective-permute-start = (s32[32,2]{0,1:T(2,128)S(1)}, s32[32,2]{0,1:T(2,128)S(1)}, u32[]{:S(2)}, u32[]{:S(2)}) collective-permute-start(s32[32,2]{0,1:T(2,128)S(1)} %multiply_add_fusion), channel_id=1, source_target_pairs={{0,2},{1,3},{2,0},{3,1},{4,6},{5,7},{6,4},{7,5},{8,10},{9,11},{10,... | collective-permute-start | bytes 776 | tf_op jit(solution)/shard_map/ppermute | solution.py:184
  16.4 0.0 copy-start.2
  16.4 2.0 %collective-permute-done = s32[32,2]{0,1:T(2,128)S(1)} collective-permute-done((s32[32,2]{0,1:T(2,128)S(1)}, s32[32,2]{0,1:T(2,128)S(1)}, u32[]{:S(2)}, u32[]{:S(2)}) %collective-permute-start) | collective-permute-done | bytes 288 | tf_op jit(solution)/shard_map/ppermute | solution.py:184
  18.4 23.8 %all-to-all-done = f16[8,32,2304]{2,1,0:T(8,128)(2,1)S(1)} async-done(((f16[8,32,2304]{2,1,0:T(8,128)(2,1)}), f16[8,32,2304]{2,1,0:T(8,128)(2,1)S(1)}, u32[]{:S(2)}, u32[]{:S(2)}) %all-to-all-start) | async-done | bytes 1179680 | tf_op jit(solution)/shard_map/all_to_all | solution.py:202
  42.2 0.2 convert_reduce_fusion
  42.4 0.0 copy-done.1
  42.4 0.1 multiply_reduce_fusion
  42.5 0.0 copy-done.2
  42.6 0.1 multiply_convert_fusion
  42.7 1.3 convolution_convert_fusion.2
  43.9 3.5 %all-to-all-start.1 = ((bf16[8,16,2304]{2,1,0:T(8,128)(2,1)}), bf16[8,16,2304]{2,1,0:T(8,128)(2,1)S(1)}, u32[]{:S(2)}, u32[]{:S(2)}) async-start(bf16[8,16,2304]{2,1,0:T(8,128)(2,1)} %bitcast.6), calls=%async_computation.1 | async-start | bytes 1179648 | tf_op jit(solution)/shard_map/all_to_all | solution.py:219
  47.5 4.9 %collective-permute-start.5 = (bf16[32,2304]{1,0:T(8,128)(2,1)S(1)}, bf16[32,2304]{1,0:T(8,128)(2,1)S(1)}, u32[]{:S(2)}, u32[]{:S(2)}) collective-permute-start(bf16[32,2304]{1,0:T(8,128)(2,1)S(1)} %multiply_convert_fusion), channel_id=1, source_target_pairs={{0,2},{1,3},{2,0},{3,1},{4,6},{5,7},{6,4},{7,5},{8,10},{9,11},{10,... | collective-permute-start | bytes 442376 | tf_op jit(solution)/shard_map/ppermute | solution.py:184
  52.4 14.4 %all-to-all-done.1 = bf16[8,16,2304]{2,1,0:T(8,128)(2,1)S(1)} async-done(((bf16[8,16,2304]{2,1,0:T(8,128)(2,1)}), bf16[8,16,2304]{2,1,0:T(8,128)(2,1)S(1)}, u32[]{:S(2)}, u32[]{:S(2)}) %all-to-all-start.1) | async-done | bytes 589856 | tf_op jit(solution)/shard_map/all_to_all | solution.py:219
  66.8 3.4 %collective-permute-start.1 = (bf16[128,2304]{1,0:T(8,128)(2,1)S(1)}, bf16[128,2304]{1,0:T(8,128)(2,1)}, u32[]{:S(2)}, u32[]{:S(2)}) collective-permute-start(bf16[128,2304]{1,0:T(8,128)(2,1)S(1)} %bitcast.30), channel_id=1, source_target_pairs={{0,1},{1,2},{2,3},{3,0},{4,5},{5,6},{6,7},{7,4},{8,9},{9,10},{10,1... | collective-permute-start | bytes 1769480 | tf_op jit(solution)/shard_map/ppermute | solution.py:184
  70.2 3.7 %collective-permute-start.2 = (bf16[128,2304]{1,0:T(8,128)(2,1)S(1)}, bf16[128,2304]{1,0:T(8,128)(2,1)}, u32[]{:S(2)}, u32[]{:S(2)}) collective-permute-start(bf16[128,2304]{1,0:T(8,128)(2,1)S(1)} %bitcast.31), channel_id=1, source_target_pairs={{0,3},{1,0},{2,1},{3,2},{4,7},{5,4},{6,5},{7,6},{8,11},{9,8},{10,9... | collective-permute-start | bytes 1769480 | tf_op jit(solution)/shard_map/ppermute | solution.py:184
  73.8 0.0 collective-permute-done.5
  73.8 1.3 convolution_convert_fusion.1
  75.1 3.5 %all-to-all-start.2 = ((bf16[8,16,2304]{2,1,0:T(8,128)(2,1)}), bf16[8,16,2304]{2,1,0:T(8,128)(2,1)S(1)}, u32[]{:S(2)}, u32[]{:S(2)}) async-start(bf16[8,16,2304]{2,1,0:T(8,128)(2,1)} %bitcast.13), calls=%async_computation.2 | async-start | bytes 1179648 | tf_op jit(solution)/shard_map/all_to_all | solution.py:219
  78.7 5.1 %shard_map.91 = (bf16[2304,1024]{1,0:T(8,128)(2,1)S(1)}, bf16[2304,1024]{1,0:T(8,128)(2,1)S(1)}, bf16[1024,2304]{1,0:T(8,128)(2,1)S(1)}) custom-call(bf16[2304,1024]{1,0:T(8,128)(2,1)} %bitcast.34, bf16[2304,1024]{1,0:T(8,128)(2,1)} %bitcast.36, bf16[1024,2304]{1,0:T(8,128)(2,1)} %bitcast.38), custom_call_target="tpu_custom_call" | custom-call | bytes 28311552 | tf_op jit(solution)/shard_map/pallas_call | solution.py:34
  83.8 2.1 %shard_map.92 = bf16[128,2304]{1,0:T(8,128)(2,1)S(1)} custom-call(bf16[128,2304]{1,0:T(8,128)(2,1)S(1)} %bitcast.32, bf16[2304,1024]{1,0:T(8,128)(2,1)S(1)} %get-tuple-element.16.refs_1_.refs_2_, bf16[2304,1024]{1,0:T(8,128)(2,1)S(1)} %get-tuple-element.17.refs_2_.refs_3_, bf16[1024,2304]{1,0:T(8,128)(2,1)S(1)} %get-tuple-element.18.refs_3_.refs_4_), custom_call_target="tpu_custom_call" | custom-call | flops 1811939328 | bytes 15335424 | tf_op jit(solution)/shard_map/pallas_call | solution.py:77
  86.0 0.0 collective-permute-done.1.refs_0_
  86.0 1.2 collective-permute-done.2.refs_1_
  87.1 6.2 %shard_map.93 = (bf16[128,2304]{1,0:T(8,128)(2,1)}, bf16[128,2304]{1,0:T(8,128)(2,1)}) custom-call(bf16[128,2304]{1,0:T(8,128)(2,1)} %collective-permute-done.1.refs_0_, bf16[128,2304]{1,0:T(8,128)(2,1)} %collective-permute-done.2.refs_1_, bf16[2304,1024]{1,0:T(8,128)(2,1)S(1)} %get-tuple-element.16.refs_1_.refs_2_, ...), custom_call_target="tpu_custom_call" | custom-call | flops 3623878656 | bytes 16515072 | tf_op jit(solution)/shard_map/pallas_call | solution.py:77
  93.4 4.9 %collective-permute-start.3 = (bf16[128,2304]{1,0:T(8,128)(2,1)}, bf16[128,2304]{1,0:T(8,128)(2,1)S(1)}, u32[]{:S(2)}, u32[]{:S(2)}) collective-permute-start(bf16[128,2304]{1,0:T(8,128)(2,1)} %get-tuple-element.21), channel_id=1, source_target_pairs={{0,3},{1,0},{2,1},{3,2},{4,7},{5,4},{6,5},{7,6},{8,11},{9,8},{10,9... | collective-permute-start | bytes 1769480 | tf_op jit(solution)/shard_map/ppermute | solution.py:184
  98.2 1.9 %collective-permute-start.4 = (bf16[128,2304]{1,0:T(8,128)(2,1)}, bf16[128,2304]{1,0:T(8,128)(2,1)}, u32[]{:S(2)}, u32[]{:S(2)}) collective-permute-start(bf16[128,2304]{1,0:T(8,128)(2,1)} %get-tuple-element.22), channel_id=1, source_target_pairs={{0,1},{1,2},{2,3},{3,0},{4,5},{5,6},{6,7},{7,4},{8,9},{9,10},{10,1... | collective-permute-start | bytes 1769480 | tf_op jit(solution)/shard_map/ppermute | solution.py:184
  100.2 0.0 all-to-all-done.2
  100.2 6.3 %shard_map.94 = bf16[128,2304]{1,0:T(8,128)(2,1)S(1)} custom-call(bf16[128,2304]{1,0:T(8,128)(2,1)S(1)} %bitcast.33, bf16[2304,1024]{1,0:T(8,128)(2,1)} %bitcast.35, bf16[2304,1024]{1,0:T(8,128)(2,1)} %bitcast.37, bf16[1024,2304]{1,0:T(8,128)(2,1)} %bitcast.39), custom_call_target="tpu_custom_call" | custom-call | flops 1811939328 | bytes 15335424 | tf_op jit(solution)/shard_map/pallas_call | solution.py:144
  106.5 3.7 %collective-permute-start.6 = (bf16[128,2304]{1,0:T(8,128)(2,1)S(1)}, bf16[128,2304]{1,0:T(8,128)(2,1)S(1)}, u32[]{:S(2)}, u32[]{:S(2)}) collective-permute-start(bf16[128,2304]{1,0:T(8,128)(2,1)S(1)} %shard_map.94), channel_id=1, source_target_pairs={{0,2},{1,3},{2,0},{3,1},{4,6},{5,7},{6,4},{7,5},{8,10},{9,11},{10,... | collective-permute-start | bytes 1769480 | tf_op jit(solution)/shard_map/ppermute | solution.py:184
  110.2 0.0 collective-permute-done.3
  110.2 17.9 %collective-permute-done.4 = bf16[128,2304]{1,0:T(8,128)(2,1)} collective-permute-done((bf16[128,2304]{1,0:T(8,128)(2,1)}, bf16[128,2304]{1,0:T(8,128)(2,1)}, u32[]{:S(2)}, u32[]{:S(2)}) %collective-permute-start.4) | collective-permute-done | bytes 589856 | tf_op jit(solution)/shard_map/ppermute | solution.py:184
  128.1 1.3 convert_add_fusion
  129.4 0.0 collective-permute-done.6
  129.4 0.9 add_convert_fusion
  130.3 0.0 copy-start.4
  130.3 5.0 %all-to-all-start.3 = ((bf16[8,16,2304]{2,1,0:T(8,128)(2,1)}), bf16[8,16,2304]{2,1,0:T(8,128)(2,1)S(1)}, u32[]{:S(2)}, u32[]{:S(2)}) async-start(bf16[8,16,2304]{2,1,0:T(8,128)(2,1)} %bitcast.15), calls=%async_computation.3 | async-start | bytes 1179648 | tf_op jit(solution)/shard_map/all_to_all | solution.py:242
  135.3 0.0 copy-done.4
  135.3 14.8 %all-to-all-done.3 = bf16[8,16,2304]{2,1,0:T(8,128)(2,1)S(1)} async-done(((bf16[8,16,2304]{2,1,0:T(8,128)(2,1)}), bf16[8,16,2304]{2,1,0:T(8,128)(2,1)S(1)}, u32[]{:S(2)}, u32[]{:S(2)}) %all-to-all-start.3) | async-done | bytes 589856 | tf_op jit(solution)/shard_map/all_to_all | solution.py:242
  150.1 0.3 convolution_multiply_fusion
  150.4 1.0 fusion.1
  (6 shorter events, 0.1 us)
Async XLA Ops:
  0.0 1.6 %copy-start = (bf16[288,2304]{1,0:T(8,128)(2,1)S(1)}, bf16[288,2304]{1,0:T(8,128)(2,1)}, u32[]{:S(2)}) copy-start(bf16[288,2304]{1,0:T(8,128)(2,1)} %param.11) | copy-start | bytes 3981316
  3.4 7.2 %copy-start.3 = (s32[32,2]{0,1:T(2,128)S(1)}, s32[32,2]{0,1:T(2,128)}, u32[]{:S(2)}) copy-start(s32[32,2]{0,1:T(2,128)} %param.16) | copy-start | bytes 772
  3.4 38.8 %all-to-all-start = ((f16[8,32,2304]{2,1,0:T(8,128)(2,1)}), f16[8,32,2304]{2,1,0:T(8,128)(2,1)S(1)}, u32[]{:S(2)}, u32[]{:S(2)}) async-start(f16[8,32,2304]{2,1,0:T(8,128)(2,1)} %bitcast.42), calls=%async_computation | async-start | bytes 2359296 | tf_op jit(solution)/shard_map/all_to_all | solution.py:202
  10.6 31.7 %copy-start.1 = (f32[32,2304]{1,0:T(8,128)S(1)}, f32[32,2304]{1,0:T(8,128)}, u32[]{:S(2)}) copy-start(f32[32,2304]{1,0:T(8,128)} %param.10) | copy-start | bytes 884740
  11.4 7.0 %collective-permute-start = (s32[32,2]{0,1:T(2,128)S(1)}, s32[32,2]{0,1:T(2,128)S(1)}, u32[]{:S(2)}, u32[]{:S(2)}) collective-permute-start(s32[32,2]{0,1:T(2,128)S(1)} %multiply_add_fusion), channel_id=1, source_target_pairs={{0,2},{1,3},{2,0},{3,1},{4,6},{5,7},{6,4},{7,5},{8,10},{9,11},{10,... | collective-permute-start | bytes 776 | tf_op jit(solution)/shard_map/ppermute | solution.py:184
  16.4 26.2 %copy-start.2 = (f32[2304]{0:T(1024)S(1)}, f32[2304]{0:T(1024)}, u32[]{:S(2)}) copy-start(f32[2304]{0:T(1024)} %param.12) | copy-start | bytes 27652
  43.9 22.8 %all-to-all-start.1 = ((bf16[8,16,2304]{2,1,0:T(8,128)(2,1)}), bf16[8,16,2304]{2,1,0:T(8,128)(2,1)S(1)}, u32[]{:S(2)}, u32[]{:S(2)}) async-start(bf16[8,16,2304]{2,1,0:T(8,128)(2,1)} %bitcast.6), calls=%async_computation.1 | async-start | bytes 1179648 | tf_op jit(solution)/shard_map/all_to_all | solution.py:219
  47.5 26.4 %collective-permute-start.5 = (bf16[32,2304]{1,0:T(8,128)(2,1)S(1)}, bf16[32,2304]{1,0:T(8,128)(2,1)S(1)}, u32[]{:S(2)}, u32[]{:S(2)}) collective-permute-start(bf16[32,2304]{1,0:T(8,128)(2,1)S(1)} %multiply_convert_fusion), channel_id=1, source_target_pairs={{0,2},{1,3},{2,0},{3,1},{4,6},{5,7},{6,4},{7,5},{8,10},{9,11},{10,... | collective-permute-start | bytes 442376 | tf_op jit(solution)/shard_map/ppermute | solution.py:184
  66.8 19.2 %collective-permute-start.1 = (bf16[128,2304]{1,0:T(8,128)(2,1)S(1)}, bf16[128,2304]{1,0:T(8,128)(2,1)}, u32[]{:S(2)}, u32[]{:S(2)}) collective-permute-start(bf16[128,2304]{1,0:T(8,128)(2,1)S(1)} %bitcast.30), channel_id=1, source_target_pairs={{0,1},{1,2},{2,3},{3,0},{4,5},{5,6},{6,7},{7,4},{8,9},{9,10},{10,1... | collective-permute-start | bytes 1769480 | tf_op jit(solution)/shard_map/ppermute | solution.py:184
  70.2 17.0 %collective-permute-start.2 = (bf16[128,2304]{1,0:T(8,128)(2,1)S(1)}, bf16[128,2304]{1,0:T(8,128)(2,1)}, u32[]{:S(2)}, u32[]{:S(2)}) collective-permute-start(bf16[128,2304]{1,0:T(8,128)(2,1)S(1)} %bitcast.31), channel_id=1, source_target_pairs={{0,3},{1,0},{2,1},{3,2},{4,7},{5,4},{6,5},{7,6},{8,11},{9,8},{10,9... | collective-permute-start | bytes 1769480 | tf_op jit(solution)/shard_map/ppermute | solution.py:184
  75.1 25.0 %all-to-all-start.2 = ((bf16[8,16,2304]{2,1,0:T(8,128)(2,1)}), bf16[8,16,2304]{2,1,0:T(8,128)(2,1)S(1)}, u32[]{:S(2)}, u32[]{:S(2)}) async-start(bf16[8,16,2304]{2,1,0:T(8,128)(2,1)} %bitcast.13), calls=%async_computation.2 | async-start | bytes 1179648 | tf_op jit(solution)/shard_map/all_to_all | solution.py:219
  93.4 16.8 %collective-permute-start.3 = (bf16[128,2304]{1,0:T(8,128)(2,1)}, bf16[128,2304]{1,0:T(8,128)(2,1)S(1)}, u32[]{:S(2)}, u32[]{:S(2)}) collective-permute-start(bf16[128,2304]{1,0:T(8,128)(2,1)} %get-tuple-element.21), channel_id=1, source_target_pairs={{0,3},{1,0},{2,1},{3,2},{4,7},{5,4},{6,5},{7,6},{8,11},{9,8},{10,9... | collective-permute-start | bytes 1769480 | tf_op jit(solution)/shard_map/ppermute | solution.py:184
  98.2 29.9 %collective-permute-start.4 = (bf16[128,2304]{1,0:T(8,128)(2,1)}, bf16[128,2304]{1,0:T(8,128)(2,1)}, u32[]{:S(2)}, u32[]{:S(2)}) collective-permute-start(bf16[128,2304]{1,0:T(8,128)(2,1)} %get-tuple-element.22), channel_id=1, source_target_pairs={{0,1},{1,2},{2,3},{3,0},{4,5},{5,6},{6,7},{7,4},{8,9},{9,10},{10,1... | collective-permute-start | bytes 1769480 | tf_op jit(solution)/shard_map/ppermute | solution.py:184
  106.5 22.9 %collective-permute-start.6 = (bf16[128,2304]{1,0:T(8,128)(2,1)S(1)}, bf16[128,2304]{1,0:T(8,128)(2,1)S(1)}, u32[]{:S(2)}, u32[]{:S(2)}) collective-permute-start(bf16[128,2304]{1,0:T(8,128)(2,1)S(1)} %shard_map.94), channel_id=1, source_target_pairs={{0,2},{1,3},{2,0},{3,1},{4,6},{5,7},{6,4},{7,5},{8,10},{9,11},{10,... | collective-permute-start | bytes 1769480 | tf_op jit(solution)/shard_map/ppermute | solution.py:184
  130.3 5.0 %copy-start.4 = (f32[32,2]{0,1:T(2,128)S(1)}, f32[32,2]{0,1:T(2,128)}, u32[]{:S(2)}) copy-start(f32[32,2]{0,1:T(2,128)} %param.17) | copy-start | bytes 772
  130.3 19.8 %all-to-all-start.3 = ((bf16[8,16,2304]{2,1,0:T(8,128)(2,1)}), bf16[8,16,2304]{2,1,0:T(8,128)(2,1)S(1)}, u32[]{:S(2)}, u32[]{:S(2)}) async-start(bf16[8,16,2304]{2,1,0:T(8,128)(2,1)} %bitcast.15), calls=%async_computation.3 | async-start | bytes 1179648 | tf_op jit(solution)/shard_map/all_to_all | solution.py:242

commit v7 on v5

--- a/solution.py
+++ b/solution.py
@@ -104,6 +104,21 @@
     unit_parts = lax.axis_size("expert")
     row_count = residual.shape[0]
     features = residual.shape[1]
+    def shift(value, by):
+        return lax.ppermute(
+            value, "expert", [(i, (i + by) % unit_parts) for i in range(unit_parts)]
+        )
+
+    expert_ids = routes.reshape(-1)
+    onehot = (expert_ids[:, None] == jnp.arange(EXPERTS, dtype=jnp.int32)[None, :]).astype(
+        jnp.int32
+    )
+    before = jnp.cumsum(onehot, axis=0) - onehot
+    position = jnp.sum(before * onehot, axis=1)
+    target = (expert_ids * MOST + position).reshape(row_count, 2)
+    far_routing = jnp.concatenate([target.astype(jnp.float32), route_weights], axis=1)
+    far_routing = shift(far_routing, 2)
+    residual, far_routing = lax.optimization_barrier((residual, far_routing))
     blocks = attn_out.reshape(model_parts, unit_parts, row_count, attn_out.shape[1])
     picked = lax.dynamic_index_in_dim(blocks, lax.axis_index("expert"), axis=1, keepdims=False)
     picked = picked.reshape(model_parts * row_count, attn_out.shape[1])
@@ -113,16 +128,17 @@
     hidden_state = residual + jnp.sum(parts, axis=0, dtype=jnp.float32)
     inverse_rms = lax.rsqrt(jnp.mean(hidden_state * hidden_state, axis=1, keepdims=True) + EPSILON)
     normed = (hidden_state * inverse_rms * norm_gain).astype(jnp.bfloat16)
-    expert_ids = routes.reshape(-1)
-    onehot = (expert_ids[:, None] == jnp.arange(EXPERTS, dtype=jnp.int32)[None, :]).astype(
-        jnp.int32
-    )
-    before = jnp.cumsum(onehot, axis=0) - onehot
-    position = jnp.sum(before * onehot, axis=1)
-    target = (expert_ids * MOST + position).reshape(row_count, 2)
     slots = jnp.arange(EXPERTS * MOST, dtype=jnp.int32)
-    first = target[:, 0][:, None] == slots[None, :]
-    second = target[:, 1][:, None] == slots[None, :]
+
+    def chosen(slot_of):
+        return slot_of[:, 0][:, None] == slots[None, :], slot_of[:, 1][:, None] == slots[None, :]
+
+    def weighted(pair, weight_of, sums):
+        one = jnp.dot(pair[0].astype(jnp.bfloat16), sums, preferred_element_type=jnp.float32)
+        two = jnp.dot(pair[1].astype(jnp.bfloat16), sums, preferred_element_type=jnp.float32)
+        return weight_of[:, 0:1] * one + weight_of[:, 1:2] * two
+
+    first, second = chosen(target)
     placement = (first | second).astype(jnp.bfloat16)
     outgoing = lax.dot_general(
         placement, normed, (((0,), (0,)), ((), ())), preferred_element_type=jnp.float32
@@ -133,11 +149,6 @@
 
     weights = load(gate_weight[0], up_weight[0], down_weight[0])
 
-    def shift(value, by):
-        return lax.ppermute(
-            value, "expert", [(i, (i + by) % unit_parts) for i in range(unit_parts)]
-        )
-
     before_rows = shift(own, 1)
     after_rows = shift(own, -1)
     (own_sum,) = ffn([own], *weights)
@@ -147,16 +158,22 @@
     back_before = shift(after_sum, 1)
     far_rows = lax.optimization_barrier((far_rows, before_sum))[0]
     (far_sum,) = ffn([far_rows], *weights)
-    back_far = shift(far_sum, 2)
+    far_sums = lax.all_to_all(
+        far_sum.reshape(model_parts, MOST, features), "mp", split_axis=0, concat_axis=0, tiled=True
+    )
     near = own_sum.astype(jnp.float32)
     near = near + back_after.astype(jnp.float32) + back_before.astype(jnp.float32)
-    outputs = lax.optimization_barrier(near) + back_far.astype(jnp.float32)
-    outputs = outputs.astype(jnp.bfloat16).reshape(model_parts, MOST, features)
-    outputs = lax.all_to_all(outputs, "mp", split_axis=0, concat_axis=0, tiled=True)
-    expert_out = outputs.reshape(EXPERTS * MOST, features)
-    one = jnp.dot(first.astype(jnp.bfloat16), expert_out, preferred_element_type=jnp.float32)
-    two = jnp.dot(second.astype(jnp.bfloat16), expert_out, preferred_element_type=jnp.float32)
-    return hidden_state + route_weights[:, 0:1] * one + route_weights[:, 1:2] * two
+    near = near.astype(jnp.bfloat16).reshape(model_parts, MOST, features)
+    near, far_sums = lax.optimization_barrier((near, far_sums))
+    near = lax.all_to_all(near, "mp", split_axis=0, concat_axis=0, tiled=True)
+    far_part = weighted(
+        chosen(far_routing[:, 0:2].astype(jnp.int32)),
+        far_routing[:, 2:4],
+        far_sums.reshape(EXPERTS * MOST, features),
+    )
+    far_part = shift(far_part, 2)
+    near_part = weighted((first, second), route_weights, near.reshape(EXPERTS * MOST, features))
+    return hidden_state + near_part + far_part
 
 
 def solution(mesh):

time: 147 us -> 151 us (1.027); the launches traced: 144 us -> 151 us
  starting transfers between devices: 33 us -> 41.7 us
  waiting for transfers between devices: 68.5 us -> 61.8 us
  matrix products: 3.49 us -> 6.14 us
    all_to_all x1, waiting for transfers between devices: 30.8 us -> 23.8 us  [body(): parts = lax.all_to_all(parts, 'mp', split_axis=0, concat_axis=0, tiled=True)]
    all_to_all x1 -> x2, waiting for transfers between devices: 13.9 us -> 20.1 us  [the longest x1 11.1 us: body(): lax.all_to_all(far_sum.reshape(model_parts, MOST, features), 'mp', split_...]
    ppermute x6 -> x7, waiting for transfers between devices: 23.8 us -> 17.9 us  [shift(): lax.ppermute(value, 'expert', [(i, (i + by) % unit_parts) for i in range(...]
    all_to_all x1 -> x2, starting transfers between devices: 3.67 us -> 8.54 us  [the longest x1 4.36 us: body(): near = lax.all_to_all(near, 'mp', split_axis=0, concat_axis=0, tiled=True)]
    ppermute x6 -> x7, starting transfers between devices: 22.1 us -> 25.9 us  [shift(): lax.ppermute(value, 'expert', [(i, (i + by) % unit_parts) for i in range(...]
    dot_general x2 -> x4, matrix products: 1.25 us -> 3.9 us  [the longest x2 2.32 us: weighted(): jnp.dot(pair[0].astype(jnp.bfloat16), sums, preferred_element_type=jnp.fl...]
  transfers between devices with their start and end apart: 8 -> 10, of which waited for: 5 -> 6; matrix products, arithmetic and copies ran while one was open for 1% -> 4% of each run, Pallas kernels for 9% -> 9%
where the time goes in v7:
time: 151 us
  waiting for transfers between devices  61.8 us (41%)
  starting transfers between devices  41.7 us (28%)
  blocking collectives  21.7 us (14%)
  Pallas kernels  14.2 us (9%)
  matrix products  6.14 us (4%)
  other arithmetic  2.97 us (2%)
  local copies, waits for them, and re-layouts  1.97 us (1%)
    ppermute x7, starting transfers between devices, shift(): lax.ppermute(value, 'expert', [(i, (i + by) % unit_parts) for i in range(...  25.9 us
    all_to_all x1, waiting for transfers between devices, body(): parts = lax.all_to_all(parts, 'mp', split_axis=0, concat_axis=0, tiled=True)  23.8 us
    all_to_all x1, blocking collectives, body(): lax.all_to_all(outgoing, 'mp', split_axis=0, concat_axis=0, tiled=True)  21.7 us
    ppermute x7, waiting for transfers between devices, shift(): lax.ppermute(value, 'expert', [(i, (i + by) % unit_parts) for i in range(...  17.9 us
    all_to_all x1, waiting for transfers between devices, body(): lax.all_to_all(far_sum.reshape(model_parts, MOST, features), 'mp', split_...  11.1 us
    pallas_call x3, Pallas kernels, ffn(): pl.pallas_call(functools.partial(ffn_kernel, count), out_shape=[jax.Shape...  9.07 us
    all_to_all x1, waiting for transfers between devices, body(): near = lax.all_to_all(near, 'mp', split_axis=0, concat_axis=0, tiled=True)  9.04 us
    all_to_all x1, starting transfers between devices, body(): parts = lax.all_to_all(parts, 'mp', split_axis=0, concat_axis=0, tiled=True)  7.23 us
  transfers between devices with their start and end apart: 10, of which 6 were waited for; matrix products, arithmetic and copies ran while one was open for 4% of the time, Pallas kernels for 9%

profile of v7, /device:TPU:448, one launch (start us, length us, event | category | flops | bytes accessed | tf_op | source)
XLA Modules:
  0.0 150.8 jit_solution(8354889568703580504)
XLA Ops:
  0.0 0.0 copy-start
  0.0 1.5 %copy.26 = bf16[1024,288]{1,0:T(8,128)(2,1)S(1)} copy(bf16[1024,288]{0,1:T(8,128)(2,1)} %param.9) | data formatting | bytes 1179648 | tf_op args[0]
  1.6 0.0 copy-done
  1.6 1.8 %convolution_convert_fusion = f16[256,2304]{1,0:T(8,128)(2,1)} fusion(bf16[256,288]{1,0:T(8,128)(2,1)S(1)} %bitcast.46, bf16[288,2304]{1,0:T(8,128)(2,1)S(1)} %copy-done), kind=kOutput, calls=%fused_computation | convolution fusion | flops 340328448 | bytes 2654208 | tf_op jit(solution)/shard_map/dot_general | solution.py:125
  3.4 0.0 copy-start.3
  3.4 0.0 copy-start.4
  3.4 7.2 %all-to-all-start = ((f16[8,32,2304]{2,1,0:T(8,128)(2,1)}), f16[8,32,2304]{2,1,0:T(8,128)(2,1)S(1)}, u32[]{:S(2)}, u32[]{:S(2)}) async-start(f16[8,32,2304]{2,1,0:T(8,128)(2,1)} %bitcast.43), calls=%async_computation | async-start | bytes 2359296 | tf_op jit(solution)/shard_map/all_to_all | solution.py:127
  10.6 0.0 copy-done.3
  10.6 0.0 copy-start.1
  10.7 0.0 copy-start.2
  10.7 0.1 copy.24
  10.8 0.1 eq.75
  10.9 0.1 fusion.6
  10.9 0.1 reduce_window_sum.11
  11.0 0.2 select_reduce_fusion
  11.2 0.1 reduce_sum.30
  11.3 0.1 copy.25
  11.4 0.0 copy-done.4
  11.4 4.9 %collective-permute-start = (f32[32,4]{0,1:T(4,128)S(1)}, f32[32,4]{0,1:T(4,128)S(1)}, u32[]{:S(2)}, u32[]{:S(2)}) collective-permute-start(f32[32,4]{0,1:T(4,128)S(1)} %pad_maximum_fusion), channel_id=1, source_target_pairs={{0,2},{1,3},{2,0},{3,1},{4,6},{5,7},{6,4},{7,5},{8,10},{9,11},{10,... | collective-permute-start | bytes 1544 | tf_op jit(solution)/shard_map/ppermute | solution.py:108
  16.4 2.0 %collective-permute-done = f32[32,4]{0,1:T(4,128)S(1)} collective-permute-done((f32[32,4]{0,1:T(4,128)S(1)}, f32[32,4]{0,1:T(4,128)S(1)}, u32[]{:S(2)}, u32[]{:S(2)}) %collective-permute-start) | collective-permute-done | bytes 544 | tf_op jit(solution)/shard_map/ppermute | solution.py:108
  18.4 23.8 %all-to-all-done = f16[8,32,2304]{2,1,0:T(8,128)(2,1)S(1)} async-done(((f16[8,32,2304]{2,1,0:T(8,128)(2,1)}), f16[8,32,2304]{2,1,0:T(8,128)(2,1)S(1)}, u32[]{:S(2)}, u32[]{:S(2)}) %all-to-all-start) | async-done | bytes 1179680 | tf_op jit(solution)/shard_map/all_to_all | solution.py:127
  42.2 0.2 convert_reduce_fusion
  42.4 0.0 copy-done.1
  42.4 0.1 multiply_reduce_fusion
  42.5 0.0 copy-done.2
  42.6 0.4 convolution_convert_fusion.1
  43.0 21.7 %all_to_all.20 = bf16[8,16,2304]{2,1,0:T(8,128)(2,1)S(1)} all-to-all(bf16[8,16,2304]{2,1,0:T(8,128)(2,1)S(1)} %bitcast.44), channel_id=1, replica_groups=mesh['dp'=16,'mp'=8,'expert'=4] {'mp'}, dimensions={0} | all-to-all | bytes 1179648 | tf_op jit(solution)/shard_map/all_to_all | solution.py:147
  64.7 3.4 %collective-permute-start.1 = (bf16[128,2304]{1,0:T(8,128)(2,1)S(1)}, bf16[128,2304]{1,0:T(8,128)(2,1)S(1)}, u32[]{:S(2)}, u32[]{:S(2)}) collective-permute-start(bf16[128,2304]{1,0:T(8,128)(2,1)S(1)} %bitcast.34), channel_id=1, source_target_pairs={{0,1},{1,2},{2,3},{3,0},{4,5},{5,6},{6,7},{7,4},{8,9},{9,10},{10,1... | collective-permute-start | bytes 1769480 | tf_op jit(solution)/shard_map/ppermute | solution.py:108
  68.1 3.7 %collective-permute-start.2 = (bf16[128,2304]{1,0:T(8,128)(2,1)S(1)}, bf16[128,2304]{1,0:T(8,128)(2,1)S(1)}, u32[]{:S(2)}, u32[]{:S(2)}) collective-permute-start(bf16[128,2304]{1,0:T(8,128)(2,1)S(1)} %bitcast.35), channel_id=1, source_target_pairs={{0,3},{1,0},{2,1},{3,2},{4,7},{5,4},{6,5},{7,6},{8,11},{9,8},{10,9... | collective-permute-start | bytes 1769480 | tf_op jit(solution)/shard_map/ppermute | solution.py:108
  71.8 5.1 %shard_map.91 = (bf16[2304,1024]{1,0:T(8,128)(2,1)S(1)}, bf16[2304,1024]{1,0:T(8,128)(2,1)S(1)}, bf16[1024,2304]{1,0:T(8,128)(2,1)S(1)}) custom-call(bf16[2304,1024]{1,0:T(8,128)(2,1)} %bitcast.40, bf16[2304,1024]{1,0:T(8,128)(2,1)} %bitcast.41, bf16[1024,2304]{1,0:T(8,128)(2,1)} %bitcast.42), custom_call_target="tpu_custom_call" | custom-call | bytes 28311552 | tf_op jit(solution)/shard_map/pallas_call | solution.py:34
  76.9 2.1 %shard_map.92 = bf16[128,2304]{1,0:T(8,128)(2,1)S(1)} custom-call(bf16[128,2304]{1,0:T(8,128)(2,1)S(1)} %bitcast.36, bf16[2304,1024]{1,0:T(8,128)(2,1)S(1)} %get-tuple-element.17.refs_1_.refs_2_, bf16[2304,1024]{1,0:T(8,128)(2,1)S(1)} %get-tuple-element.18.refs_2_.refs_3_, bf16[1024,2304]{1,0:T(8,128)(2,1)S(1)} %get-tuple-element.19.refs_3_.refs_4_), custom_call_target="tpu_custom_call" | custom-call | flops 1811939328 | bytes 15335424 | tf_op jit(solution)/shard_map/pallas_call | solution.py:77
  79.1 3.7 %collective-permute-start.5 = (bf16[128,2304]{1,0:T(8,128)(2,1)S(1)}, bf16[128,2304]{1,0:T(8,128)(2,1)S(1)}, u32[]{:S(2)}, u32[]{:S(2)}) collective-permute-start(bf16[128,2304]{1,0:T(8,128)(2,1)S(1)} %bitcast.37), channel_id=1, source_target_pairs={{0,2},{1,3},{2,0},{3,1},{4,6},{5,7},{6,4},{7,5},{8,10},{9,11},{10,... | collective-permute-start | bytes 1769480 | tf_op jit(solution)/shard_map/ppermute | solution.py:108
  82.8 0.0 collective-permute-done.1.refs_0_
  82.8 11.9 %collective-permute-done.2.refs_1_ = bf16[128,2304]{1,0:T(8,128)(2,1)S(1)} collective-permute-done((bf16[128,2304]{1,0:T(8,128)(2,1)S(1)}, bf16[128,2304]{1,0:T(8,128)(2,1)S(1)}, u32[]{:S(2)}, u32[]{:S(2)}) %collective-permute-start.2) | collective-permute-done | bytes 589856 | tf_op jit(solution)/shard_map/ppermute | solution.py:108
  94.7 4.0 %shard_map.93 = (bf16[128,2304]{1,0:T(8,128)(2,1)S(1)}, bf16[128,2304]{1,0:T(8,128)(2,1)S(1)}) custom-call(bf16[128,2304]{1,0:T(8,128)(2,1)S(1)} %collective-permute-done.1.refs_0_, bf16[128,2304]{1,0:T(8,128)(2,1)S(1)} %collective-permute-done.2.refs_1_, bf16[2304,1024]{1,0:T(8,128)(2,1)S(1)} %get-tuple-element.17.refs_1_.refs_2_, ...), custom_call_target="tpu_custom_call" | custom-call | flops 3623878656 | bytes 16515072 | tf_op jit(solution)/shard_map/pallas_call | solution.py:77
  98.7 6.0 %collective-permute-start.3 = (bf16[128,2304]{1,0:T(8,128)(2,1)S(1)}, bf16[128,2304]{1,0:T(8,128)(2,1)}, u32[]{:S(2)}, u32[]{:S(2)}) collective-permute-start(bf16[128,2304]{1,0:T(8,128)(2,1)S(1)} %get-tuple-element.20), channel_id=1, source_target_pairs={{0,3},{1,0},{2,1},{3,2},{4,7},{5,4},{6,5},{7,6},{8,11},{9,8},{10,9... | collective-permute-start | bytes 1769480 | tf_op jit(solution)/shard_map/ppermute | solution.py:108
  104.8 1.9 %collective-permute-start.4 = (bf16[128,2304]{1,0:T(8,128)(2,1)S(1)}, bf16[128,2304]{1,0:T(8,128)(2,1)}, u32[]{:S(2)}, u32[]{:S(2)}) collective-permute-start(bf16[128,2304]{1,0:T(8,128)(2,1)S(1)} %get-tuple-element.21), channel_id=1, source_target_pairs={{0,1},{1,2},{2,3},{3,0},{4,5},{5,6},{6,7},{7,4},{8,9},{9,10},{10,1... | collective-permute-start | bytes 1769480 | tf_op jit(solution)/shard_map/ppermute | solution.py:108
  106.7 0.0 collective-permute-done.5.refs_0_
  106.7 3.0 %shard_map.94 = bf16[128,2304]{1,0:T(8,128)(2,1)} custom-call(bf16[128,2304]{1,0:T(8,128)(2,1)S(1)} %collective-permute-done.5.refs_0_, bf16[2304,1024]{1,0:T(8,128)(2,1)S(1)} %get-tuple-element.17.refs_1_.refs_2_, bf16[2304,1024]{1,0:T(8,128)(2,1)S(1)} %get-tuple-element.18.refs_2_.refs_3_, bf16[1024,2304]{1,0:T(8,128)(2,1)S(1)} %get-tuple-element.19.refs_3_.refs_4_), custom_call_target="tpu_custom_call" | custom-call | flops 1811939328 | bytes 15335424 | tf_op jit(solution)/shard_map/pallas_call | solution.py:77
  109.7 4.2 %all-to-all-start.2 = ((bf16[8,16,2304]{2,1,0:T(8,128)(2,1)}), bf16[8,16,2304]{2,1,0:T(8,128)(2,1)}, u32[]{:S(2)}, u32[]{:S(2)}) async-start(bf16[8,16,2304]{2,1,0:T(8,128)(2,1)} %bitcast.12), calls=%async_computation.2 | async-start | bytes 1179648 | tf_op jit(solution)/shard_map/all_to_all | solution.py:161
  113.9 0.0 collective-permute-done.3
  113.9 4.0 %collective-permute-done.4 = bf16[128,2304]{1,0:T(8,128)(2,1)} collective-permute-done((bf16[128,2304]{1,0:T(8,128)(2,1)S(1)}, bf16[128,2304]{1,0:T(8,128)(2,1)}, u32[]{:S(2)}, u32[]{:S(2)}) %collective-permute-start.4) | collective-permute-done | bytes 589856 | tf_op jit(solution)/shard_map/ppermute | solution.py:108
  117.9 2.3 %add_convert_fusion = bf16[128,2304]{1,0:T(8,128)(2,1)} fusion(bf16[128,2304]{1,0:T(8,128)(2,1)} %collective-permute-done.4, bf16[128,2304]{1,0:T(8,128)(2,1)} %collective-permute-done.3, bf16[128,2304]{1,0:T(8,128)(2,1)S(1)} %shard_map.92), kind=kLoop, calls=%fused_computation.11 | loop fusion | flops 1769472 | bytes 2359296 | tf_op jit(solution)/shard_map/convert_element_type | solution.py:166
  120.1 11.1 %all-to-all-done.2 = bf16[8,16,2304]{2,1,0:T(8,128)(2,1)} async-done(((bf16[8,16,2304]{2,1,0:T(8,128)(2,1)}), bf16[8,16,2304]{2,1,0:T(8,128)(2,1)}, u32[]{:S(2)}, u32[]{:S(2)}) %all-to-all-start.2) | async-done | bytes 589856 | tf_op jit(solution)/shard_map/all_to_all | solution.py:161
  131.2 4.4 %all-to-all-start.3 = ((bf16[8,16,2304]{2,1,0:T(8,128)(2,1)}), bf16[8,16,2304]{2,1,0:T(8,128)(2,1)S(1)}, u32[]{:S(2)}, u32[]{:S(2)}) async-start(bf16[8,16,2304]{2,1,0:T(8,128)(2,1)} %bitcast.11), calls=%async_computation.3 | async-start | bytes 1179648 | tf_op jit(solution)/shard_map/all_to_all | solution.py:168
  135.6 1.3 convolution_multiply_fusion
  136.9 1.3 fusion.3
  138.2 2.3 %collective-permute-start.6 = (f32[32,2304]{1,0:T(8,128)S(1)}, f32[32,2304]{1,0:T(8,128)S(1)}, u32[]{:S(2)}, u32[]{:S(2)}) collective-permute-start(f32[32,2304]{1,0:T(8,128)S(1)} %fusion.3), channel_id=1, source_target_pairs={{0,2},{1,3},{2,0},{3,1},{4,6},{5,7},{6,4},{7,5},{8,10},{9,11},{10,... | collective-permute-start | bytes 884744 | tf_op jit(solution)/shard_map/ppermute | solution.py:108
  140.5 9.0 %all-to-all-done.3 = bf16[8,16,2304]{2,1,0:T(8,128)(2,1)S(1)} async-done(((bf16[8,16,2304]{2,1,0:T(8,128)(2,1)}), bf16[8,16,2304]{2,1,0:T(8,128)(2,1)S(1)}, u32[]{:S(2)}, u32[]{:S(2)}) %all-to-all-start.3) | async-done | bytes 589856 | tf_op jit(solution)/shard_map/all_to_all | solution.py:168
  149.5 0.3 convolution_multiply_fusion.2
  149.8 0.0 collective-permute-done.6
  149.8 1.0 fusion.2
  (9 shorter events, 0.1 us)
Async XLA Ops:
  0.0 1.6 %copy-start = (bf16[288,2304]{1,0:T(8,128)(2,1)S(1)}, bf16[288,2304]{1,0:T(8,128)(2,1)}, u32[]{:S(2)}) copy-start(bf16[288,2304]{1,0:T(8,128)(2,1)} %param.11) | copy-start | bytes 3981316
  3.4 7.2 %copy-start.3 = (s32[32,2]{0,1:T(2,128)S(1)}, s32[32,2]{0,1:T(2,128)}, u32[]{:S(2)}) copy-start(s32[32,2]{0,1:T(2,128)} %param.16) | copy-start | bytes 772
  3.4 8.0 %copy-start.4 = (f32[32,2]{0,1:T(2,128)S(1)}, f32[32,2]{0,1:T(2,128)}, u32[]{:S(2)}) copy-start(f32[32,2]{0,1:T(2,128)} %param.17) | copy-start | bytes 772
  3.4 38.8 %all-to-all-start = ((f16[8,32,2304]{2,1,0:T(8,128)(2,1)}), f16[8,32,2304]{2,1,0:T(8,128)(2,1)S(1)}, u32[]{:S(2)}, u32[]{:S(2)}) async-start(f16[8,32,2304]{2,1,0:T(8,128)(2,1)} %bitcast.43), calls=%async_computation | async-start | bytes 2359296 | tf_op jit(solution)/shard_map/all_to_all | solution.py:127
  10.6 31.7 %copy-start.1 = (f32[32,2304]{1,0:T(8,128)S(1)}, f32[32,2304]{1,0:T(8,128)}, u32[]{:S(2)}) copy-start(f32[32,2304]{1,0:T(8,128)} %param.10) | copy-start | bytes 884740
  10.7 31.9 %copy-start.2 = (f32[2304]{0:T(1024)S(1)}, f32[2304]{0:T(1024)}, u32[]{:S(2)}) copy-start(f32[2304]{0:T(1024)} %param.12) | copy-start | bytes 27652
  11.4 7.0 %collective-permute-start = (f32[32,4]{0,1:T(4,128)S(1)}, f32[32,4]{0,1:T(4,128)S(1)}, u32[]{:S(2)}, u32[]{:S(2)}) collective-permute-start(f32[32,4]{0,1:T(4,128)S(1)} %pad_maximum_fusion), channel_id=1, source_target_pairs={{0,2},{1,3},{2,0},{3,1},{4,6},{5,7},{6,4},{7,5},{8,10},{9,11},{10,... | collective-permute-start | bytes 1544 | tf_op jit(solution)/shard_map/ppermute | solution.py:108
  64.7 18.1 %collective-permute-start.1 = (bf16[128,2304]{1,0:T(8,128)(2,1)S(1)}, bf16[128,2304]{1,0:T(8,128)(2,1)S(1)}, u32[]{:S(2)}, u32[]{:S(2)}) collective-permute-start(bf16[128,2304]{1,0:T(8,128)(2,1)S(1)} %bitcast.34), channel_id=1, source_target_pairs={{0,1},{1,2},{2,3},{3,0},{4,5},{5,6},{6,7},{7,4},{8,9},{9,10},{10,1... | collective-permute-start | bytes 1769480 | tf_op jit(solution)/shard_map/ppermute | solution.py:108
  68.1 26.6 %collective-permute-start.2 = (bf16[128,2304]{1,0:T(8,128)(2,1)S(1)}, bf16[128,2304]{1,0:T(8,128)(2,1)S(1)}, u32[]{:S(2)}, u32[]{:S(2)}) collective-permute-start(bf16[128,2304]{1,0:T(8,128)(2,1)S(1)} %bitcast.35), channel_id=1, source_target_pairs={{0,3},{1,0},{2,1},{3,2},{4,7},{5,4},{6,5},{7,6},{8,11},{9,8},{10,9... | collective-permute-start | bytes 1769480 | tf_op jit(solution)/shard_map/ppermute | solution.py:108
  79.1 27.6 %collective-permute-start.5 = (bf16[128,2304]{1,0:T(8,128)(2,1)S(1)}, bf16[128,2304]{1,0:T(8,128)(2,1)S(1)}, u32[]{:S(2)}, u32[]{:S(2)}) collective-permute-start(bf16[128,2304]{1,0:T(8,128)(2,1)S(1)} %bitcast.37), channel_id=1, source_target_pairs={{0,2},{1,3},{2,0},{3,1},{4,6},{5,7},{6,4},{7,5},{8,10},{9,11},{10,... | collective-permute-start | bytes 1769480 | tf_op jit(solution)/shard_map/ppermute | solution.py:108
  98.7 15.1 %collective-permute-start.3 = (bf16[128,2304]{1,0:T(8,128)(2,1)S(1)}, bf16[128,2304]{1,0:T(8,128)(2,1)}, u32[]{:S(2)}, u32[]{:S(2)}) collective-permute-start(bf16[128,2304]{1,0:T(8,128)(2,1)S(1)} %get-tuple-element.20), channel_id=1, source_target_pairs={{0,3},{1,0},{2,1},{3,2},{4,7},{5,4},{6,5},{7,6},{8,11},{9,8},{10,9... | collective-permute-start | bytes 1769480 | tf_op jit(solution)/shard_map/ppermute | solution.py:108
  104.8 13.1 %collective-permute-start.4 = (bf16[128,2304]{1,0:T(8,128)(2,1)S(1)}, bf16[128,2304]{1,0:T(8,128)(2,1)}, u32[]{:S(2)}, u32[]{:S(2)}) collective-permute-start(bf16[128,2304]{1,0:T(8,128)(2,1)S(1)} %get-tuple-element.21), channel_id=1, source_target_pairs={{0,1},{1,2},{2,3},{3,0},{4,5},{5,6},{6,7},{7,4},{8,9},{9,10},{10,1... | collective-permute-start | bytes 1769480 | tf_op jit(solution)/shard_map/ppermute | solution.py:108
  109.7 21.5 %all-to-all-start.2 = ((bf16[8,16,2304]{2,1,0:T(8,128)(2,1)}), bf16[8,16,2304]{2,1,0:T(8,128)(2,1)}, u32[]{:S(2)}, u32[]{:S(2)}) async-start(bf16[8,16,2304]{2,1,0:T(8,128)(2,1)} %bitcast.12), calls=%async_computation.2 | async-start | bytes 1179648 | tf_op jit(solution)/shard_map/all_to_all | solution.py:161
  131.2 18.4 %all-to-all-start.3 = ((bf16[8,16,2304]{2,1,0:T(8,128)(2,1)}), bf16[8,16,2304]{2,1,0:T(8,128)(2,1)S(1)}, u32[]{:S(2)}, u32[]{:S(2)}) async-start(bf16[8,16,2304]{2,1,0:T(8,128)(2,1)} %bitcast.11), calls=%async_computation.3 | async-start | bytes 1179648 | tf_op jit(solution)/shard_map/all_to_all | solution.py:168
  138.2 11.6 %collective-permute-start.6 = (f32[32,2304]{1,0:T(8,128)S(1)}, f32[32,2304]{1,0:T(8,128)S(1)}, u32[]{:S(2)}, u32[]{:S(2)}) collective-permute-start(f32[32,2304]{1,0:T(8,128)S(1)} %fusion.3), channel_id=1, source_target_pairs={{0,2},{1,3},{2,0},{3,1},{4,6},{5,7},{6,4},{7,5},{8,10},{9,11},{10,... | collective-permute-start | bytes 884744 | tf_op jit(solution)/shard_map/ppermute | solution.py:108

commit v8 on v7

--- a/solution.py
+++ b/solution.py
@@ -9,6 +9,7 @@
 
 EXPERTS = 8
 MOST = 16
+HALF = 8
 EPSILON = 1e-06
 
 UNIT_CHUNK = 512
@@ -42,10 +43,10 @@
     )(*(pltpu.with_memory_space_constraint(w, pltpu.HBM) for w in weights))
 
 
-def ffn_kernel(count, *refs):
+def ffn_kernel(count, halves, *refs):
     row_refs, refs = refs[:count], refs[count:]
     (gate_ref, up_ref, down_ref), refs = refs[:3], refs[3:]
-    out_refs, refs = refs[:count], refs[count:]
+    out_refs, refs = refs[: 2 if halves else count], refs[2 if halves else count :]
     act_ref = refs[0]
     depth = row_refs[0].shape[0]
     if count == 1:
@@ -62,11 +63,16 @@
     for start in range(0, down_ref.shape[1], OUT_CHUNK):
         at = pl.ds(start, OUT_CHUNK)
         out = jnp.dot(act_ref[...], down_ref[:, at], preferred_element_type=jnp.float32)
+        if halves:
+            for block in range(depth // HALF):
+                rows = out[block * HALF : (block + 1) * HALF].astype(jnp.bfloat16)
+                out_refs[block % 2][pl.ds(block // 2 * HALF, HALF), at] = rows
+            continue
         for piece in range(count):
             out_refs[piece][:, at] = out[piece * depth : (piece + 1) * depth].astype(jnp.bfloat16)
 
 
-def ffn(pieces, *weights):
+def ffn(pieces, *weights, halves=False):
     count = len(pieces)
     depth, features = pieces[0].shape
     units = weights[0].shape[1]
@@ -75,10 +81,11 @@
     if count > 1:
         scratch.append(pltpu.VMEM((count * depth, features), jnp.bfloat16))
     return pl.pallas_call(
-        functools.partial(ffn_kernel, count),
-        out_shape=[jax.ShapeDtypeStruct((depth, features), jnp.bfloat16)] * count,
+        functools.partial(ffn_kernel, count, halves),
+        out_shape=[jax.ShapeDtypeStruct((depth // 2 if halves else depth, features), jnp.bfloat16)]
+        * (2 if halves else count),
         in_specs=[vmem] * (count + 3),
-        out_specs=[vmem] * count,
+        out_specs=[vmem] * (2 if halves else count),
         scratch_shapes=scratch,
         compiler_params=pltpu.CompilerParams(vmem_limit_bytes=24 << 20),
         cost_estimate=pl.CostEstimate(
@@ -118,7 +125,16 @@
     target = (expert_ids * MOST + position).reshape(row_count, 2)
     far_routing = jnp.concatenate([target.astype(jnp.float32), route_weights], axis=1)
     far_routing = shift(far_routing, 2)
-    residual, far_routing = lax.optimization_barrier((residual, far_routing))
+    slots = jnp.arange(EXPERTS * MOST, dtype=jnp.int32)
+    late_slots = slots.reshape(EXPERTS, MOST)[:, HALF:].reshape(-1)
+
+    def chosen(slot_of, among):
+        return slot_of[:, 0][:, None] == among[None, :], slot_of[:, 1][:, None] == among[None, :]
+
+    far_pair = chosen(far_routing[:, 0:2].astype(jnp.int32), late_slots)
+    far_pair = tuple(value.astype(jnp.bfloat16) for value in far_pair)
+    far_weights = far_routing[:, 2:4]
+    residual, far_pair, far_weights = lax.optimization_barrier((residual, far_pair, far_weights))
     blocks = attn_out.reshape(model_parts, unit_parts, row_count, attn_out.shape[1])
     picked = lax.dynamic_index_in_dim(blocks, lax.axis_index("expert"), axis=1, keepdims=False)
     picked = picked.reshape(model_parts * row_count, attn_out.shape[1])
@@ -128,17 +144,13 @@
     hidden_state = residual + jnp.sum(parts, axis=0, dtype=jnp.float32)
     inverse_rms = lax.rsqrt(jnp.mean(hidden_state * hidden_state, axis=1, keepdims=True) + EPSILON)
     normed = (hidden_state * inverse_rms * norm_gain).astype(jnp.bfloat16)
-    slots = jnp.arange(EXPERTS * MOST, dtype=jnp.int32)
-
-    def chosen(slot_of):
-        return slot_of[:, 0][:, None] == slots[None, :], slot_of[:, 1][:, None] == slots[None, :]
 
     def weighted(pair, weight_of, sums):
         one = jnp.dot(pair[0].astype(jnp.bfloat16), sums, preferred_element_type=jnp.float32)
         two = jnp.dot(pair[1].astype(jnp.bfloat16), sums, preferred_element_type=jnp.float32)
         return weight_of[:, 0:1] * one + weight_of[:, 1:2] * two
 
-    first, second = chosen(target)
+    first, second = chosen(target, slots)
     placement = (first | second).astype(jnp.bfloat16)
     outgoing = lax.dot_general(
         placement, normed, (((0,), (0,)), ((), ())), preferred_element_type=jnp.float32
@@ -157,19 +169,21 @@
     back_after = shift(before_sum, -1)
     back_before = shift(after_sum, 1)
     far_rows = lax.optimization_barrier((far_rows, before_sum))[0]
-    (far_sum,) = ffn([far_rows], *weights)
-    far_sums = lax.all_to_all(
-        far_sum.reshape(model_parts, MOST, features), "mp", split_axis=0, concat_axis=0, tiled=True
-    )
+    far_sum, late_sum = ffn([far_rows], *weights, halves=True)
+    late_sum = late_sum.reshape(model_parts, MOST - HALF, features)
+    far_sums = lax.all_to_all(late_sum, "mp", split_axis=0, concat_axis=0, tiled=True)
+    back_far = shift(far_sum, 2).reshape(model_parts, HALF, features)
     near = own_sum.astype(jnp.float32)
     near = near + back_after.astype(jnp.float32) + back_before.astype(jnp.float32)
-    near = near.astype(jnp.bfloat16).reshape(model_parts, MOST, features)
+    near = lax.optimization_barrier(near).reshape(model_parts, MOST, features)
+    near = jnp.concatenate([near[:, :HALF] + back_far.astype(jnp.float32), near[:, HALF:]], axis=1)
+    near = near.astype(jnp.bfloat16)
     near, far_sums = lax.optimization_barrier((near, far_sums))
     near = lax.all_to_all(near, "mp", split_axis=0, concat_axis=0, tiled=True)
     far_part = weighted(
-        chosen(far_routing[:, 0:2].astype(jnp.int32)),
-        far_routing[:, 2:4],
-        far_sums.reshape(EXPERTS * MOST, features),
+        far_pair,
+        far_weights,
+        far_sums.reshape(EXPERTS * (MOST - HALF), features),
     )
     far_part = shift(far_part, 2)
     near_part = weighted((first, second), route_weights, near.reshape(EXPERTS * MOST, features))

time: 151 us -> 152 us (level)
  starting transfers between devices: 41.7 us -> 43.3 us
    all_to_all x1, waiting for transfers between devices: 11.1 us -> 1.66 us  [body(): lax.all_to_all(late_sum, 'mp', split_axis=0, concat_axis=0, tiled=True)]
    ppermute x7 -> x8, waiting for transfers between devices: 17.9 us -> 25.7 us  [shift(): lax.ppermute(value, 'expert', [(i, (i + by) % unit_parts) for i in range(...]
    convert_element_type x2 -> x1, other arithmetic: 2.28 us -> 0.08 us  [body(): far_pair = tuple((value.astype(jnp.bfloat16) for value in far_pair))]
    ppermute x7 -> x8, starting transfers between devices: 25.9 us -> 26.6 us  [shift(): lax.ppermute(value, 'expert', [(i, (i + by) % unit_parts) for i in range(...]
  transfers between devices with their start and end apart: 10 -> 11, of which waited for: 6 -> 6; matrix products, arithmetic and copies ran while one was open for 4% -> 4% of each run, Pallas kernels for 9% -> 9%
where the time goes in v8:
time: 152 us; the launch traced here: 151 us
  waiting for transfers between devices  60.8 us (40%)
  starting transfers between devices  43.3 us (28%)
  blocking collectives  21.7 us (14%)
  Pallas kernels  14.1 us (9%)
  matrix products  5.82 us (4%)
  other arithmetic  3.13 us (2%)
  local copies, waits for them, and re-layouts  2.16 us (1%)
    ppermute x8, starting transfers between devices, shift(): lax.ppermute(value, 'expert', [(i, (i + by) % unit_parts) for i in range(...  26.6 us
    ppermute x8, waiting for transfers between devices, shift(): lax.ppermute(value, 'expert', [(i, (i + by) % unit_parts) for i in range(...  25.7 us
    all_to_all x1, waiting for transfers between devices, body(): parts = lax.all_to_all(parts, 'mp', split_axis=0, concat_axis=0, tiled=True)  23.7 us
    all_to_all x1, blocking collectives, body(): lax.all_to_all(outgoing, 'mp', split_axis=0, concat_axis=0, tiled=True)  21.7 us
    all_to_all x1, waiting for transfers between devices, body(): near = lax.all_to_all(near, 'mp', split_axis=0, concat_axis=0, tiled=True)  9.71 us
    pallas_call x3, Pallas kernels, ffn(): pl.pallas_call(functools.partial(ffn_kernel, count, halves), out_shape=[j...  8.96 us
    all_to_all x1, starting transfers between devices, body(): parts = lax.all_to_all(parts, 'mp', split_axis=0, concat_axis=0, tiled=True)  7.23 us
    all_to_all x1, starting transfers between devices, body(): near = lax.all_to_all(near, 'mp', split_axis=0, concat_axis=0, tiled=True)  5.43 us
  transfers between devices with their start and end apart: 11, of which 6 were waited for; matrix products, arithmetic and copies ran while one was open for 4% of the time, Pallas kernels for 9%

profile of v8, /device:TPU:448, one launch (start us, length us, event | category | flops | bytes accessed | tf_op | source)
XLA Modules:
  0.0 151.4 jit_solution(8526355261465456682)
XLA Ops:
  0.0 0.0 copy-start
  0.0 1.5 %copy.26 = bf16[1024,288]{1,0:T(8,128)(2,1)S(1)} copy(bf16[1024,288]{0,1:T(8,128)(2,1)} %param.9) | data formatting | bytes 1179648 | tf_op args[0]
  1.6 0.0 copy-done
  1.6 1.8 %convolution_convert_fusion = f16[256,2304]{1,0:T(8,128)(2,1)} fusion(bf16[256,288]{1,0:T(8,128)(2,1)S(1)} %bitcast.55, bf16[288,2304]{1,0:T(8,128)(2,1)S(1)} %copy-done), kind=kOutput, calls=%fused_computation | convolution fusion | flops 340328448 | bytes 2654208 | tf_op jit(solution)/shard_map/dot_general | solution.py:141
  3.4 0.0 copy-start.5
  3.4 0.0 copy-start.6
  3.4 7.2 %all-to-all-start = ((f16[8,32,2304]{2,1,0:T(8,128)(2,1)}), f16[8,32,2304]{2,1,0:T(8,128)(2,1)S(1)}, u32[]{:S(2)}, u32[]{:S(2)}) async-start(f16[8,32,2304]{2,1,0:T(8,128)(2,1)} %bitcast.50), calls=%async_computation | async-start | bytes 2359296 | tf_op jit(solution)/shard_map/all_to_all | solution.py:143
  10.6 0.0 copy-done.5
  10.6 0.0 copy-start.3
  10.7 0.1 copy.24
  10.7 0.1 eq.79
  10.9 0.1 fusion.9
  10.9 0.1 reduce_window_sum.11
  11.0 0.2 select_reduce_fusion
  11.2 0.1 reduce_sum.30
  11.3 0.1 copy.25
  11.4 0.0 copy-done.6
  11.4 4.9 %collective-permute-start = (f32[32,4]{0,1:T(4,128)S(1)}, f32[32,4]{0,1:T(4,128)S(1)}, u32[]{:S(2)}, u32[]{:S(2)}) collective-permute-start(f32[32,4]{0,1:T(4,128)S(1)} %pad_maximum_fusion.1), channel_id=1, source_target_pairs={{0,2},{1,3},{2,0},{3,1},{4,6},{5,7},{6,4},{7,5},{8,10},{9,11},{10,... | collective-permute-start | bytes 1544 | tf_op jit(solution)/shard_map/ppermute | solution.py:115
  16.4 0.1 slice.44
  16.5 0.1 eq.85
  16.6 1.9 %collective-permute-done = f32[32,4]{0,1:T(4,128)S(1)} collective-permute-done((f32[32,4]{0,1:T(4,128)S(1)}, f32[32,4]{0,1:T(4,128)S(1)}, u32[]{:S(2)}, u32[]{:S(2)}) %collective-permute-start) | collective-permute-done | bytes 544 | tf_op jit(solution)/shard_map/ppermute | solution.py:115
  18.4 0.1 compare_convert_fusion
  18.5 0.0 copy-start.4
  18.5 23.7 %all-to-all-done = f16[8,32,2304]{2,1,0:T(8,128)(2,1)S(1)} async-done(((f16[8,32,2304]{2,1,0:T(8,128)(2,1)}), f16[8,32,2304]{2,1,0:T(8,128)(2,1)S(1)}, u32[]{:S(2)}, u32[]{:S(2)}) %all-to-all-start) | async-done | bytes 1179680 | tf_op jit(solution)/shard_map/all_to_all | solution.py:143
  42.2 0.2 convert_reduce_fusion
  42.4 0.0 copy-done.3
  42.4 0.1 multiply_reduce_fusion
  42.5 0.0 copy-start.1
  42.6 0.0 copy-done.4
  42.6 0.4 convolution_convert_fusion.1
  43.0 21.7 %all_to_all.20 = bf16[8,16,2304]{2,1,0:T(8,128)(2,1)S(1)} all-to-all(bf16[8,16,2304]{2,1,0:T(8,128)(2,1)S(1)} %bitcast.53), channel_id=1, replica_groups=mesh['dp'=16,'mp'=8,'expert'=4] {'mp'}, dimensions={0} | all-to-all | bytes 1179648 | tf_op jit(solution)/shard_map/all_to_all | solution.py:159
  64.7 4.7 %collective-permute-start.2 = (bf16[128,2304]{1,0:T(8,128)(2,1)S(1)}, bf16[128,2304]{1,0:T(8,128)(2,1)S(1)}, u32[]{:S(2)}, u32[]{:S(2)}) collective-permute-start(bf16[128,2304]{1,0:T(8,128)(2,1)S(1)} %bitcast.41), channel_id=1, source_target_pairs={{0,3},{1,0},{2,1},{3,2},{4,7},{5,4},{6,5},{7,6},{8,11},{9,8},{10,9... | collective-permute-start | bytes 1769480 | tf_op jit(solution)/shard_map/ppermute | solution.py:115
  69.4 1.9 %collective-permute-start.1 = (bf16[128,2304]{1,0:T(8,128)(2,1)S(1)}, bf16[128,2304]{1,0:T(8,128)(2,1)S(1)}, u32[]{:S(2)}, u32[]{:S(2)}) collective-permute-start(bf16[128,2304]{1,0:T(8,128)(2,1)S(1)} %bitcast.42), channel_id=1, source_target_pairs={{0,1},{1,2},{2,3},{3,0},{4,5},{5,6},{6,7},{7,4},{8,9},{9,10},{10,1... | collective-permute-start | bytes 1769480 | tf_op jit(solution)/shard_map/ppermute | solution.py:115
  71.3 0.0 copy-done.1
  71.4 5.1 %shard_map.91 = (bf16[2304,1024]{1,0:T(8,128)(2,1)S(1)}, bf16[2304,1024]{1,0:T(8,128)(2,1)S(1)}, bf16[1024,2304]{1,0:T(8,128)(2,1)S(1)}) custom-call(bf16[2304,1024]{1,0:T(8,128)(2,1)} %bitcast.47, bf16[2304,1024]{1,0:T(8,128)(2,1)} %bitcast.48, bf16[1024,2304]{1,0:T(8,128)(2,1)} %bitcast.49), custom_call_target="tpu_custom_call" | custom-call | bytes 28311552 | tf_op jit(solution)/shard_map/pallas_call | solution.py:35
  76.5 2.1 %shard_map.92 = bf16[128,2304]{1,0:T(8,128)(2,1)S(1)} custom-call(bf16[128,2304]{1,0:T(8,128)(2,1)S(1)} %bitcast.43, bf16[2304,1024]{1,0:T(8,128)(2,1)S(1)} %get-tuple-element.21.refs_1_.refs_2_, bf16[2304,1024]{1,0:T(8,128)(2,1)S(1)} %get-tuple-element.22.refs_2_.refs_3_, bf16[1024,2304]{1,0:T(8,128)(2,1)S(1)} %get-tuple-element.23.refs_3_.refs_4_), custom_call_target="tpu_custom_call" | custom-call | flops 1811939328 | bytes 15335424 | tf_op jit(solution)/shard_map/pallas_call | solution.py:83
  78.6 4.2 %collective-permute-start.5 = (bf16[128,2304]{1,0:T(8,128)(2,1)S(1)}, bf16[128,2304]{1,0:T(8,128)(2,1)S(1)}, u32[]{:S(2)}, u32[]{:S(2)}) collective-permute-start(bf16[128,2304]{1,0:T(8,128)(2,1)S(1)} %bitcast.44), channel_id=1, source_target_pairs={{0,2},{1,3},{2,0},{3,1},{4,6},{5,7},{6,4},{7,5},{8,10},{9,11},{10,... | collective-permute-start | bytes 1769480 | tf_op jit(solution)/shard_map/ppermute | solution.py:115
  82.8 0.0 collective-permute-done.2.refs_1_
  82.9 17.1 %collective-permute-done.1.refs_0_ = bf16[128,2304]{1,0:T(8,128)(2,1)S(1)} collective-permute-done((bf16[128,2304]{1,0:T(8,128)(2,1)S(1)}, bf16[128,2304]{1,0:T(8,128)(2,1)S(1)}, u32[]{:S(2)}, u32[]{:S(2)}) %collective-permute-start.1) | collective-permute-done | bytes 589856 | tf_op jit(solution)/shard_map/ppermute | solution.py:115
  99.9 4.0 %shard_map.93 = (bf16[128,2304]{1,0:T(8,128)(2,1)S(1)}, bf16[128,2304]{1,0:T(8,128)(2,1)S(1)}) custom-call(bf16[128,2304]{1,0:T(8,128)(2,1)S(1)} %collective-permute-done.1.refs_0_, bf16[128,2304]{1,0:T(8,128)(2,1)S(1)} %collective-permute-done.2.refs_1_, bf16[2304,1024]{1,0:T(8,128)(2,1)S(1)} %get-tuple-element.21.refs_1_.refs_2_, ...), custom_call_target="tpu_custom_call" | custom-call | flops 3623878656 | bytes 16515072 | tf_op jit(solution)/shard_map/pallas_call | solution.py:83
  103.9 1.9 %collective-permute-start.4 = (bf16[128,2304]{1,0:T(8,128)(2,1)S(1)}, bf16[128,2304]{1,0:T(8,128)(2,1)}, u32[]{:S(2)}, u32[]{:S(2)}) collective-permute-start(bf16[128,2304]{1,0:T(8,128)(2,1)S(1)} %get-tuple-element.25), channel_id=1, source_target_pairs={{0,1},{1,2},{2,3},{3,0},{4,5},{5,6},{6,7},{7,4},{8,9},{9,10},{10,1... | collective-permute-start | bytes 1769480 | tf_op jit(solution)/shard_map/ppermute | solution.py:115
  105.8 5.1 %collective-permute-start.3 = (bf16[128,2304]{1,0:T(8,128)(2,1)S(1)}, bf16[128,2304]{1,0:T(8,128)(2,1)}, u32[]{:S(2)}, u32[]{:S(2)}) collective-permute-start(bf16[128,2304]{1,0:T(8,128)(2,1)S(1)} %get-tuple-element.24), channel_id=1, source_target_pairs={{0,3},{1,0},{2,1},{3,2},{4,7},{5,4},{6,5},{7,6},{8,11},{9,8},{10,9... | collective-permute-start | bytes 1769480 | tf_op jit(solution)/shard_map/ppermute | solution.py:115
  111.0 0.0 collective-permute-done.5.refs_0_
  111.0 2.9 %shard_map.94 = (bf16[64,2304]{1,0:T(8,128)(2,1)S(1)}, bf16[64,2304]{1,0:T(8,128)(2,1)}) custom-call(bf16[128,2304]{1,0:T(8,128)(2,1)S(1)} %collective-permute-done.5.refs_0_, bf16[2304,1024]{1,0:T(8,128)(2,1)S(1)} %get-tuple-element.21.refs_1_.refs_2_, bf16[2304,1024]{1,0:T(8,128)(2,1)S(1)} %get-tuple-element.22.refs_2_.refs_3_, ...), custom_call_target="tpu_custom_call" | custom-call | flops 1811939328 | bytes 15335424 | tf_op jit(solution)/shard_map/pallas_call | solution.py:83
  113.8 4.1 %all-to-all-start.2 = ((bf16[8,8,2304]{2,1,0:T(8,128)(2,1)}), bf16[8,8,2304]{2,1,0:T(8,128)(2,1)}, u32[]{:S(2)}, u32[]{:S(2)}) async-start(bf16[8,8,2304]{2,1,0:T(8,128)(2,1)} %bitcast.15), calls=%async_computation.2 | async-start | bytes 589824 | tf_op jit(solution)/shard_map/all_to_all | solution.py:174
  117.9 1.9 %collective-permute-start.6 = (bf16[64,2304]{1,0:T(8,128)(2,1)S(1)}, bf16[64,2304]{1,0:T(8,128)(2,1)S(1)}, u32[]{:S(2)}, u32[]{:S(2)}) collective-permute-start(bf16[64,2304]{1,0:T(8,128)(2,1)S(1)} %get-tuple-element.28), channel_id=1, source_target_pairs={{0,2},{1,3},{2,0},{3,1},{4,6},{5,7},{6,4},{7,5},{8,10},{9,11},{10,... | collective-permute-start | bytes 884744 | tf_op jit(solution)/shard_map/ppermute | solution.py:115
  119.8 0.0 collective-permute-done.4
  119.9 0.0 collective-permute-done.3
  119.9 1.4 convert_add_fusion
  121.3 6.7 %collective-permute-done.6 = bf16[64,2304]{1,0:T(8,128)(2,1)S(1)} collective-permute-done((bf16[64,2304]{1,0:T(8,128)(2,1)S(1)}, bf16[64,2304]{1,0:T(8,128)(2,1)S(1)}, u32[]{:S(2)}, u32[]{:S(2)}) %collective-permute-start.6) | collective-permute-done | bytes 294944 | tf_op jit(solution)/shard_map/ppermute | solution.py:115
  128.0 0.1 fusion.4
  128.1 0.9 pad_maximum_fusion
  129.0 1.7 %all-to-all-done.2 = bf16[8,8,2304]{2,1,0:T(8,128)(2,1)} async-done(((bf16[8,8,2304]{2,1,0:T(8,128)(2,1)}), bf16[8,8,2304]{2,1,0:T(8,128)(2,1)}, u32[]{:S(2)}, u32[]{:S(2)}) %all-to-all-start.2) | async-done | bytes 294944 | tf_op jit(solution)/shard_map/all_to_all | solution.py:174
  130.7 5.4 %all-to-all-start.3 = ((bf16[8,16,2304]{2,1,0:T(8,128)(2,1)}), bf16[8,16,2304]{2,1,0:T(8,128)(2,1)S(1)}, u32[]{:S(2)}, u32[]{:S(2)}) async-start(bf16[8,16,2304]{2,1,0:T(8,128)(2,1)} %pad_maximum_fusion), calls=%async_computation.3 | async-start | bytes 1179648 | tf_op jit(solution)/shard_map/all_to_all | solution.py:182
  136.1 0.0 copy-start.2
  136.1 1.2 convolution_multiply_fusion.3
  137.3 1.1 fusion.3
  138.4 1.9 %collective-permute-start.7 = (f32[32,2304]{1,0:T(8,128)S(1)}, f32[32,2304]{1,0:T(8,128)S(1)}, u32[]{:S(2)}, u32[]{:S(2)}) collective-permute-start(f32[32,2304]{1,0:T(8,128)S(1)} %fusion.3), channel_id=1, source_target_pairs={{0,2},{1,3},{2,0},{3,1},{4,6},{5,7},{6,4},{7,5},{8,10},{9,11},{10,... | collective-permute-start | bytes 884744 | tf_op jit(solution)/shard_map/ppermute | solution.py:115
  140.4 9.7 %all-to-all-done.3 = bf16[8,16,2304]{2,1,0:T(8,128)(2,1)S(1)} async-done(((bf16[8,16,2304]{2,1,0:T(8,128)(2,1)}), bf16[8,16,2304]{2,1,0:T(8,128)(2,1)S(1)}, u32[]{:S(2)}, u32[]{:S(2)}) %all-to-all-start.3) | async-done | bytes 589856 | tf_op jit(solution)/shard_map/all_to_all | solution.py:182
  150.1 0.3 convolution_multiply_fusion
  150.3 0.0 collective-permute-done.7
  150.4 0.0 copy-done.2
  150.4 1.0 fusion.2
  (11 shorter events, 0.1 us)
Async XLA Ops:
  0.0 1.6 %copy-start = (bf16[288,2304]{1,0:T(8,128)(2,1)S(1)}, bf16[288,2304]{1,0:T(8,128)(2,1)}, u32[]{:S(2)}) copy-start(bf16[288,2304]{1,0:T(8,128)(2,1)} %param.11) | copy-start | bytes 3981316
  3.4 7.2 %copy-start.5 = (s32[32,2]{0,1:T(2,128)S(1)}, s32[32,2]{0,1:T(2,128)}, u32[]{:S(2)}) copy-start(s32[32,2]{0,1:T(2,128)} %param.16) | copy-start | bytes 772
  3.4 8.0 %copy-start.6 = (f32[32,2]{0,1:T(2,128)S(1)}, f32[32,2]{0,1:T(2,128)}, u32[]{:S(2)}) copy-start(f32[32,2]{0,1:T(2,128)} %param.17) | copy-start | bytes 772
  3.4 38.8 %all-to-all-start = ((f16[8,32,2304]{2,1,0:T(8,128)(2,1)}), f16[8,32,2304]{2,1,0:T(8,128)(2,1)S(1)}, u32[]{:S(2)}, u32[]{:S(2)}) async-start(f16[8,32,2304]{2,1,0:T(8,128)(2,1)} %bitcast.50), calls=%async_computation | async-start | bytes 2359296 | tf_op jit(solution)/shard_map/all_to_all | solution.py:143
  10.6 31.7 %copy-start.3 = (f32[32,2304]{1,0:T(8,128)S(1)}, f32[32,2304]{1,0:T(8,128)}, u32[]{:S(2)}) copy-start(f32[32,2304]{1,0:T(8,128)} %param.10) | copy-start | bytes 884740
  11.4 7.0 %collective-permute-start = (f32[32,4]{0,1:T(4,128)S(1)}, f32[32,4]{0,1:T(4,128)S(1)}, u32[]{:S(2)}, u32[]{:S(2)}) collective-permute-start(f32[32,4]{0,1:T(4,128)S(1)} %pad_maximum_fusion.1), channel_id=1, source_target_pairs={{0,2},{1,3},{2,0},{3,1},{4,6},{5,7},{6,4},{7,5},{8,10},{9,11},{10,... | collective-permute-start | bytes 1544 | tf_op jit(solution)/shard_map/ppermute | solution.py:115
  18.5 24.1 %copy-start.4 = (f32[2304]{0:T(1024)S(1)}, f32[2304]{0:T(1024)}, u32[]{:S(2)}) copy-start(f32[2304]{0:T(1024)} %param.12) | copy-start | bytes 27652
  42.5 28.8 %copy-start.1 = (f32[32,2304]{1,0:T(8,128)}, f32[32,2304]{1,0:T(8,128)S(1)}, u32[]{:S(2)}) copy-start(f32[32,2304]{1,0:T(8,128)S(1)} %get-tuple-element.36) | copy-start | bytes 884740
  64.7 18.1 %collective-permute-start.2 = (bf16[128,2304]{1,0:T(8,128)(2,1)S(1)}, bf16[128,2304]{1,0:T(8,128)(2,1)S(1)}, u32[]{:S(2)}, u32[]{:S(2)}) collective-permute-start(bf16[128,2304]{1,0:T(8,128)(2,1)S(1)} %bitcast.41), channel_id=1, source_target_pairs={{0,3},{1,0},{2,1},{3,2},{4,7},{5,4},{6,5},{7,6},{8,11},{9,8},{10,9... | collective-permute-start | bytes 1769480 | tf_op jit(solution)/shard_map/ppermute | solution.py:115
  69.4 30.5 %collective-permute-start.1 = (bf16[128,2304]{1,0:T(8,128)(2,1)S(1)}, bf16[128,2304]{1,0:T(8,128)(2,1)S(1)}, u32[]{:S(2)}, u32[]{:S(2)}) collective-permute-start(bf16[128,2304]{1,0:T(8,128)(2,1)S(1)} %bitcast.42), channel_id=1, source_target_pairs={{0,1},{1,2},{2,3},{3,0},{4,5},{5,6},{6,7},{7,4},{8,9},{9,10},{10,1... | collective-permute-start | bytes 1769480 | tf_op jit(solution)/shard_map/ppermute | solution.py:115
  78.6 32.3 %collective-permute-start.5 = (bf16[128,2304]{1,0:T(8,128)(2,1)S(1)}, bf16[128,2304]{1,0:T(8,128)(2,1)S(1)}, u32[]{:S(2)}, u32[]{:S(2)}) collective-permute-start(bf16[128,2304]{1,0:T(8,128)(2,1)S(1)} %bitcast.44), channel_id=1, source_target_pairs={{0,2},{1,3},{2,0},{3,1},{4,6},{5,7},{6,4},{7,5},{8,10},{9,11},{10,... | collective-permute-start | bytes 1769480 | tf_op jit(solution)/shard_map/ppermute | solution.py:115
  103.9 15.9 %collective-permute-start.4 = (bf16[128,2304]{1,0:T(8,128)(2,1)S(1)}, bf16[128,2304]{1,0:T(8,128)(2,1)}, u32[]{:S(2)}, u32[]{:S(2)}) collective-permute-start(bf16[128,2304]{1,0:T(8,128)(2,1)S(1)} %get-tuple-element.25), channel_id=1, source_target_pairs={{0,1},{1,2},{2,3},{3,0},{4,5},{5,6},{6,7},{7,4},{8,9},{9,10},{10,1... | collective-permute-start | bytes 1769480 | tf_op jit(solution)/shard_map/ppermute | solution.py:115
  105.8 14.0 %collective-permute-start.3 = (bf16[128,2304]{1,0:T(8,128)(2,1)S(1)}, bf16[128,2304]{1,0:T(8,128)(2,1)}, u32[]{:S(2)}, u32[]{:S(2)}) collective-permute-start(bf16[128,2304]{1,0:T(8,128)(2,1)S(1)} %get-tuple-element.24), channel_id=1, source_target_pairs={{0,3},{1,0},{2,1},{3,2},{4,7},{5,4},{6,5},{7,6},{8,11},{9,8},{10,9... | collective-permute-start | bytes 1769480 | tf_op jit(solution)/shard_map/ppermute | solution.py:115
  113.8 16.8 %all-to-all-start.2 = ((bf16[8,8,2304]{2,1,0:T(8,128)(2,1)}), bf16[8,8,2304]{2,1,0:T(8,128)(2,1)}, u32[]{:S(2)}, u32[]{:S(2)}) async-start(bf16[8,8,2304]{2,1,0:T(8,128)(2,1)} %bitcast.15), calls=%async_computation.2 | async-start | bytes 589824 | tf_op jit(solution)/shard_map/all_to_all | solution.py:174
  117.9 10.1 %collective-permute-start.6 = (bf16[64,2304]{1,0:T(8,128)(2,1)S(1)}, bf16[64,2304]{1,0:T(8,128)(2,1)S(1)}, u32[]{:S(2)}, u32[]{:S(2)}) collective-permute-start(bf16[64,2304]{1,0:T(8,128)(2,1)S(1)} %get-tuple-element.28), channel_id=1, source_target_pairs={{0,2},{1,3},{2,0},{3,1},{4,6},{5,7},{6,4},{7,5},{8,10},{9,11},{10,... | collective-permute-start | bytes 884744 | tf_op jit(solution)/shard_map/ppermute | solution.py:115
  130.7 19.4 %all-to-all-start.3 = ((bf16[8,16,2304]{2,1,0:T(8,128)(2,1)}), bf16[8,16,2304]{2,1,0:T(8,128)(2,1)S(1)}, u32[]{:S(2)}, u32[]{:S(2)}) async-start(bf16[8,16,2304]{2,1,0:T(8,128)(2,1)} %pad_maximum_fusion), calls=%async_computation.3 | async-start | bytes 1179648 | tf_op jit(solution)/shard_map/all_to_all | solution.py:182
  136.1 14.3 %copy-start.2 = (f32[32,2304]{1,0:T(8,128)S(1)}, f32[32,2304]{1,0:T(8,128)}, u32[]{:S(2)}) copy-start(f32[32,2304]{1,0:T(8,128)} %copy-done.1) | copy-start | bytes 884740
  138.4 11.9 %collective-permute-start.7 = (f32[32,2304]{1,0:T(8,128)S(1)}, f32[32,2304]{1,0:T(8,128)S(1)}, u32[]{:S(2)}, u32[]{:S(2)}) collective-permute-start(f32[32,2304]{1,0:T(8,128)S(1)} %fusion.3), channel_id=1, source_target_pairs={{0,2},{1,3},{2,0},{3,1},{4,6},{5,7},{6,4},{7,5},{8,10},{9,11},{10,... | collective-permute-start | bytes 884744 | tf_op jit(solution)/shard_map/ppermute | solution.py:115

commit v9 on v8

--- a/solution.py
+++ b/solution.py
@@ -164,7 +164,10 @@
     before_rows = shift(own, 1)
     after_rows = shift(own, -1)
     (own_sum,) = ffn([own], *weights)
-    far_rows = shift(lax.optimization_barrier((own, own_sum))[0], 2)
+    later, before_rows, after_rows, own_sum = lax.optimization_barrier(
+        (own, before_rows, after_rows, own_sum)
+    )
+    far_rows = shift(later, 2)
     before_sum, after_sum = ffn([before_rows, after_rows], *weights)
     back_after = shift(before_sum, -1)
     back_before = shift(after_sum, 1)
@@ -172,7 +175,9 @@
     far_sum, late_sum = ffn([far_rows], *weights, halves=True)
     late_sum = late_sum.reshape(model_parts, MOST - HALF, features)
     far_sums = lax.all_to_all(late_sum, "mp", split_axis=0, concat_axis=0, tiled=True)
-    back_far = shift(far_sum, 2).reshape(model_parts, HALF, features)
+    back_far = shift(far_sum, 2)
+    far_sums, back_far = lax.optimization_barrier((far_sums, back_far))
+    back_far = back_far.reshape(model_parts, HALF, features)
     near = own_sum.astype(jnp.float32)
     near = near + back_after.astype(jnp.float32) + back_before.astype(jnp.float32)
     near = lax.optimization_barrier(near).reshape(model_parts, MOST, features)

time: 152 us -> 148 us (0.974)
  waiting for transfers between devices: 60.8 us -> 54.1 us
    ppermute x8, waiting for transfers between devices: 25.7 us -> 17.2 us  [shift(): lax.ppermute(value, 'expert', [(i, (i + by) % unit_parts) for i in range(...]
    ppermute x8, starting transfers between devices: 26.6 us -> 29.8 us  [shift(): lax.ppermute(value, 'expert', [(i, (i + by) % unit_parts) for i in range(...]
    all_to_all x1, waiting for transfers between devices: 1.66 us -> 4.14 us  [body(): lax.all_to_all(late_sum, 'mp', split_axis=0, concat_axis=0, tiled=True)]
    all_to_all x1, starting transfers between devices: 5.43 us -> 3.54 us  [body(): near = lax.all_to_all(near, 'mp', split_axis=0, concat_axis=0, tiled=True)]
  transfers between devices with their start and end apart: 11 -> 11, of which waited for: 6 -> 9; matrix products, arithmetic and copies ran while one was open for 4% -> 3% of each run, Pallas kernels for 9% -> 10%
where the time goes in v9:
time: 148 us; the launch traced here: 147 us
  waiting for transfers between devices  54.1 us (37%)
  starting transfers between devices  44.6 us (30%)
  blocking collectives  21.7 us (15%)
  Pallas kernels  14.1 us (10%)
  matrix products  5.82 us (4%)
  other arithmetic  4.09 us (3%)
  local copies, waits for them, and re-layouts  2.16 us (1%)
    ppermute x8, starting transfers between devices, shift(): lax.ppermute(value, 'expert', [(i, (i + by) % unit_parts) for i in range(...  29.8 us
    all_to_all x1, waiting for transfers between devices, body(): parts = lax.all_to_all(parts, 'mp', split_axis=0, concat_axis=0, tiled=True)  23.7 us
    all_to_all x1, blocking collectives, body(): lax.all_to_all(outgoing, 'mp', split_axis=0, concat_axis=0, tiled=True)  21.7 us
    ppermute x8, waiting for transfers between devices, shift(): lax.ppermute(value, 'expert', [(i, (i + by) % unit_parts) for i in range(...  17.2 us
    all_to_all x1, waiting for transfers between devices, body(): near = lax.all_to_all(near, 'mp', split_axis=0, concat_axis=0, tiled=True)  9.04 us
    pallas_call x3, Pallas kernels, ffn(): pl.pallas_call(functools.partial(ffn_kernel, count, halves), out_shape=[j...  8.95 us
    all_to_all x1, starting transfers between devices, body(): parts = lax.all_to_all(parts, 'mp', split_axis=0, concat_axis=0, tiled=True)  7.23 us
    pallas_call x1, Pallas kernels, load(): pl.pallas_call(load_kernel, out_shape=[pltpu.VMEM(w.shape, w.dtype) for w...  5.15 us
  transfers between devices with their start and end apart: 11, of which 9 were waited for; matrix products, arithmetic and copies ran while one was open for 3% of the time, Pallas kernels for 10%

profile of v9, /device:TPU:448, one launch (start us, length us, event | category | flops | bytes accessed | tf_op | source)
XLA Modules:
  0.0 147.0 jit_solution(2826923345125653187)
XLA Ops:
  0.0 0.0 copy-start
  0.0 1.5 %copy.26 = bf16[1024,288]{1,0:T(8,128)(2,1)S(1)} copy(bf16[1024,288]{0,1:T(8,128)(2,1)} %param.9) | data formatting | bytes 1179648 | tf_op args[0]
  1.6 0.0 copy-done
  1.6 1.8 %convolution_convert_fusion = f16[256,2304]{1,0:T(8,128)(2,1)} fusion(bf16[256,288]{1,0:T(8,128)(2,1)S(1)} %bitcast.55, bf16[288,2304]{1,0:T(8,128)(2,1)S(1)} %copy-done), kind=kOutput, calls=%fused_computation | convolution fusion | flops 340328448 | bytes 2654208 | tf_op jit(solution)/shard_map/dot_general | solution.py:141
  3.4 0.0 copy-start.5
  3.4 0.0 copy-start.6
  3.4 7.2 %all-to-all-start = ((f16[8,32,2304]{2,1,0:T(8,128)(2,1)}), f16[8,32,2304]{2,1,0:T(8,128)(2,1)S(1)}, u32[]{:S(2)}, u32[]{:S(2)}) async-start(f16[8,32,2304]{2,1,0:T(8,128)(2,1)} %bitcast.50), calls=%async_computation | async-start | bytes 2359296 | tf_op jit(solution)/shard_map/all_to_all | solution.py:143
  10.6 0.0 copy-done.5
  10.6 0.0 copy-start.3
  10.7 0.1 copy.24
  10.7 0.1 eq.79
  10.9 0.1 fusion.9
  10.9 0.1 reduce_window_sum.11
  11.0 0.2 select_reduce_fusion
  11.2 0.1 reduce_sum.30
  11.3 0.1 copy.25
  11.4 0.0 copy-done.6
  11.4 4.9 %collective-permute-start = (f32[32,4]{0,1:T(4,128)S(1)}, f32[32,4]{0,1:T(4,128)S(1)}, u32[]{:S(2)}, u32[]{:S(2)}) collective-permute-start(f32[32,4]{0,1:T(4,128)S(1)} %pad_maximum_fusion.1), channel_id=1, source_target_pairs={{0,2},{1,3},{2,0},{3,1},{4,6},{5,7},{6,4},{7,5},{8,10},{9,11},{10,... | collective-permute-start | bytes 1544 | tf_op jit(solution)/shard_map/ppermute | solution.py:115
  16.4 0.1 slice.44
  16.5 0.1 eq.85
  16.6 1.9 %collective-permute-done = f32[32,4]{0,1:T(4,128)S(1)} collective-permute-done((f32[32,4]{0,1:T(4,128)S(1)}, f32[32,4]{0,1:T(4,128)S(1)}, u32[]{:S(2)}, u32[]{:S(2)}) %collective-permute-start) | collective-permute-done | bytes 544 | tf_op jit(solution)/shard_map/ppermute | solution.py:115
  18.4 0.1 compare_convert_fusion
  18.5 0.0 copy-start.4
  18.5 23.7 %all-to-all-done = f16[8,32,2304]{2,1,0:T(8,128)(2,1)S(1)} async-done(((f16[8,32,2304]{2,1,0:T(8,128)(2,1)}), f16[8,32,2304]{2,1,0:T(8,128)(2,1)S(1)}, u32[]{:S(2)}, u32[]{:S(2)}) %all-to-all-start) | async-done | bytes 1179680 | tf_op jit(solution)/shard_map/all_to_all | solution.py:143
  42.2 0.2 convert_reduce_fusion
  42.4 0.0 copy-done.3
  42.4 0.1 multiply_reduce_fusion
  42.5 0.0 copy-start.1
  42.6 0.0 copy-done.4
  42.6 0.4 convolution_convert_fusion.1
  43.0 21.7 %all_to_all.20 = bf16[8,16,2304]{2,1,0:T(8,128)(2,1)S(1)} all-to-all(bf16[8,16,2304]{2,1,0:T(8,128)(2,1)S(1)} %bitcast.53), channel_id=1, replica_groups=mesh['dp'=16,'mp'=8,'expert'=4] {'mp'}, dimensions={0} | all-to-all | bytes 1179648 | tf_op jit(solution)/shard_map/all_to_all | solution.py:159
  64.7 3.4 %collective-permute-start.1 = (bf16[128,2304]{1,0:T(8,128)(2,1)S(1)}, bf16[128,2304]{1,0:T(8,128)(2,1)S(1)}, u32[]{:S(2)}, u32[]{:S(2)}) collective-permute-start(bf16[128,2304]{1,0:T(8,128)(2,1)S(1)} %bitcast.41), channel_id=1, source_target_pairs={{0,1},{1,2},{2,3},{3,0},{4,5},{5,6},{6,7},{7,4},{8,9},{9,10},{10,1... | collective-permute-start | bytes 1769480 | tf_op jit(solution)/shard_map/ppermute | solution.py:115
  68.1 3.7 %collective-permute-start.2 = (bf16[128,2304]{1,0:T(8,128)(2,1)S(1)}, bf16[128,2304]{1,0:T(8,128)(2,1)S(1)}, u32[]{:S(2)}, u32[]{:S(2)}) collective-permute-start(bf16[128,2304]{1,0:T(8,128)(2,1)S(1)} %bitcast.42), channel_id=1, source_target_pairs={{0,3},{1,0},{2,1},{3,2},{4,7},{5,4},{6,5},{7,6},{8,11},{9,8},{10,9... | collective-permute-start | bytes 1769480 | tf_op jit(solution)/shard_map/ppermute | solution.py:115
  71.8 0.0 copy-done.1
  71.8 5.1 %shard_map.91 = (bf16[2304,1024]{1,0:T(8,128)(2,1)S(1)}, bf16[2304,1024]{1,0:T(8,128)(2,1)S(1)}, bf16[1024,2304]{1,0:T(8,128)(2,1)S(1)}) custom-call(bf16[2304,1024]{1,0:T(8,128)(2,1)} %bitcast.47, bf16[2304,1024]{1,0:T(8,128)(2,1)} %bitcast.48, bf16[1024,2304]{1,0:T(8,128)(2,1)} %bitcast.49), custom_call_target="tpu_custom_call" | custom-call | bytes 28311552 | tf_op jit(solution)/shard_map/pallas_call | solution.py:35
  77.0 2.1 %shard_map.92 = bf16[128,2304]{1,0:T(8,128)(2,1)S(1)} custom-call(bf16[128,2304]{1,0:T(8,128)(2,1)S(1)} %bitcast.43, bf16[2304,1024]{1,0:T(8,128)(2,1)S(1)} %get-tuple-element.26.refs_1_.refs_2_, bf16[2304,1024]{1,0:T(8,128)(2,1)S(1)} %get-tuple-element.27.refs_2_.refs_3_, bf16[1024,2304]{1,0:T(8,128)(2,1)S(1)} %get-tuple-element.28.refs_3_.refs_4_), custom_call_target="tpu_custom_call" | custom-call | flops 1811939328 | bytes 15335424 | tf_op jit(solution)/shard_map/pallas_call | solution.py:83
  79.1 3.3 %collective-permute-done.1.refs_0_ = bf16[128,2304]{1,0:T(8,128)(2,1)S(1)} collective-permute-done((bf16[128,2304]{1,0:T(8,128)(2,1)S(1)}, bf16[128,2304]{1,0:T(8,128)(2,1)S(1)}, u32[]{:S(2)}, u32[]{:S(2)}) %collective-permute-start.1) | collective-permute-done | bytes 589856 | tf_op jit(solution)/shard_map/ppermute | solution.py:115
  82.4 1.9 %collective-permute-done.2.refs_1_ = bf16[128,2304]{1,0:T(8,128)(2,1)S(1)} collective-permute-done((bf16[128,2304]{1,0:T(8,128)(2,1)S(1)}, bf16[128,2304]{1,0:T(8,128)(2,1)S(1)}, u32[]{:S(2)}, u32[]{:S(2)}) %collective-permute-start.2) | collective-permute-done | bytes 589856 | tf_op jit(solution)/shard_map/ppermute | solution.py:115
  84.3 4.6 %collective-permute-start.5 = (bf16[128,2304]{1,0:T(8,128)(2,1)S(1)}, bf16[128,2304]{1,0:T(8,128)(2,1)S(1)}, u32[]{:S(2)}, u32[]{:S(2)}) collective-permute-start(bf16[128,2304]{1,0:T(8,128)(2,1)S(1)} %bitcast.44), channel_id=1, source_target_pairs={{0,2},{1,3},{2,0},{3,1},{4,6},{5,7},{6,4},{7,5},{8,10},{9,11},{10,... | collective-permute-start | bytes 1769480 | tf_op jit(solution)/shard_map/ppermute | solution.py:115
  89.0 4.0 %shard_map.93 = (bf16[128,2304]{1,0:T(8,128)(2,1)S(1)}, bf16[128,2304]{1,0:T(8,128)(2,1)S(1)}) custom-call(bf16[128,2304]{1,0:T(8,128)(2,1)S(1)} %collective-permute-done.1.refs_0_, bf16[128,2304]{1,0:T(8,128)(2,1)S(1)} %collective-permute-done.2.refs_1_, bf16[2304,1024]{1,0:T(8,128)(2,1)S(1)} %get-tuple-element.26.refs_1_.refs_2_, ...), custom_call_target="tpu_custom_call" | custom-call | flops 3623878656 | bytes 16515072 | tf_op jit(solution)/shard_map/pallas_call | solution.py:83
  92.9 3.3 %collective-permute-start.3 = (bf16[128,2304]{1,0:T(8,128)(2,1)S(1)}, bf16[128,2304]{1,0:T(8,128)(2,1)}, u32[]{:S(2)}, u32[]{:S(2)}) collective-permute-start(bf16[128,2304]{1,0:T(8,128)(2,1)S(1)} %get-tuple-element.32), channel_id=1, source_target_pairs={{0,3},{1,0},{2,1},{3,2},{4,7},{5,4},{6,5},{7,6},{8,11},{9,8},{10,9... | collective-permute-start | bytes 1769480 | tf_op jit(solution)/shard_map/ppermute | solution.py:115
  96.3 2.5 %collective-permute-start.4 = (bf16[128,2304]{1,0:T(8,128)(2,1)S(1)}, bf16[128,2304]{1,0:T(8,128)(2,1)}, u32[]{:S(2)}, u32[]{:S(2)}) collective-permute-start(bf16[128,2304]{1,0:T(8,128)(2,1)S(1)} %get-tuple-element.33), channel_id=1, source_target_pairs={{0,1},{1,2},{2,3},{3,0},{4,5},{5,6},{6,7},{7,4},{8,9},{9,10},{10,1... | collective-permute-start | bytes 1769480 | tf_op jit(solution)/shard_map/ppermute | solution.py:115
  98.8 5.0 %collective-permute-done.5.refs_0_ = bf16[128,2304]{1,0:T(8,128)(2,1)S(1)} collective-permute-done((bf16[128,2304]{1,0:T(8,128)(2,1)S(1)}, bf16[128,2304]{1,0:T(8,128)(2,1)S(1)}, u32[]{:S(2)}, u32[]{:S(2)}) %collective-permute-start.5) | collective-permute-done | bytes 589856 | tf_op jit(solution)/shard_map/ppermute | solution.py:115
  103.8 2.8 %shard_map.94 = (bf16[64,2304]{1,0:T(8,128)(2,1)S(1)}, bf16[64,2304]{1,0:T(8,128)(2,1)}) custom-call(bf16[128,2304]{1,0:T(8,128)(2,1)S(1)} %collective-permute-done.5.refs_0_, bf16[2304,1024]{1,0:T(8,128)(2,1)S(1)} %get-tuple-element.26.refs_1_.refs_2_, bf16[2304,1024]{1,0:T(8,128)(2,1)S(1)} %get-tuple-element.27.refs_2_.refs_3_, ...), custom_call_target="tpu_custom_call" | custom-call | flops 1811939328 | bytes 15335424 | tf_op jit(solution)/shard_map/pallas_call | solution.py:83
  106.6 4.8 %collective-permute-start.6 = (bf16[64,2304]{1,0:T(8,128)(2,1)S(1)}, bf16[64,2304]{1,0:T(8,128)(2,1)}, u32[]{:S(2)}, u32[]{:S(2)}) collective-permute-start(bf16[64,2304]{1,0:T(8,128)(2,1)S(1)} %get-tuple-element.37), channel_id=1, source_target_pairs={{0,2},{1,3},{2,0},{3,1},{4,6},{5,7},{6,4},{7,5},{8,10},{9,11},{10,... | collective-permute-start | bytes 884744 | tf_op jit(solution)/shard_map/ppermute | solution.py:115
  111.5 4.1 %all-to-all-start.2 = ((bf16[8,8,2304]{2,1,0:T(8,128)(2,1)}), bf16[8,8,2304]{2,1,0:T(8,128)(2,1)}, u32[]{:S(2)}, u32[]{:S(2)}) async-start(bf16[8,8,2304]{2,1,0:T(8,128)(2,1)} %bitcast.14), calls=%async_computation.2 | async-start | bytes 589824 | tf_op jit(solution)/shard_map/all_to_all | solution.py:177
  115.5 1.5 %collective-permute-done.3 = bf16[128,2304]{1,0:T(8,128)(2,1)} collective-permute-done((bf16[128,2304]{1,0:T(8,128)(2,1)S(1)}, bf16[128,2304]{1,0:T(8,128)(2,1)}, u32[]{:S(2)}, u32[]{:S(2)}) %collective-permute-start.3) | collective-permute-done | bytes 589856 | tf_op jit(solution)/shard_map/ppermute | solution.py:115
  117.1 3.7 %collective-permute-done.4 = bf16[128,2304]{1,0:T(8,128)(2,1)} collective-permute-done((bf16[128,2304]{1,0:T(8,128)(2,1)S(1)}, bf16[128,2304]{1,0:T(8,128)(2,1)}, u32[]{:S(2)}, u32[]{:S(2)}) %collective-permute-start.4) | collective-permute-done | bytes 589856 | tf_op jit(solution)/shard_map/ppermute | solution.py:115
  120.7 1.4 convert_add_fusion
  122.2 0.0 collective-permute-done.6
  122.2 4.1 %all-to-all-done.2 = bf16[8,8,2304]{2,1,0:T(8,128)(2,1)} async-done(((bf16[8,8,2304]{2,1,0:T(8,128)(2,1)}), bf16[8,8,2304]{2,1,0:T(8,128)(2,1)}, u32[]{:S(2)}, u32[]{:S(2)}) %all-to-all-start.2) | async-done | bytes 294944 | tf_op jit(solution)/shard_map/all_to_all | solution.py:177
  126.4 1.0 fusion.4
  127.4 0.9 pad_maximum_fusion
  128.2 3.5 %all-to-all-start.3 = ((bf16[8,16,2304]{2,1,0:T(8,128)(2,1)}), bf16[8,16,2304]{2,1,0:T(8,128)(2,1)S(1)}, u32[]{:S(2)}, u32[]{:S(2)}) async-start(bf16[8,16,2304]{2,1,0:T(8,128)(2,1)} %pad_maximum_fusion), calls=%async_computation.3 | async-start | bytes 1179648 | tf_op jit(solution)/shard_map/all_to_all | solution.py:187
  131.8 0.0 copy-start.2
  131.8 1.2 convolution_multiply_fusion.3
  133.0 1.1 fusion.3
  134.1 2.5 %collective-permute-start.7 = (f32[32,2304]{1,0:T(8,128)S(1)}, f32[32,2304]{1,0:T(8,128)S(1)}, u32[]{:S(2)}, u32[]{:S(2)}) collective-permute-start(f32[32,2304]{1,0:T(8,128)S(1)} %fusion.3), channel_id=1, source_target_pairs={{0,2},{1,3},{2,0},{3,1},{4,6},{5,7},{6,4},{7,5},{8,10},{9,11},{10,... | collective-permute-start | bytes 884744 | tf_op jit(solution)/shard_map/ppermute | solution.py:115
  136.7 9.0 %all-to-all-done.3 = bf16[8,16,2304]{2,1,0:T(8,128)(2,1)S(1)} async-done(((bf16[8,16,2304]{2,1,0:T(8,128)(2,1)}), bf16[8,16,2304]{2,1,0:T(8,128)(2,1)S(1)}, u32[]{:S(2)}, u32[]{:S(2)}) %all-to-all-start.3) | async-done | bytes 589856 | tf_op jit(solution)/shard_map/all_to_all | solution.py:187
  145.7 0.3 convolution_multiply_fusion
  146.0 0.0 collective-permute-done.7
  146.0 0.0 copy-done.2
  146.0 1.0 fusion.2
  (11 shorter events, 0.1 us)
Async XLA Ops:
  0.0 1.6 %copy-start = (bf16[288,2304]{1,0:T(8,128)(2,1)S(1)}, bf16[288,2304]{1,0:T(8,128)(2,1)}, u32[]{:S(2)}) copy-start(bf16[288,2304]{1,0:T(8,128)(2,1)} %param.11) | copy-start | bytes 3981316
  3.4 7.2 %copy-start.5 = (s32[32,2]{0,1:T(2,128)S(1)}, s32[32,2]{0,1:T(2,128)}, u32[]{:S(2)}) copy-start(s32[32,2]{0,1:T(2,128)} %param.16) | copy-start | bytes 772
  3.4 8.0 %copy-start.6 = (f32[32,2]{0,1:T(2,128)S(1)}, f32[32,2]{0,1:T(2,128)}, u32[]{:S(2)}) copy-start(f32[32,2]{0,1:T(2,128)} %param.17) | copy-start | bytes 772
  3.4 38.8 %all-to-all-start = ((f16[8,32,2304]{2,1,0:T(8,128)(2,1)}), f16[8,32,2304]{2,1,0:T(8,128)(2,1)S(1)}, u32[]{:S(2)}, u32[]{:S(2)}) async-start(f16[8,32,2304]{2,1,0:T(8,128)(2,1)} %bitcast.50), calls=%async_computation | async-start | bytes 2359296 | tf_op jit(solution)/shard_map/all_to_all | solution.py:143
  10.6 31.7 %copy-start.3 = (f32[32,2304]{1,0:T(8,128)S(1)}, f32[32,2304]{1,0:T(8,128)}, u32[]{:S(2)}) copy-start(f32[32,2304]{1,0:T(8,128)} %param.10) | copy-start | bytes 884740
  11.4 7.0 %collective-permute-start = (f32[32,4]{0,1:T(4,128)S(1)}, f32[32,4]{0,1:T(4,128)S(1)}, u32[]{:S(2)}, u32[]{:S(2)}) collective-permute-start(f32[32,4]{0,1:T(4,128)S(1)} %pad_maximum_fusion.1), channel_id=1, source_target_pairs={{0,2},{1,3},{2,0},{3,1},{4,6},{5,7},{6,4},{7,5},{8,10},{9,11},{10,... | collective-permute-start | bytes 1544 | tf_op jit(solution)/shard_map/ppermute | solution.py:115
  18.5 24.1 %copy-start.4 = (f32[2304]{0:T(1024)S(1)}, f32[2304]{0:T(1024)}, u32[]{:S(2)}) copy-start(f32[2304]{0:T(1024)} %param.12) | copy-start | bytes 27652
  42.5 29.3 %copy-start.1 = (f32[32,2304]{1,0:T(8,128)}, f32[32,2304]{1,0:T(8,128)S(1)}, u32[]{:S(2)}) copy-start(f32[32,2304]{1,0:T(8,128)S(1)} %get-tuple-element.46) | copy-start | bytes 884740
  64.7 17.7 %collective-permute-start.1 = (bf16[128,2304]{1,0:T(8,128)(2,1)S(1)}, bf16[128,2304]{1,0:T(8,128)(2,1)S(1)}, u32[]{:S(2)}, u32[]{:S(2)}) collective-permute-start(bf16[128,2304]{1,0:T(8,128)(2,1)S(1)} %bitcast.41), channel_id=1, source_target_pairs={{0,1},{1,2},{2,3},{3,0},{4,5},{5,6},{6,7},{7,4},{8,9},{9,10},{10,1... | collective-permute-start | bytes 1769480 | tf_op jit(solution)/shard_map/ppermute | solution.py:115
  68.1 16.2 %collective-permute-start.2 = (bf16[128,2304]{1,0:T(8,128)(2,1)S(1)}, bf16[128,2304]{1,0:T(8,128)(2,1)S(1)}, u32[]{:S(2)}, u32[]{:S(2)}) collective-permute-start(bf16[128,2304]{1,0:T(8,128)(2,1)S(1)} %bitcast.42), channel_id=1, source_target_pairs={{0,3},{1,0},{2,1},{3,2},{4,7},{5,4},{6,5},{7,6},{8,11},{9,8},{10,9... | collective-permute-start | bytes 1769480 | tf_op jit(solution)/shard_map/ppermute | solution.py:115
  84.3 19.4 %collective-permute-start.5 = (bf16[128,2304]{1,0:T(8,128)(2,1)S(1)}, bf16[128,2304]{1,0:T(8,128)(2,1)S(1)}, u32[]{:S(2)}, u32[]{:S(2)}) collective-permute-start(bf16[128,2304]{1,0:T(8,128)(2,1)S(1)} %bitcast.44), channel_id=1, source_target_pairs={{0,2},{1,3},{2,0},{3,1},{4,6},{5,7},{6,4},{7,5},{8,10},{9,11},{10,... | collective-permute-start | bytes 1769480 | tf_op jit(solution)/shard_map/ppermute | solution.py:115
  92.9 24.1 %collective-permute-start.3 = (bf16[128,2304]{1,0:T(8,128)(2,1)S(1)}, bf16[128,2304]{1,0:T(8,128)(2,1)}, u32[]{:S(2)}, u32[]{:S(2)}) collective-permute-start(bf16[128,2304]{1,0:T(8,128)(2,1)S(1)} %get-tuple-element.32), channel_id=1, source_target_pairs={{0,3},{1,0},{2,1},{3,2},{4,7},{5,4},{6,5},{7,6},{8,11},{9,8},{10,9... | collective-permute-start | bytes 1769480 | tf_op jit(solution)/shard_map/ppermute | solution.py:115
  96.3 24.4 %collective-permute-start.4 = (bf16[128,2304]{1,0:T(8,128)(2,1)S(1)}, bf16[128,2304]{1,0:T(8,128)(2,1)}, u32[]{:S(2)}, u32[]{:S(2)}) collective-permute-start(bf16[128,2304]{1,0:T(8,128)(2,1)S(1)} %get-tuple-element.33), channel_id=1, source_target_pairs={{0,1},{1,2},{2,3},{3,0},{4,5},{5,6},{6,7},{7,4},{8,9},{9,10},{10,1... | collective-permute-start | bytes 1769480 | tf_op jit(solution)/shard_map/ppermute | solution.py:115
  106.6 15.6 %collective-permute-start.6 = (bf16[64,2304]{1,0:T(8,128)(2,1)S(1)}, bf16[64,2304]{1,0:T(8,128)(2,1)}, u32[]{:S(2)}, u32[]{:S(2)}) collective-permute-start(bf16[64,2304]{1,0:T(8,128)(2,1)S(1)} %get-tuple-element.37), channel_id=1, source_target_pairs={{0,2},{1,3},{2,0},{3,1},{4,6},{5,7},{6,4},{7,5},{8,10},{9,11},{10,... | collective-permute-start | bytes 884744 | tf_op jit(solution)/shard_map/ppermute | solution.py:115
  111.5 14.9 %all-to-all-start.2 = ((bf16[8,8,2304]{2,1,0:T(8,128)(2,1)}), bf16[8,8,2304]{2,1,0:T(8,128)(2,1)}, u32[]{:S(2)}, u32[]{:S(2)}) async-start(bf16[8,8,2304]{2,1,0:T(8,128)(2,1)} %bitcast.14), calls=%async_computation.2 | async-start | bytes 589824 | tf_op jit(solution)/shard_map/all_to_all | solution.py:177
  128.2 17.4 %all-to-all-start.3 = ((bf16[8,16,2304]{2,1,0:T(8,128)(2,1)}), bf16[8,16,2304]{2,1,0:T(8,128)(2,1)S(1)}, u32[]{:S(2)}, u32[]{:S(2)}) async-start(bf16[8,16,2304]{2,1,0:T(8,128)(2,1)} %pad_maximum_fusion), calls=%async_computation.3 | async-start | bytes 1179648 | tf_op jit(solution)/shard_map/all_to_all | solution.py:187
  131.8 14.2 %copy-start.2 = (f32[32,2304]{1,0:T(8,128)S(1)}, f32[32,2304]{1,0:T(8,128)}, u32[]{:S(2)}) copy-start(f32[32,2304]{1,0:T(8,128)} %copy-done.1) | copy-start | bytes 884740
  134.1 11.8 %collective-permute-start.7 = (f32[32,2304]{1,0:T(8,128)S(1)}, f32[32,2304]{1,0:T(8,128)S(1)}, u32[]{:S(2)}, u32[]{:S(2)}) collective-permute-start(f32[32,2304]{1,0:T(8,128)S(1)} %fusion.3), channel_id=1, source_target_pairs={{0,2},{1,3},{2,0},{3,1},{4,6},{5,7},{6,4},{7,5},{8,10},{9,11},{10,... | collective-permute-start | bytes 884744 | tf_op jit(solution)/shard_map/ppermute | solution.py:115

commit v10 on v5

--- a/solution.py
+++ b/solution.py
@@ -141,7 +141,10 @@
     before_rows = shift(own, 1)
     after_rows = shift(own, -1)
     (own_sum,) = ffn([own], *weights)
-    far_rows = shift(lax.optimization_barrier((own, own_sum))[0], 2)
+    later, before_rows, after_rows, own_sum = lax.optimization_barrier(
+        (own, before_rows, after_rows, own_sum)
+    )
+    far_rows = shift(later, 2)
     before_sum, after_sum = ffn([before_rows, after_rows], *weights)
     back_after = shift(before_sum, -1)
     back_before = shift(after_sum, 1)

time: 147 us -> 150 us (1.020); the launches traced: 144 us -> 149 us
  waiting for transfers between devices: 68.5 us -> 73.1 us
    ppermute x6, waiting for transfers between devices: 23.8 us -> 26.4 us  [shift(): lax.ppermute(value, 'expert', [(i, (i + by) % unit_parts) for i in range(...]
    all_to_all x1, waiting for transfers between devices: 13.9 us -> 15.9 us  [body(): lax.all_to_all(outputs, 'mp', split_axis=0, concat_axis=0, tiled=True)]
  transfers between devices with their start and end apart: 8 -> 8, of which waited for: 5 -> 7; matrix products, arithmetic and copies ran while one was open for 1% -> 1% of each run, Pallas kernels for 9% -> 9%
where the time goes in v10:
time: 150 us; the launch traced here: 149 us
  waiting for transfers between devices  73.1 us (49%)
  starting transfers between devices  33.3 us (22%)
  blocking collectives  21.7 us (14%)
  Pallas kernels  13.4 us (9%)
  matrix products  3.49 us (2%)
  local copies, waits for them, and re-layouts  1.96 us (1%)
  other arithmetic  1.79 us (1%)
    all_to_all x1, waiting for transfers between devices, body(): parts = lax.all_to_all(parts, 'mp', split_axis=0, concat_axis=0, tiled=True)  30.8 us
    ppermute x6, waiting for transfers between devices, shift(): lax.ppermute(value, 'expert', [(i, (i + by) % unit_parts) for i in range(...  26.4 us
    ppermute x6, starting transfers between devices, shift(): lax.ppermute(value, 'expert', [(i, (i + by) % unit_parts) for i in range(...  22.4 us
    all_to_all x1, blocking collectives, body(): lax.all_to_all(outgoing, 'mp', split_axis=0, concat_axis=0, tiled=True)  21.7 us
    all_to_all x1, waiting for transfers between devices, body(): lax.all_to_all(outputs, 'mp', split_axis=0, concat_axis=0, tiled=True)  15.9 us
    pallas_call x3, Pallas kernels, ffn(): pl.pallas_call(functools.partial(ffn_kernel, count), out_shape=[jax.Shape...  8.24 us
    all_to_all x1, starting transfers between devices, body(): parts = lax.all_to_all(parts, 'mp', split_axis=0, concat_axis=0, tiled=True)  7.23 us
    pallas_call x1, Pallas kernels, load(): pl.pallas_call(load_kernel, out_shape=[pltpu.VMEM(w.shape, w.dtype) for w...  5.15 us
  transfers between devices with their start and end apart: 8, of which 7 were waited for; matrix products, arithmetic and copies ran while one was open for 1% of the time, Pallas kernels for 9%

profile of v10, /device:TPU:448, one launch (start us, length us, event | category | flops | bytes accessed | tf_op | source)
XLA Modules:
  0.0 148.9 jit_solution(5474640947210239613)
XLA Ops:
  0.0 0.0 copy-start
  0.0 1.5 %copy.17 = bf16[1024,288]{1,0:T(8,128)(2,1)S(1)} copy(bf16[1024,288]{0,1:T(8,128)(2,1)} %param.9) | data formatting | bytes 1179648 | tf_op args[0]
  1.6 0.0 copy-done
  1.6 1.8 %convolution_convert_fusion = f16[256,2304]{1,0:T(8,128)(2,1)} fusion(bf16[256,288]{1,0:T(8,128)(2,1)S(1)} %bitcast.34, bf16[288,2304]{1,0:T(8,128)(2,1)S(1)} %copy-done), kind=kOutput, calls=%fused_computation | convolution fusion | flops 340328448 | bytes 2654208 | tf_op jit(solution)/shard_map/dot_general | solution.py:110
  3.4 0.0 copy-start.3
  3.4 7.2 %all-to-all-start = ((f16[8,32,2304]{2,1,0:T(8,128)(2,1)}), f16[8,32,2304]{2,1,0:T(8,128)(2,1)S(1)}, u32[]{:S(2)}, u32[]{:S(2)}) async-start(f16[8,32,2304]{2,1,0:T(8,128)(2,1)} %bitcast.31), calls=%async_computation | async-start | bytes 2359296 | tf_op jit(solution)/shard_map/all_to_all | solution.py:112
  10.6 0.0 copy-done.3
  10.6 0.0 copy-start.1
  10.6 0.1 copy.18
  10.7 0.1 eq.45
  10.8 0.1 fusion.4
  10.9 0.1 reduce_window_sum.11
  11.0 0.2 select_reduce_fusion
  11.2 0.1 reduce_sum.31
  11.3 0.1 copy.19
  11.4 0.0 copy-start.2
  11.4 30.8 %all-to-all-done = f16[8,32,2304]{2,1,0:T(8,128)(2,1)S(1)} async-done(((f16[8,32,2304]{2,1,0:T(8,128)(2,1)}), f16[8,32,2304]{2,1,0:T(8,128)(2,1)S(1)}, u32[]{:S(2)}, u32[]{:S(2)}) %all-to-all-start) | async-done | bytes 1179680 | tf_op jit(solution)/shard_map/all_to_all | solution.py:112
  42.2 0.2 convert_reduce_fusion
  42.4 0.0 copy-done.1
  42.4 0.1 multiply_reduce_fusion
  42.5 0.0 copy-done.2
  42.5 0.4 convolution_convert_fusion.1
  43.0 21.7 %all_to_all.15 = bf16[8,16,2304]{2,1,0:T(8,128)(2,1)S(1)} all-to-all(bf16[8,16,2304]{2,1,0:T(8,128)(2,1)S(1)} %bitcast.32), channel_id=1, replica_groups=mesh['dp'=16,'mp'=8,'expert'=4] {'mp'}, dimensions={0} | all-to-all | bytes 1179648 | tf_op jit(solution)/shard_map/all_to_all | solution.py:131
  64.7 3.4 %collective-permute-start = (bf16[128,2304]{1,0:T(8,128)(2,1)S(1)}, bf16[128,2304]{1,0:T(8,128)(2,1)S(1)}, u32[]{:S(2)}, u32[]{:S(2)}) collective-permute-start(bf16[128,2304]{1,0:T(8,128)(2,1)S(1)} %bitcast.22), channel_id=1, source_target_pairs={{0,1},{1,2},{2,3},{3,0},{4,5},{5,6},{6,7},{7,4},{8,9},{9,10},{10,1... | collective-permute-start | bytes 1769480 | tf_op jit(solution)/shard_map/ppermute | solution.py:137
  68.1 3.7 %collective-permute-start.1 = (bf16[128,2304]{1,0:T(8,128)(2,1)S(1)}, bf16[128,2304]{1,0:T(8,128)(2,1)S(1)}, u32[]{:S(2)}, u32[]{:S(2)}) collective-permute-start(bf16[128,2304]{1,0:T(8,128)(2,1)S(1)} %bitcast.23), channel_id=1, source_target_pairs={{0,3},{1,0},{2,1},{3,2},{4,7},{5,4},{6,5},{7,6},{8,11},{9,8},{10,9... | collective-permute-start | bytes 1769480 | tf_op jit(solution)/shard_map/ppermute | solution.py:137
  71.8 5.1 %shard_map.91 = (bf16[2304,1024]{1,0:T(8,128)(2,1)S(1)}, bf16[2304,1024]{1,0:T(8,128)(2,1)S(1)}, bf16[1024,2304]{1,0:T(8,128)(2,1)S(1)}) custom-call(bf16[2304,1024]{1,0:T(8,128)(2,1)} %bitcast.28, bf16[2304,1024]{1,0:T(8,128)(2,1)} %bitcast.29, bf16[1024,2304]{1,0:T(8,128)(2,1)} %bitcast.30), custom_call_target="tpu_custom_call" | custom-call | bytes 28311552 | tf_op jit(solution)/shard_map/pallas_call | solution.py:34
  76.9 2.1 %shard_map.92 = bf16[128,2304]{1,0:T(8,128)(2,1)S(1)} custom-call(bf16[128,2304]{1,0:T(8,128)(2,1)S(1)} %bitcast.24, bf16[2304,1024]{1,0:T(8,128)(2,1)S(1)} %get-tuple-element.15.refs_1_.refs_2_, bf16[2304,1024]{1,0:T(8,128)(2,1)S(1)} %get-tuple-element.16.refs_2_.refs_3_, bf16[1024,2304]{1,0:T(8,128)(2,1)S(1)} %get-tuple-element.17.refs_3_.refs_4_), custom_call_target="tpu_custom_call" | custom-call | flops 1811939328 | bytes 15335424 | tf_op jit(solution)/shard_map/pallas_call | solution.py:77
  79.1 3.3 %collective-permute-done.refs_0_ = bf16[128,2304]{1,0:T(8,128)(2,1)S(1)} collective-permute-done((bf16[128,2304]{1,0:T(8,128)(2,1)S(1)}, bf16[128,2304]{1,0:T(8,128)(2,1)S(1)}, u32[]{:S(2)}, u32[]{:S(2)}) %collective-permute-start) | collective-permute-done | bytes 589856 | tf_op jit(solution)/shard_map/ppermute | solution.py:137
  82.4 1.9 %collective-permute-done.1.refs_1_ = bf16[128,2304]{1,0:T(8,128)(2,1)S(1)} collective-permute-done((bf16[128,2304]{1,0:T(8,128)(2,1)S(1)}, bf16[128,2304]{1,0:T(8,128)(2,1)S(1)}, u32[]{:S(2)}, u32[]{:S(2)}) %collective-permute-start.1) | collective-permute-done | bytes 589856 | tf_op jit(solution)/shard_map/ppermute | solution.py:137
  84.3 4.6 %collective-permute-start.4 = (bf16[128,2304]{1,0:T(8,128)(2,1)S(1)}, bf16[128,2304]{1,0:T(8,128)(2,1)S(1)}, u32[]{:S(2)}, u32[]{:S(2)}) collective-permute-start(bf16[128,2304]{1,0:T(8,128)(2,1)S(1)} %bitcast.25), channel_id=1, source_target_pairs={{0,2},{1,3},{2,0},{3,1},{4,6},{5,7},{6,4},{7,5},{8,10},{9,11},{10,... | collective-permute-start | bytes 1769480 | tf_op jit(solution)/shard_map/ppermute | solution.py:137
  88.9 4.0 %shard_map.93 = (bf16[128,2304]{1,0:T(8,128)(2,1)S(1)}, bf16[128,2304]{1,0:T(8,128)(2,1)S(1)}) custom-call(bf16[128,2304]{1,0:T(8,128)(2,1)S(1)} %collective-permute-done.refs_0_, bf16[128,2304]{1,0:T(8,128)(2,1)S(1)} %collective-permute-done.1.refs_1_, bf16[2304,1024]{1,0:T(8,128)(2,1)S(1)} %get-tuple-element.15.refs_1_.refs_2_, ...), custom_call_target="tpu_custom_call" | custom-call | flops 3623878656 | bytes 16515072 | tf_op jit(solution)/shard_map/pallas_call | solution.py:77
  92.9 3.3 %collective-permute-start.2 = (bf16[128,2304]{1,0:T(8,128)(2,1)S(1)}, bf16[128,2304]{1,0:T(8,128)(2,1)S(1)}, u32[]{:S(2)}, u32[]{:S(2)}) collective-permute-start(bf16[128,2304]{1,0:T(8,128)(2,1)S(1)} %get-tuple-element.21), channel_id=1, source_target_pairs={{0,3},{1,0},{2,1},{3,2},{4,7},{5,4},{6,5},{7,6},{8,11},{9,8},{10,9... | collective-permute-start | bytes 1769480 | tf_op jit(solution)/shard_map/ppermute | solution.py:137
  96.3 2.5 %collective-permute-start.3 = (bf16[128,2304]{1,0:T(8,128)(2,1)S(1)}, bf16[128,2304]{1,0:T(8,128)(2,1)S(1)}, u32[]{:S(2)}, u32[]{:S(2)}) collective-permute-start(bf16[128,2304]{1,0:T(8,128)(2,1)S(1)} %get-tuple-element.22), channel_id=1, source_target_pairs={{0,1},{1,2},{2,3},{3,0},{4,5},{5,6},{6,7},{7,4},{8,9},{9,10},{10,1... | collective-permute-start | bytes 1769480 | tf_op jit(solution)/shard_map/ppermute | solution.py:137
  98.8 5.0 %collective-permute-done.4.refs_0_ = bf16[128,2304]{1,0:T(8,128)(2,1)S(1)} collective-permute-done((bf16[128,2304]{1,0:T(8,128)(2,1)S(1)}, bf16[128,2304]{1,0:T(8,128)(2,1)S(1)}, u32[]{:S(2)}, u32[]{:S(2)}) %collective-permute-start.4) | collective-permute-done | bytes 589856 | tf_op jit(solution)/shard_map/ppermute | solution.py:137
  103.7 2.1 %shard_map.94 = bf16[128,2304]{1,0:T(8,128)(2,1)S(1)} custom-call(bf16[128,2304]{1,0:T(8,128)(2,1)S(1)} %collective-permute-done.4.refs_0_, bf16[2304,1024]{1,0:T(8,128)(2,1)S(1)} %get-tuple-element.15.refs_1_.refs_2_, bf16[2304,1024]{1,0:T(8,128)(2,1)S(1)} %get-tuple-element.16.refs_2_.refs_3_, bf16[1024,2304]{1,0:T(8,128)(2,1)S(1)} %get-tuple-element.17.refs_3_.refs_4_), custom_call_target="tpu_custom_call" | custom-call | flops 1811939328 | bytes 15335424 | tf_op jit(solution)/shard_map/pallas_call | solution.py:77
  105.9 4.9 %collective-permute-start.5 = (bf16[128,2304]{1,0:T(8,128)(2,1)S(1)}, bf16[128,2304]{1,0:T(8,128)(2,1)S(1)}, u32[]{:S(2)}, u32[]{:S(2)}) collective-permute-start(bf16[128,2304]{1,0:T(8,128)(2,1)S(1)} %shard_map.94), channel_id=1, source_target_pairs={{0,2},{1,3},{2,0},{3,1},{4,6},{5,7},{6,4},{7,5},{8,10},{9,11},{10,... | collective-permute-start | bytes 1769480 | tf_op jit(solution)/shard_map/ppermute | solution.py:137
  110.7 6.2 %collective-permute-done.2 = bf16[128,2304]{1,0:T(8,128)(2,1)S(1)} collective-permute-done((bf16[128,2304]{1,0:T(8,128)(2,1)S(1)}, bf16[128,2304]{1,0:T(8,128)(2,1)S(1)}, u32[]{:S(2)}, u32[]{:S(2)}) %collective-permute-start.2) | collective-permute-done | bytes 589856 | tf_op jit(solution)/shard_map/ppermute | solution.py:137
  116.9 10.0 %collective-permute-done.3 = bf16[128,2304]{1,0:T(8,128)(2,1)S(1)} collective-permute-done((bf16[128,2304]{1,0:T(8,128)(2,1)S(1)}, bf16[128,2304]{1,0:T(8,128)(2,1)S(1)}, u32[]{:S(2)}, u32[]{:S(2)}) %collective-permute-start.3) | collective-permute-done | bytes 589856 | tf_op jit(solution)/shard_map/ppermute | solution.py:137
  126.9 0.2 convert_add_fusion
  127.1 0.0 collective-permute-done.5
  127.1 0.9 add_convert_fusion
  128.1 0.0 copy-start.4
  128.1 3.7 %all-to-all-start.2 = ((bf16[8,16,2304]{2,1,0:T(8,128)(2,1)}), bf16[8,16,2304]{2,1,0:T(8,128)(2,1)S(1)}, u32[]{:S(2)}, u32[]{:S(2)}) async-start(bf16[8,16,2304]{2,1,0:T(8,128)(2,1)} %bitcast.11), calls=%async_computation.2 | async-start | bytes 1179648 | tf_op jit(solution)/shard_map/all_to_all | solution.py:158
  131.7 0.0 copy-done.4
  131.8 15.9 %all-to-all-done.2 = bf16[8,16,2304]{2,1,0:T(8,128)(2,1)S(1)} async-done(((bf16[8,16,2304]{2,1,0:T(8,128)(2,1)}), bf16[8,16,2304]{2,1,0:T(8,128)(2,1)S(1)}, u32[]{:S(2)}, u32[]{:S(2)}) %all-to-all-start.2) | async-done | bytes 589856 | tf_op jit(solution)/shard_map/all_to_all | solution.py:158
  147.7 0.3 convolution_multiply_fusion
  148.0 1.0 fusion.1
  (5 shorter events, 0.1 us)
Async XLA Ops:
  0.0 1.6 %copy-start = (bf16[288,2304]{1,0:T(8,128)(2,1)S(1)}, bf16[288,2304]{1,0:T(8,128)(2,1)}, u32[]{:S(2)}) copy-start(bf16[288,2304]{1,0:T(8,128)(2,1)} %param.11) | copy-start | bytes 3981316
  3.4 7.2 %copy-start.3 = (s32[32,2]{0,1:T(2,128)S(1)}, s32[32,2]{0,1:T(2,128)}, u32[]{:S(2)}) copy-start(s32[32,2]{0,1:T(2,128)} %param.16) | copy-start | bytes 772
  3.4 38.8 %all-to-all-start = ((f16[8,32,2304]{2,1,0:T(8,128)(2,1)}), f16[8,32,2304]{2,1,0:T(8,128)(2,1)S(1)}, u32[]{:S(2)}, u32[]{:S(2)}) async-start(f16[8,32,2304]{2,1,0:T(8,128)(2,1)} %bitcast.31), calls=%async_computation | async-start | bytes 2359296 | tf_op jit(solution)/shard_map/all_to_all | solution.py:112
  10.6 31.7 %copy-start.1 = (f32[32,2304]{1,0:T(8,128)S(1)}, f32[32,2304]{1,0:T(8,128)}, u32[]{:S(2)}) copy-start(f32[32,2304]{1,0:T(8,128)} %param.10) | copy-start | bytes 884740
  11.4 31.1 %copy-start.2 = (f32[2304]{0:T(1024)S(1)}, f32[2304]{0:T(1024)}, u32[]{:S(2)}) copy-start(f32[2304]{0:T(1024)} %param.12) | copy-start | bytes 27652
  64.7 17.7 %collective-permute-start = (bf16[128,2304]{1,0:T(8,128)(2,1)S(1)}, bf16[128,2304]{1,0:T(8,128)(2,1)S(1)}, u32[]{:S(2)}, u32[]{:S(2)}) collective-permute-start(bf16[128,2304]{1,0:T(8,128)(2,1)S(1)} %bitcast.22), channel_id=1, source_target_pairs={{0,1},{1,2},{2,3},{3,0},{4,5},{5,6},{6,7},{7,4},{8,9},{9,10},{10,1... | collective-permute-start | bytes 1769480 | tf_op jit(solution)/shard_map/ppermute | solution.py:137
  68.1 16.2 %collective-permute-start.1 = (bf16[128,2304]{1,0:T(8,128)(2,1)S(1)}, bf16[128,2304]{1,0:T(8,128)(2,1)S(1)}, u32[]{:S(2)}, u32[]{:S(2)}) collective-permute-start(bf16[128,2304]{1,0:T(8,128)(2,1)S(1)} %bitcast.23), channel_id=1, source_target_pairs={{0,3},{1,0},{2,1},{3,2},{4,7},{5,4},{6,5},{7,6},{8,11},{9,8},{10,9... | collective-permute-start | bytes 1769480 | tf_op jit(solution)/shard_map/ppermute | solution.py:137
  84.3 19.4 %collective-permute-start.4 = (bf16[128,2304]{1,0:T(8,128)(2,1)S(1)}, bf16[128,2304]{1,0:T(8,128)(2,1)S(1)}, u32[]{:S(2)}, u32[]{:S(2)}) collective-permute-start(bf16[128,2304]{1,0:T(8,128)(2,1)S(1)} %bitcast.25), channel_id=1, source_target_pairs={{0,2},{1,3},{2,0},{3,1},{4,6},{5,7},{6,4},{7,5},{8,10},{9,11},{10,... | collective-permute-start | bytes 1769480 | tf_op jit(solution)/shard_map/ppermute | solution.py:137
  92.9 24.0 %collective-permute-start.2 = (bf16[128,2304]{1,0:T(8,128)(2,1)S(1)}, bf16[128,2304]{1,0:T(8,128)(2,1)S(1)}, u32[]{:S(2)}, u32[]{:S(2)}) collective-permute-start(bf16[128,2304]{1,0:T(8,128)(2,1)S(1)} %get-tuple-element.21), channel_id=1, source_target_pairs={{0,3},{1,0},{2,1},{3,2},{4,7},{5,4},{6,5},{7,6},{8,11},{9,8},{10,9... | collective-permute-start | bytes 1769480 | tf_op jit(solution)/shard_map/ppermute | solution.py:137
  96.3 30.7 %collective-permute-start.3 = (bf16[128,2304]{1,0:T(8,128)(2,1)S(1)}, bf16[128,2304]{1,0:T(8,128)(2,1)S(1)}, u32[]{:S(2)}, u32[]{:S(2)}) collective-permute-start(bf16[128,2304]{1,0:T(8,128)(2,1)S(1)} %get-tuple-element.22), channel_id=1, source_target_pairs={{0,1},{1,2},{2,3},{3,0},{4,5},{5,6},{6,7},{7,4},{8,9},{9,10},{10,1... | collective-permute-start | bytes 1769480 | tf_op jit(solution)/shard_map/ppermute | solution.py:137
  105.9 21.2 %collective-permute-start.5 = (bf16[128,2304]{1,0:T(8,128)(2,1)S(1)}, bf16[128,2304]{1,0:T(8,128)(2,1)S(1)}, u32[]{:S(2)}, u32[]{:S(2)}) collective-permute-start(bf16[128,2304]{1,0:T(8,128)(2,1)S(1)} %shard_map.94), channel_id=1, source_target_pairs={{0,2},{1,3},{2,0},{3,1},{4,6},{5,7},{6,4},{7,5},{8,10},{9,11},{10,... | collective-permute-start | bytes 1769480 | tf_op jit(solution)/shard_map/ppermute | solution.py:137
  128.1 3.7 %copy-start.4 = (f32[32,2]{0,1:T(2,128)S(1)}, f32[32,2]{0,1:T(2,128)}, u32[]{:S(2)}) copy-start(f32[32,2]{0,1:T(2,128)} %param.17) | copy-start | bytes 772
  128.1 19.6 %all-to-all-start.2 = ((bf16[8,16,2304]{2,1,0:T(8,128)(2,1)}), bf16[8,16,2304]{2,1,0:T(8,128)(2,1)S(1)}, u32[]{:S(2)}, u32[]{:S(2)}) async-start(bf16[8,16,2304]{2,1,0:T(8,128)(2,1)} %bitcast.11), calls=%async_computation.2 | async-start | bytes 1179648 | tf_op jit(solution)/shard_map/all_to_all | solution.py:158

commit v11 on v5

--- a/solution.py
+++ b/solution.py
@@ -142,14 +142,17 @@
     after_rows = shift(own, -1)
     (own_sum,) = ffn([own], *weights)
     far_rows = shift(lax.optimization_barrier((own, own_sum))[0], 2)
-    before_sum, after_sum = ffn([before_rows, after_rows], *weights)
+    before_rows, after_rows = lax.optimization_barrier((before_rows, after_rows))
+    (before_sum,) = ffn([before_rows], *weights)
     back_after = shift(before_sum, -1)
+    after_rows = lax.optimization_barrier((after_rows, before_sum))[0]
+    (after_sum,) = ffn([after_rows], *weights)
     back_before = shift(after_sum, 1)
-    far_rows = lax.optimization_barrier((far_rows, before_sum))[0]
+    far_rows = lax.optimization_barrier((far_rows, after_sum))[0]
     (far_sum,) = ffn([far_rows], *weights)
     back_far = shift(far_sum, 2)
-    near = own_sum.astype(jnp.float32)
-    near = near + back_after.astype(jnp.float32) + back_before.astype(jnp.float32)
+    near = own_sum.astype(jnp.float32) + back_after.astype(jnp.float32)
+    near = lax.optimization_barrier(near) + back_before.astype(jnp.float32)
     outputs = lax.optimization_barrier(near) + back_far.astype(jnp.float32)
     outputs = outputs.astype(jnp.bfloat16).reshape(model_parts, MOST, features)
     outputs = lax.all_to_all(outputs, "mp", split_axis=0, concat_axis=0, tiled=True)

time: 147 us -> 147 us (level)
    pallas_call x3 -> x4, Pallas kernels: 8.24 us -> 8.53 us  [ffn(): pl.pallas_call(functools.partial(ffn_kernel, count), out_shape=[jax.Shape...]
where the time goes in v11:
time: 147 us; the launch traced here: 144 us
  waiting for transfers between devices  68.3 us (46%)
  starting transfers between devices  33 us (22%)
  blocking collectives  21.7 us (15%)
  Pallas kernels  13.7 us (9%)
  matrix products  3.47 us (2%)
  local copies, waits for them, and re-layouts  1.96 us (1%)
  other arithmetic  1.8 us (1%)
    all_to_all x1, waiting for transfers between devices, body(): parts = lax.all_to_all(parts, 'mp', split_axis=0, concat_axis=0, tiled=True)  30.8 us
    ppermute x6, waiting for transfers between devices, shift(): lax.ppermute(value, 'expert', [(i, (i + by) % unit_parts) for i in range(...  23.7 us
    ppermute x6, starting transfers between devices, shift(): lax.ppermute(value, 'expert', [(i, (i + by) % unit_parts) for i in range(...  22.1 us
    all_to_all x1, blocking collectives, body(): lax.all_to_all(outgoing, 'mp', split_axis=0, concat_axis=0, tiled=True)  21.7 us
    all_to_all x1, waiting for transfers between devices, body(): lax.all_to_all(outputs, 'mp', split_axis=0, concat_axis=0, tiled=True)  13.9 us
    pallas_call x4, Pallas kernels, ffn(): pl.pallas_call(functools.partial(ffn_kernel, count), out_shape=[jax.Shape...  8.53 us
    all_to_all x1, starting transfers between devices, body(): parts = lax.all_to_all(parts, 'mp', split_axis=0, concat_axis=0, tiled=True)  7.23 us
    pallas_call x1, Pallas kernels, load(): pl.pallas_call(load_kernel, out_shape=[pltpu.VMEM(w.shape, w.dtype) for w...  5.15 us
  transfers between devices with their start and end apart: 8, of which 5 were waited for; matrix products, arithmetic and copies ran while one was open for 1% of the time, Pallas kernels for 9%

profile of v11, /device:TPU:448, one launch (start us, length us, event | category | flops | bytes accessed | tf_op | source)
XLA Modules:
  0.0 144.2 jit_solution(13813261462316503284)
XLA Ops:
  0.0 0.0 copy-start
  0.0 1.5 %copy.17 = bf16[1024,288]{1,0:T(8,128)(2,1)S(1)} copy(bf16[1024,288]{0,1:T(8,128)(2,1)} %param.9) | data formatting | bytes 1179648 | tf_op args[0]
  1.6 0.0 copy-done
  1.6 1.8 %convolution_convert_fusion = f16[256,2304]{1,0:T(8,128)(2,1)} fusion(bf16[256,288]{1,0:T(8,128)(2,1)S(1)} %bitcast.34, bf16[288,2304]{1,0:T(8,128)(2,1)S(1)} %copy-done), kind=kOutput, calls=%fused_computation | convolution fusion | flops 340328448 | bytes 2654208 | tf_op jit(solution)/shard_map/dot_general | solution.py:110
  3.4 0.0 copy-start.3
  3.4 7.2 %all-to-all-start = ((f16[8,32,2304]{2,1,0:T(8,128)(2,1)}), f16[8,32,2304]{2,1,0:T(8,128)(2,1)S(1)}, u32[]{:S(2)}, u32[]{:S(2)}) async-start(f16[8,32,2304]{2,1,0:T(8,128)(2,1)} %bitcast.31), calls=%async_computation | async-start | bytes 2359296 | tf_op jit(solution)/shard_map/all_to_all | solution.py:112
  10.6 0.0 copy-done.3
  10.6 0.0 copy-start.1
  10.6 0.1 copy.18
  10.7 0.1 eq.45
  10.8 0.1 fusion.4
  10.9 0.1 reduce_window_sum.11
  11.0 0.2 select_reduce_fusion
  11.2 0.1 reduce_sum.31
  11.3 0.1 copy.19
  11.4 0.0 copy-start.2
  11.4 30.8 %all-to-all-done = f16[8,32,2304]{2,1,0:T(8,128)(2,1)S(1)} async-done(((f16[8,32,2304]{2,1,0:T(8,128)(2,1)}), f16[8,32,2304]{2,1,0:T(8,128)(2,1)S(1)}, u32[]{:S(2)}, u32[]{:S(2)}) %all-to-all-start) | async-done | bytes 1179680 | tf_op jit(solution)/shard_map/all_to_all | solution.py:112
  42.2 0.2 convert_reduce_fusion
  42.4 0.0 copy-done.1
  42.4 0.1 multiply_reduce_fusion
  42.5 0.0 copy-done.2
  42.5 0.4 convolution_convert_fusion.1
  43.0 21.7 %all_to_all.15 = bf16[8,16,2304]{2,1,0:T(8,128)(2,1)S(1)} all-to-all(bf16[8,16,2304]{2,1,0:T(8,128)(2,1)S(1)} %bitcast.32), channel_id=1, replica_groups=mesh['dp'=16,'mp'=8,'expert'=4] {'mp'}, dimensions={0} | all-to-all | bytes 1179648 | tf_op jit(solution)/shard_map/all_to_all | solution.py:131
  64.7 3.4 %collective-permute-start = (bf16[128,2304]{1,0:T(8,128)(2,1)S(1)}, bf16[128,2304]{1,0:T(8,128)(2,1)S(1)}, u32[]{:S(2)}, u32[]{:S(2)}) collective-permute-start(bf16[128,2304]{1,0:T(8,128)(2,1)S(1)} %bitcast.22), channel_id=1, source_target_pairs={{0,1},{1,2},{2,3},{3,0},{4,5},{5,6},{6,7},{7,4},{8,9},{9,10},{10,1... | collective-permute-start | bytes 1769480 | tf_op jit(solution)/shard_map/ppermute | solution.py:137
  68.1 3.7 %collective-permute-start.1 = (bf16[128,2304]{1,0:T(8,128)(2,1)S(1)}, bf16[128,2304]{1,0:T(8,128)(2,1)S(1)}, u32[]{:S(2)}, u32[]{:S(2)}) collective-permute-start(bf16[128,2304]{1,0:T(8,128)(2,1)S(1)} %bitcast.23), channel_id=1, source_target_pairs={{0,3},{1,0},{2,1},{3,2},{4,7},{5,4},{6,5},{7,6},{8,11},{9,8},{10,9... | collective-permute-start | bytes 1769480 | tf_op jit(solution)/shard_map/ppermute | solution.py:137
  71.8 5.1 %shard_map.91 = (bf16[2304,1024]{1,0:T(8,128)(2,1)S(1)}, bf16[2304,1024]{1,0:T(8,128)(2,1)S(1)}, bf16[1024,2304]{1,0:T(8,128)(2,1)S(1)}) custom-call(bf16[2304,1024]{1,0:T(8,128)(2,1)} %bitcast.28, bf16[2304,1024]{1,0:T(8,128)(2,1)} %bitcast.29, bf16[1024,2304]{1,0:T(8,128)(2,1)} %bitcast.30), custom_call_target="tpu_custom_call" | custom-call | bytes 28311552 | tf_op jit(solution)/shard_map/pallas_call | solution.py:34
  76.9 2.1 %shard_map.92 = bf16[128,2304]{1,0:T(8,128)(2,1)S(1)} custom-call(bf16[128,2304]{1,0:T(8,128)(2,1)S(1)} %bitcast.24, bf16[2304,1024]{1,0:T(8,128)(2,1)S(1)} %get-tuple-element.13.refs_1_, bf16[2304,1024]{1,0:T(8,128)(2,1)S(1)} %get-tuple-element.14.refs_2_, bf16[1024,2304]{1,0:T(8,128)(2,1)S(1)} %get-tuple-element.15.refs_3_), custom_call_target="tpu_custom_call" | custom-call | flops 1811939328 | bytes 15335424 | tf_op jit(solution)/shard_map/pallas_call | solution.py:77
  79.1 3.7 %collective-permute-start.4 = (bf16[128,2304]{1,0:T(8,128)(2,1)S(1)}, bf16[128,2304]{1,0:T(8,128)(2,1)S(1)}, u32[]{:S(2)}, u32[]{:S(2)}) collective-permute-start(bf16[128,2304]{1,0:T(8,128)(2,1)S(1)} %bitcast.25), channel_id=1, source_target_pairs={{0,2},{1,3},{2,0},{3,1},{4,6},{5,7},{6,4},{7,5},{8,10},{9,11},{10,... | collective-permute-start | bytes 1769480 | tf_op jit(solution)/shard_map/ppermute | solution.py:137
  82.8 0.0 collective-permute-done.refs_0_
  82.8 11.9 %collective-permute-done.1.refs_0_ = bf16[128,2304]{1,0:T(8,128)(2,1)S(1)} collective-permute-done((bf16[128,2304]{1,0:T(8,128)(2,1)S(1)}, bf16[128,2304]{1,0:T(8,128)(2,1)S(1)}, u32[]{:S(2)}, u32[]{:S(2)}) %collective-permute-start.1) | collective-permute-done | bytes 589856 | tf_op jit(solution)/shard_map/ppermute | solution.py:137
  94.7 2.1 %shard_map.93 = bf16[128,2304]{1,0:T(8,128)(2,1)S(1)} custom-call(bf16[128,2304]{1,0:T(8,128)(2,1)S(1)} %collective-permute-done.refs_0_, bf16[2304,1024]{1,0:T(8,128)(2,1)S(1)} %get-tuple-element.13.refs_1_, bf16[2304,1024]{1,0:T(8,128)(2,1)S(1)} %get-tuple-element.14.refs_2_, bf16[1024,2304]{1,0:T(8,128)(2,1)S(1)} %get-tuple-element.15.refs_3_), custom_call_target="tpu_custom_call" | custom-call | flops 1811939328 | bytes 15335424 | tf_op jit(solution)/shard_map/pallas_call | solution.py:77
  96.9 6.0 %collective-permute-start.2 = (bf16[128,2304]{1,0:T(8,128)(2,1)S(1)}, bf16[128,2304]{1,0:T(8,128)(2,1)S(1)}, u32[]{:S(2)}, u32[]{:S(2)}) collective-permute-start(bf16[128,2304]{1,0:T(8,128)(2,1)S(1)} %shard_map.93), channel_id=1, source_target_pairs={{0,3},{1,0},{2,1},{3,2},{4,7},{5,4},{6,5},{7,6},{8,11},{9,8},{10,9... | collective-permute-start | bytes 1769480 | tf_op jit(solution)/shard_map/ppermute | solution.py:137
  102.9 2.1 %shard_map.94 = bf16[128,2304]{1,0:T(8,128)(2,1)S(1)} custom-call(bf16[128,2304]{1,0:T(8,128)(2,1)S(1)} %collective-permute-done.1.refs_0_, bf16[2304,1024]{1,0:T(8,128)(2,1)S(1)} %get-tuple-element.13.refs_1_, bf16[2304,1024]{1,0:T(8,128)(2,1)S(1)} %get-tuple-element.14.refs_2_, bf16[1024,2304]{1,0:T(8,128)(2,1)S(1)} %get-tuple-element.15.refs_3_), custom_call_target="tpu_custom_call" | custom-call | flops 1811939328 | bytes 15335424 | tf_op jit(solution)/shard_map/pallas_call | solution.py:77
  105.0 1.9 %collective-permute-start.3 = (bf16[128,2304]{1,0:T(8,128)(2,1)S(1)}, bf16[128,2304]{1,0:T(8,128)(2,1)S(1)}, u32[]{:S(2)}, u32[]{:S(2)}) collective-permute-start(bf16[128,2304]{1,0:T(8,128)(2,1)S(1)} %shard_map.94), channel_id=1, source_target_pairs={{0,1},{1,2},{2,3},{3,0},{4,5},{5,6},{6,7},{7,4},{8,9},{9,10},{10,1... | collective-permute-start | bytes 1769480 | tf_op jit(solution)/shard_map/ppermute | solution.py:137
  107.0 0.0 collective-permute-done.4.refs_0_
  107.0 2.1 %shard_map.95 = bf16[128,2304]{1,0:T(8,128)(2,1)S(1)} custom-call(bf16[128,2304]{1,0:T(8,128)(2,1)S(1)} %collective-permute-done.4.refs_0_, bf16[2304,1024]{1,0:T(8,128)(2,1)S(1)} %get-tuple-element.13.refs_1_, bf16[2304,1024]{1,0:T(8,128)(2,1)S(1)} %get-tuple-element.14.refs_2_, bf16[1024,2304]{1,0:T(8,128)(2,1)S(1)} %get-tuple-element.15.refs_3_), custom_call_target="tpu_custom_call" | custom-call | flops 1811939328 | bytes 15335424 | tf_op jit(solution)/shard_map/pallas_call | solution.py:77
  109.1 3.4 %collective-permute-start.5 = (bf16[128,2304]{1,0:T(8,128)(2,1)S(1)}, bf16[128,2304]{1,0:T(8,128)(2,1)S(1)}, u32[]{:S(2)}, u32[]{:S(2)}) collective-permute-start(bf16[128,2304]{1,0:T(8,128)(2,1)S(1)} %shard_map.95), channel_id=1, source_target_pairs={{0,2},{1,3},{2,0},{3,1},{4,6},{5,7},{6,4},{7,5},{8,10},{9,11},{10,... | collective-permute-start | bytes 1769480 | tf_op jit(solution)/shard_map/ppermute | solution.py:137
  112.5 10.1 %collective-permute-done.2 = bf16[128,2304]{1,0:T(8,128)(2,1)S(1)} collective-permute-done((bf16[128,2304]{1,0:T(8,128)(2,1)S(1)}, bf16[128,2304]{1,0:T(8,128)(2,1)S(1)}, u32[]{:S(2)}, u32[]{:S(2)}) %collective-permute-start.2) | collective-permute-done | bytes 589856 | tf_op jit(solution)/shard_map/ppermute | solution.py:137
  122.6 0.1 convert_add_fusion.1
  122.7 1.6 %collective-permute-done.3 = bf16[128,2304]{1,0:T(8,128)(2,1)S(1)} collective-permute-done((bf16[128,2304]{1,0:T(8,128)(2,1)S(1)}, bf16[128,2304]{1,0:T(8,128)(2,1)S(1)}, u32[]{:S(2)}, u32[]{:S(2)}) %collective-permute-start.3) | collective-permute-done | bytes 589856 | tf_op jit(solution)/shard_map/ppermute | solution.py:137
  124.3 0.1 convert_add_fusion
  124.4 0.0 collective-permute-done.5
  124.4 0.9 add_convert_fusion
  125.4 0.0 copy-start.4
  125.4 3.7 %all-to-all-start.2 = ((bf16[8,16,2304]{2,1,0:T(8,128)(2,1)}), bf16[8,16,2304]{2,1,0:T(8,128)(2,1)S(1)}, u32[]{:S(2)}, u32[]{:S(2)}) async-start(bf16[8,16,2304]{2,1,0:T(8,128)(2,1)} %bitcast.11), calls=%async_computation.2 | async-start | bytes 1179648 | tf_op jit(solution)/shard_map/all_to_all | solution.py:158
  129.0 0.0 copy-done.4
  129.1 13.9 %all-to-all-done.2 = bf16[8,16,2304]{2,1,0:T(8,128)(2,1)S(1)} async-done(((bf16[8,16,2304]{2,1,0:T(8,128)(2,1)}), bf16[8,16,2304]{2,1,0:T(8,128)(2,1)S(1)}, u32[]{:S(2)}, u32[]{:S(2)}) %all-to-all-start.2) | async-done | bytes 589856 | tf_op jit(solution)/shard_map/all_to_all | solution.py:158
  142.9 0.3 convolution_multiply_fusion
  143.2 1.0 fusion.1
  (5 shorter events, 0.1 us)
Async XLA Ops:
  0.0 1.6 %copy-start = (bf16[288,2304]{1,0:T(8,128)(2,1)S(1)}, bf16[288,2304]{1,0:T(8,128)(2,1)}, u32[]{:S(2)}) copy-start(bf16[288,2304]{1,0:T(8,128)(2,1)} %param.11) | copy-start | bytes 3981316
  3.4 7.2 %copy-start.3 = (s32[32,2]{0,1:T(2,128)S(1)}, s32[32,2]{0,1:T(2,128)}, u32[]{:S(2)}) copy-start(s32[32,2]{0,1:T(2,128)} %param.16) | copy-start | bytes 772
  3.4 38.8 %all-to-all-start = ((f16[8,32,2304]{2,1,0:T(8,128)(2,1)}), f16[8,32,2304]{2,1,0:T(8,128)(2,1)S(1)}, u32[]{:S(2)}, u32[]{:S(2)}) async-start(f16[8,32,2304]{2,1,0:T(8,128)(2,1)} %bitcast.31), calls=%async_computation | async-start | bytes 2359296 | tf_op jit(solution)/shard_map/all_to_all | solution.py:112
  10.6 31.7 %copy-start.1 = (f32[32,2304]{1,0:T(8,128)S(1)}, f32[32,2304]{1,0:T(8,128)}, u32[]{:S(2)}) copy-start(f32[32,2304]{1,0:T(8,128)} %param.10) | copy-start | bytes 884740
  11.4 31.1 %copy-start.2 = (f32[2304]{0:T(1024)S(1)}, f32[2304]{0:T(1024)}, u32[]{:S(2)}) copy-start(f32[2304]{0:T(1024)} %param.12) | copy-start | bytes 27652
  64.7 18.1 %collective-permute-start = (bf16[128,2304]{1,0:T(8,128)(2,1)S(1)}, bf16[128,2304]{1,0:T(8,128)(2,1)S(1)}, u32[]{:S(2)}, u32[]{:S(2)}) collective-permute-start(bf16[128,2304]{1,0:T(8,128)(2,1)S(1)} %bitcast.22), channel_id=1, source_target_pairs={{0,1},{1,2},{2,3},{3,0},{4,5},{5,6},{6,7},{7,4},{8,9},{9,10},{10,1... | collective-permute-start | bytes 1769480 | tf_op jit(solution)/shard_map/ppermute | solution.py:137
  68.1 26.6 %collective-permute-start.1 = (bf16[128,2304]{1,0:T(8,128)(2,1)S(1)}, bf16[128,2304]{1,0:T(8,128)(2,1)S(1)}, u32[]{:S(2)}, u32[]{:S(2)}) collective-permute-start(bf16[128,2304]{1,0:T(8,128)(2,1)S(1)} %bitcast.23), channel_id=1, source_target_pairs={{0,3},{1,0},{2,1},{3,2},{4,7},{5,4},{6,5},{7,6},{8,11},{9,8},{10,9... | collective-permute-start | bytes 1769480 | tf_op jit(solution)/shard_map/ppermute | solution.py:137
  79.1 27.9 %collective-permute-start.4 = (bf16[128,2304]{1,0:T(8,128)(2,1)S(1)}, bf16[128,2304]{1,0:T(8,128)(2,1)S(1)}, u32[]{:S(2)}, u32[]{:S(2)}) collective-permute-start(bf16[128,2304]{1,0:T(8,128)(2,1)S(1)} %bitcast.25), channel_id=1, source_target_pairs={{0,2},{1,3},{2,0},{3,1},{4,6},{5,7},{6,4},{7,5},{8,10},{9,11},{10,... | collective-permute-start | bytes 1769480 | tf_op jit(solution)/shard_map/ppermute | solution.py:137
  96.9 25.7 %collective-permute-start.2 = (bf16[128,2304]{1,0:T(8,128)(2,1)S(1)}, bf16[128,2304]{1,0:T(8,128)(2,1)S(1)}, u32[]{:S(2)}, u32[]{:S(2)}) collective-permute-start(bf16[128,2304]{1,0:T(8,128)(2,1)S(1)} %shard_map.93), channel_id=1, source_target_pairs={{0,3},{1,0},{2,1},{3,2},{4,7},{5,4},{6,5},{7,6},{8,11},{9,8},{10,9... | collective-permute-start | bytes 1769480 | tf_op jit(solution)/shard_map/ppermute | solution.py:137
  105.0 19.3 %collective-permute-start.3 = (bf16[128,2304]{1,0:T(8,128)(2,1)S(1)}, bf16[128,2304]{1,0:T(8,128)(2,1)S(1)}, u32[]{:S(2)}, u32[]{:S(2)}) collective-permute-start(bf16[128,2304]{1,0:T(8,128)(2,1)S(1)} %shard_map.94), channel_id=1, source_target_pairs={{0,1},{1,2},{2,3},{3,0},{4,5},{5,6},{6,7},{7,4},{8,9},{9,10},{10,1... | collective-permute-start | bytes 1769480 | tf_op jit(solution)/shard_map/ppermute | solution.py:137
  109.1 15.3 %collective-permute-start.5 = (bf16[128,2304]{1,0:T(8,128)(2,1)S(1)}, bf16[128,2304]{1,0:T(8,128)(2,1)S(1)}, u32[]{:S(2)}, u32[]{:S(2)}) collective-permute-start(bf16[128,2304]{1,0:T(8,128)(2,1)S(1)} %shard_map.95), channel_id=1, source_target_pairs={{0,2},{1,3},{2,0},{3,1},{4,6},{5,7},{6,4},{7,5},{8,10},{9,11},{10,... | collective-permute-start | bytes 1769480 | tf_op jit(solution)/shard_map/ppermute | solution.py:137
  125.4 3.7 %copy-start.4 = (f32[32,2]{0,1:T(2,128)S(1)}, f32[32,2]{0,1:T(2,128)}, u32[]{:S(2)}) copy-start(f32[32,2]{0,1:T(2,128)} %param.17) | copy-start | bytes 772
  125.4 17.6 %all-to-all-start.2 = ((bf16[8,16,2304]{2,1,0:T(8,128)(2,1)}), bf16[8,16,2304]{2,1,0:T(8,128)(2,1)S(1)}, u32[]{:S(2)}, u32[]{:S(2)}) async-start(bf16[8,16,2304]{2,1,0:T(8,128)(2,1)} %bitcast.11), calls=%async_computation.2 | async-start | bytes 1179648 | tf_op jit(solution)/shard_map/all_to_all | solution.py:158

commit v12 on v11

--- a/solution.py
+++ b/solution.py
@@ -13,6 +13,34 @@
 
 UNIT_CHUNK = 512
 OUT_CHUNK = 1152
+ROW_BLOCK = 32
+
+
+def pick_kernel(place_ref, columns_ref, out_ref):
+    count = columns_ref.shape[1]
+    rows = out_ref.shape[0]
+    row = lax.broadcasted_iota(jnp.int32, (rows, count), 0)
+    source = lax.broadcasted_iota(jnp.int32, (rows, count), 1)
+    group = count // rows
+    wanted = (row // ROW_BLOCK * group + place_ref[0]) * ROW_BLOCK + row % ROW_BLOCK
+    pick = (source == wanted).astype(jnp.float32).astype(jnp.bfloat16)
+    out_ref[...] = lax.dot_general(
+        pick,
+        columns_ref[...],
+        (((1,), (1,)), ((), ())),
+        preferred_element_type=jnp.float32,
+    ).astype(jnp.bfloat16)
+
+
+def pick_rows(place, attn_out, rows):
+    vmem = pl.BlockSpec(memory_space=pltpu.VMEM)
+    return pl.pallas_call(
+        pick_kernel,
+        out_shape=jax.ShapeDtypeStruct((rows, attn_out.shape[1]), attn_out.dtype),
+        in_specs=[pl.BlockSpec(memory_space=pltpu.SMEM), vmem],
+        out_specs=vmem,
+        compiler_params=pltpu.CompilerParams(vmem_limit_bytes=16 << 20),
+    )(place.reshape(1), attn_out.T)
 
 
 def load_kernel(*refs):
@@ -104,9 +132,7 @@
     unit_parts = lax.axis_size("expert")
     row_count = residual.shape[0]
     features = residual.shape[1]
-    blocks = attn_out.reshape(model_parts, unit_parts, row_count, attn_out.shape[1])
-    picked = lax.dynamic_index_in_dim(blocks, lax.axis_index("expert"), axis=1, keepdims=False)
-    picked = picked.reshape(model_parts * row_count, attn_out.shape[1])
+    picked = pick_rows(lax.axis_index("expert"), attn_out, model_parts * row_count)
     parts = jnp.dot(picked, proj_weight, preferred_element_type=jnp.float32).astype(jnp.float16)
     parts = parts.reshape(model_parts, row_count, features)
     parts = lax.all_to_all(parts, "mp", split_axis=0, concat_axis=0, tiled=True)

time: 147 us -> 147 us (level)
  no operation moved by 1% of the time
where the time goes in v12:
time: 147 us; the launch traced here: 144 us
  waiting for transfers between devices  68.3 us (46%)
  starting transfers between devices  33 us (22%)
  blocking collectives  21.7 us (15%)
  Pallas kernels  14.1 us (10%)
  matrix products  3.49 us (2%)
  other arithmetic  1.81 us (1%)
  local copies, waits for them, and re-layouts  1.58 us (1%)
    all_to_all x1, waiting for transfers between devices, body(): parts = lax.all_to_all(parts, 'mp', split_axis=0, concat_axis=0, tiled=True)  30.8 us
    ppermute x6, waiting for transfers between devices, shift(): lax.ppermute(value, 'expert', [(i, (i + by) % unit_parts) for i in range(...  23.6 us
    ppermute x6, starting transfers between devices, shift(): lax.ppermute(value, 'expert', [(i, (i + by) % unit_parts) for i in range(...  22.1 us
    all_to_all x1, blocking collectives, body(): lax.all_to_all(outgoing, 'mp', split_axis=0, concat_axis=0, tiled=True)  21.7 us
    all_to_all x1, waiting for transfers between devices, body(): lax.all_to_all(outputs, 'mp', split_axis=0, concat_axis=0, tiled=True)  13.9 us
    pallas_call x4, Pallas kernels, ffn(): pl.pallas_call(functools.partial(ffn_kernel, count), out_shape=[jax.Shape...  8.52 us
    all_to_all x1, starting transfers between devices, body(): parts = lax.all_to_all(parts, 'mp', split_axis=0, concat_axis=0, tiled=True)  7.23 us
    pallas_call x1, Pallas kernels, load(): pl.pallas_call(load_kernel, out_shape=[pltpu.VMEM(w.shape, w.dtype) for w...  5.15 us
  transfers between devices with their start and end apart: 8, of which 5 were waited for; matrix products, arithmetic and copies ran while one was open for 1% of the time, Pallas kernels for 9%

profile of v12, /device:TPU:448, one launch (start us, length us, event | category | flops | bytes accessed | tf_op | source)
XLA Modules:
  0.0 144.3 jit_solution(4847889636583695700)
XLA Ops:
  0.0 0.0 copy-start
  0.0 0.0 copy-start.1
  0.0 1.2 copy-done.1
  1.2 0.5 shard_map.91
  1.6 0.0 copy-done
  1.6 1.8 %convolution_convert_fusion = f16[256,2304]{1,0:T(8,128)(2,1)} fusion(bf16[256,288]{1,0:T(8,128)(2,1)S(1)} %shard_map.91, bf16[288,2304]{1,0:T(8,128)(2,1)S(1)} %copy-done), kind=kOutput, calls=%fused_computation | convolution fusion | flops 340328448 | bytes 2654208 | tf_op jit(solution)/shard_map/dot_general | solution.py:136
  3.5 0.0 copy-start.4
  3.5 7.2 %all-to-all-start = ((f16[8,32,2304]{2,1,0:T(8,128)(2,1)}), f16[8,32,2304]{2,1,0:T(8,128)(2,1)S(1)}, u32[]{:S(2)}, u32[]{:S(2)}) async-start(f16[8,32,2304]{2,1,0:T(8,128)(2,1)} %bitcast.32), calls=%async_computation | async-start | bytes 2359296 | tf_op jit(solution)/shard_map/all_to_all | solution.py:138
  10.7 0.0 copy-done.4
  10.7 0.0 copy-start.2
  10.7 0.1 copy.16
  10.8 0.1 eq.45
  10.9 0.1 fusion.4
  11.0 0.1 reduce_window_sum.11
  11.1 0.2 select_reduce_fusion
  11.3 0.1 reduce_sum.31
  11.4 0.1 copy.17
  11.5 0.0 copy-start.3
  11.5 30.8 %all-to-all-done = f16[8,32,2304]{2,1,0:T(8,128)(2,1)S(1)} async-done(((f16[8,32,2304]{2,1,0:T(8,128)(2,1)}), f16[8,32,2304]{2,1,0:T(8,128)(2,1)S(1)}, u32[]{:S(2)}, u32[]{:S(2)}) %all-to-all-start) | async-done | bytes 1179680 | tf_op jit(solution)/shard_map/all_to_all | solution.py:138
  42.3 0.2 convert_reduce_fusion
  42.4 0.0 copy-done.2
  42.4 0.1 multiply_reduce_fusion
  42.6 0.0 copy-done.3
  42.6 0.4 convolution_convert_fusion.1
  43.1 21.7 %all_to_all.15 = bf16[8,16,2304]{2,1,0:T(8,128)(2,1)S(1)} all-to-all(bf16[8,16,2304]{2,1,0:T(8,128)(2,1)S(1)} %bitcast.33), channel_id=1, replica_groups=mesh['dp'=16,'mp'=8,'expert'=4] {'mp'}, dimensions={0} | all-to-all | bytes 1179648 | tf_op jit(solution)/shard_map/all_to_all | solution.py:157
  64.8 3.4 %collective-permute-start = (bf16[128,2304]{1,0:T(8,128)(2,1)S(1)}, bf16[128,2304]{1,0:T(8,128)(2,1)S(1)}, u32[]{:S(2)}, u32[]{:S(2)}) collective-permute-start(bf16[128,2304]{1,0:T(8,128)(2,1)S(1)} %bitcast.22), channel_id=1, source_target_pairs={{0,1},{1,2},{2,3},{3,0},{4,5},{5,6},{6,7},{7,4},{8,9},{9,10},{10,1... | collective-permute-start | bytes 1769480 | tf_op jit(solution)/shard_map/ppermute | solution.py:163
  68.2 3.7 %collective-permute-start.1 = (bf16[128,2304]{1,0:T(8,128)(2,1)S(1)}, bf16[128,2304]{1,0:T(8,128)(2,1)S(1)}, u32[]{:S(2)}, u32[]{:S(2)}) collective-permute-start(bf16[128,2304]{1,0:T(8,128)(2,1)S(1)} %bitcast.23), channel_id=1, source_target_pairs={{0,3},{1,0},{2,1},{3,2},{4,7},{5,4},{6,5},{7,6},{8,11},{9,8},{10,9... | collective-permute-start | bytes 1769480 | tf_op jit(solution)/shard_map/ppermute | solution.py:163
  71.8 5.1 %shard_map.92 = (bf16[2304,1024]{1,0:T(8,128)(2,1)S(1)}, bf16[2304,1024]{1,0:T(8,128)(2,1)S(1)}, bf16[1024,2304]{1,0:T(8,128)(2,1)S(1)}) custom-call(bf16[2304,1024]{1,0:T(8,128)(2,1)} %bitcast.29, bf16[2304,1024]{1,0:T(8,128)(2,1)} %bitcast.30, bf16[1024,2304]{1,0:T(8,128)(2,1)} %bitcast.31), custom_call_target="tpu_custom_call" | custom-call | bytes 28311552 | tf_op jit(solution)/shard_map/pallas_call | solution.py:62
  77.0 2.1 %shard_map.93 = bf16[128,2304]{1,0:T(8,128)(2,1)S(1)} custom-call(bf16[128,2304]{1,0:T(8,128)(2,1)S(1)} %bitcast.24, bf16[2304,1024]{1,0:T(8,128)(2,1)S(1)} %get-tuple-element.13.refs_1_, bf16[2304,1024]{1,0:T(8,128)(2,1)S(1)} %get-tuple-element.14.refs_2_, bf16[1024,2304]{1,0:T(8,128)(2,1)S(1)} %get-tuple-element.15.refs_3_), custom_call_target="tpu_custom_call" | custom-call | flops 1811939328 | bytes 15335424 | tf_op jit(solution)/shard_map/pallas_call | solution.py:105
  79.1 3.7 %collective-permute-start.4 = (bf16[128,2304]{1,0:T(8,128)(2,1)S(1)}, bf16[128,2304]{1,0:T(8,128)(2,1)S(1)}, u32[]{:S(2)}, u32[]{:S(2)}) collective-permute-start(bf16[128,2304]{1,0:T(8,128)(2,1)S(1)} %bitcast.25), channel_id=1, source_target_pairs={{0,2},{1,3},{2,0},{3,1},{4,6},{5,7},{6,4},{7,5},{8,10},{9,11},{10,... | collective-permute-start | bytes 1769480 | tf_op jit(solution)/shard_map/ppermute | solution.py:163
  82.9 0.0 collective-permute-done.refs_0_
  82.9 11.9 %collective-permute-done.1.refs_0_ = bf16[128,2304]{1,0:T(8,128)(2,1)S(1)} collective-permute-done((bf16[128,2304]{1,0:T(8,128)(2,1)S(1)}, bf16[128,2304]{1,0:T(8,128)(2,1)S(1)}, u32[]{:S(2)}, u32[]{:S(2)}) %collective-permute-start.1) | collective-permute-done | bytes 589856 | tf_op jit(solution)/shard_map/ppermute | solution.py:163
  94.8 2.1 %shard_map.94 = bf16[128,2304]{1,0:T(8,128)(2,1)S(1)} custom-call(bf16[128,2304]{1,0:T(8,128)(2,1)S(1)} %collective-permute-done.refs_0_, bf16[2304,1024]{1,0:T(8,128)(2,1)S(1)} %get-tuple-element.13.refs_1_, bf16[2304,1024]{1,0:T(8,128)(2,1)S(1)} %get-tuple-element.14.refs_2_, bf16[1024,2304]{1,0:T(8,128)(2,1)S(1)} %get-tuple-element.15.refs_3_), custom_call_target="tpu_custom_call" | custom-call | flops 1811939328 | bytes 15335424 | tf_op jit(solution)/shard_map/pallas_call | solution.py:105
  96.9 6.0 %collective-permute-start.2 = (bf16[128,2304]{1,0:T(8,128)(2,1)S(1)}, bf16[128,2304]{1,0:T(8,128)(2,1)S(1)}, u32[]{:S(2)}, u32[]{:S(2)}) collective-permute-start(bf16[128,2304]{1,0:T(8,128)(2,1)S(1)} %shard_map.94), channel_id=1, source_target_pairs={{0,3},{1,0},{2,1},{3,2},{4,7},{5,4},{6,5},{7,6},{8,11},{9,8},{10,9... | collective-permute-start | bytes 1769480 | tf_op jit(solution)/shard_map/ppermute | solution.py:163
  103.0 2.1 %shard_map.95 = bf16[128,2304]{1,0:T(8,128)(2,1)S(1)} custom-call(bf16[128,2304]{1,0:T(8,128)(2,1)S(1)} %collective-permute-done.1.refs_0_, bf16[2304,1024]{1,0:T(8,128)(2,1)S(1)} %get-tuple-element.13.refs_1_, bf16[2304,1024]{1,0:T(8,128)(2,1)S(1)} %get-tuple-element.14.refs_2_, bf16[1024,2304]{1,0:T(8,128)(2,1)S(1)} %get-tuple-element.15.refs_3_), custom_call_target="tpu_custom_call" | custom-call | flops 1811939328 | bytes 15335424 | tf_op jit(solution)/shard_map/pallas_call | solution.py:105
  105.1 1.9 %collective-permute-start.3 = (bf16[128,2304]{1,0:T(8,128)(2,1)S(1)}, bf16[128,2304]{1,0:T(8,128)(2,1)S(1)}, u32[]{:S(2)}, u32[]{:S(2)}) collective-permute-start(bf16[128,2304]{1,0:T(8,128)(2,1)S(1)} %shard_map.95), channel_id=1, source_target_pairs={{0,1},{1,2},{2,3},{3,0},{4,5},{5,6},{6,7},{7,4},{8,9},{9,10},{10,1... | collective-permute-start | bytes 1769480 | tf_op jit(solution)/shard_map/ppermute | solution.py:163
  107.0 0.0 collective-permute-done.4.refs_0_
  107.0 2.1 %shard_map.96 = bf16[128,2304]{1,0:T(8,128)(2,1)S(1)} custom-call(bf16[128,2304]{1,0:T(8,128)(2,1)S(1)} %collective-permute-done.4.refs_0_, bf16[2304,1024]{1,0:T(8,128)(2,1)S(1)} %get-tuple-element.13.refs_1_, bf16[2304,1024]{1,0:T(8,128)(2,1)S(1)} %get-tuple-element.14.refs_2_, bf16[1024,2304]{1,0:T(8,128)(2,1)S(1)} %get-tuple-element.15.refs_3_), custom_call_target="tpu_custom_call" | custom-call | flops 1811939328 | bytes 15335424 | tf_op jit(solution)/shard_map/pallas_call | solution.py:105
  109.2 3.4 %collective-permute-start.5 = (bf16[128,2304]{1,0:T(8,128)(2,1)S(1)}, bf16[128,2304]{1,0:T(8,128)(2,1)S(1)}, u32[]{:S(2)}, u32[]{:S(2)}) collective-permute-start(bf16[128,2304]{1,0:T(8,128)(2,1)S(1)} %shard_map.96), channel_id=1, source_target_pairs={{0,2},{1,3},{2,0},{3,1},{4,6},{5,7},{6,4},{7,5},{8,10},{9,11},{10,... | collective-permute-start | bytes 1769480 | tf_op jit(solution)/shard_map/ppermute | solution.py:163
  112.6 10.1 %collective-permute-done.2 = bf16[128,2304]{1,0:T(8,128)(2,1)S(1)} collective-permute-done((bf16[128,2304]{1,0:T(8,128)(2,1)S(1)}, bf16[128,2304]{1,0:T(8,128)(2,1)S(1)}, u32[]{:S(2)}, u32[]{:S(2)}) %collective-permute-start.2) | collective-permute-done | bytes 589856 | tf_op jit(solution)/shard_map/ppermute | solution.py:163
  122.7 0.1 convert_add_fusion.1
  122.8 1.6 %collective-permute-done.3 = bf16[128,2304]{1,0:T(8,128)(2,1)S(1)} collective-permute-done((bf16[128,2304]{1,0:T(8,128)(2,1)S(1)}, bf16[128,2304]{1,0:T(8,128)(2,1)S(1)}, u32[]{:S(2)}, u32[]{:S(2)}) %collective-permute-start.3) | collective-permute-done | bytes 589856 | tf_op jit(solution)/shard_map/ppermute | solution.py:163
  124.4 0.1 convert_add_fusion
  124.5 0.0 collective-permute-done.5
  124.5 0.9 add_convert_fusion
  125.4 0.0 copy-start.5
  125.4 3.7 %all-to-all-start.2 = ((bf16[8,16,2304]{2,1,0:T(8,128)(2,1)}), bf16[8,16,2304]{2,1,0:T(8,128)(2,1)S(1)}, u32[]{:S(2)}, u32[]{:S(2)}) async-start(bf16[8,16,2304]{2,1,0:T(8,128)(2,1)} %bitcast.11), calls=%async_computation.2 | async-start | bytes 1179648 | tf_op jit(solution)/shard_map/all_to_all | solution.py:184
  129.1 0.0 copy-done.5
  129.1 13.9 %all-to-all-done.2 = bf16[8,16,2304]{2,1,0:T(8,128)(2,1)S(1)} async-done(((bf16[8,16,2304]{2,1,0:T(8,128)(2,1)}), bf16[8,16,2304]{2,1,0:T(8,128)(2,1)S(1)}, u32[]{:S(2)}, u32[]{:S(2)}) %all-to-all-start.2) | async-done | bytes 589856 | tf_op jit(solution)/shard_map/all_to_all | solution.py:184
  143.0 0.3 convolution_multiply_fusion
  143.3 1.0 fusion.1
  (4 shorter events, 0.0 us)
Async XLA Ops:
  0.0 1.6 %copy-start = (bf16[288,2304]{1,0:T(8,128)(2,1)S(1)}, bf16[288,2304]{1,0:T(8,128)(2,1)}, u32[]{:S(2)}) copy-start(bf16[288,2304]{1,0:T(8,128)(2,1)} %param.11) | copy-start | bytes 3981316
  0.0 1.2 copy-start.1
  3.5 7.2 %copy-start.4 = (s32[32,2]{0,1:T(2,128)S(1)}, s32[32,2]{0,1:T(2,128)}, u32[]{:S(2)}) copy-start(s32[32,2]{0,1:T(2,128)} %param.16) | copy-start | bytes 772
  3.5 38.8 %all-to-all-start = ((f16[8,32,2304]{2,1,0:T(8,128)(2,1)}), f16[8,32,2304]{2,1,0:T(8,128)(2,1)S(1)}, u32[]{:S(2)}, u32[]{:S(2)}) async-start(f16[8,32,2304]{2,1,0:T(8,128)(2,1)} %bitcast.32), calls=%async_computation | async-start | bytes 2359296 | tf_op jit(solution)/shard_map/all_to_all | solution.py:138
  10.7 31.7 %copy-start.2 = (f32[32,2304]{1,0:T(8,128)S(1)}, f32[32,2304]{1,0:T(8,128)}, u32[]{:S(2)}) copy-start(f32[32,2304]{1,0:T(8,128)} %param.10) | copy-start | bytes 884740
  11.5 31.1 %copy-start.3 = (f32[2304]{0:T(1024)S(1)}, f32[2304]{0:T(1024)}, u32[]{:S(2)}) copy-start(f32[2304]{0:T(1024)} %param.12) | copy-start | bytes 27652
  64.8 18.1 %collective-permute-start = (bf16[128,2304]{1,0:T(8,128)(2,1)S(1)}, bf16[128,2304]{1,0:T(8,128)(2,1)S(1)}, u32[]{:S(2)}, u32[]{:S(2)}) collective-permute-start(bf16[128,2304]{1,0:T(8,128)(2,1)S(1)} %bitcast.22), channel_id=1, source_target_pairs={{0,1},{1,2},{2,3},{3,0},{4,5},{5,6},{6,7},{7,4},{8,9},{9,10},{10,1... | collective-permute-start | bytes 1769480 | tf_op jit(solution)/shard_map/ppermute | solution.py:163
  68.2 26.6 %collective-permute-start.1 = (bf16[128,2304]{1,0:T(8,128)(2,1)S(1)}, bf16[128,2304]{1,0:T(8,128)(2,1)S(1)}, u32[]{:S(2)}, u32[]{:S(2)}) collective-permute-start(bf16[128,2304]{1,0:T(8,128)(2,1)S(1)} %bitcast.23), channel_id=1, source_target_pairs={{0,3},{1,0},{2,1},{3,2},{4,7},{5,4},{6,5},{7,6},{8,11},{9,8},{10,9... | collective-permute-start | bytes 1769480 | tf_op jit(solution)/shard_map/ppermute | solution.py:163
  79.1 27.9 %collective-permute-start.4 = (bf16[128,2304]{1,0:T(8,128)(2,1)S(1)}, bf16[128,2304]{1,0:T(8,128)(2,1)S(1)}, u32[]{:S(2)}, u32[]{:S(2)}) collective-permute-start(bf16[128,2304]{1,0:T(8,128)(2,1)S(1)} %bitcast.25), channel_id=1, source_target_pairs={{0,2},{1,3},{2,0},{3,1},{4,6},{5,7},{6,4},{7,5},{8,10},{9,11},{10,... | collective-permute-start | bytes 1769480 | tf_op jit(solution)/shard_map/ppermute | solution.py:163
  96.9 25.7 %collective-permute-start.2 = (bf16[128,2304]{1,0:T(8,128)(2,1)S(1)}, bf16[128,2304]{1,0:T(8,128)(2,1)S(1)}, u32[]{:S(2)}, u32[]{:S(2)}) collective-permute-start(bf16[128,2304]{1,0:T(8,128)(2,1)S(1)} %shard_map.94), channel_id=1, source_target_pairs={{0,3},{1,0},{2,1},{3,2},{4,7},{5,4},{6,5},{7,6},{8,11},{9,8},{10,9... | collective-permute-start | bytes 1769480 | tf_op jit(solution)/shard_map/ppermute | solution.py:163
  105.1 19.3 %collective-permute-start.3 = (bf16[128,2304]{1,0:T(8,128)(2,1)S(1)}, bf16[128,2304]{1,0:T(8,128)(2,1)S(1)}, u32[]{:S(2)}, u32[]{:S(2)}) collective-permute-start(bf16[128,2304]{1,0:T(8,128)(2,1)S(1)} %shard_map.95), channel_id=1, source_target_pairs={{0,1},{1,2},{2,3},{3,0},{4,5},{5,6},{6,7},{7,4},{8,9},{9,10},{10,1... | collective-permute-start | bytes 1769480 | tf_op jit(solution)/shard_map/ppermute | solution.py:163
  109.2 15.3 %collective-permute-start.5 = (bf16[128,2304]{1,0:T(8,128)(2,1)S(1)}, bf16[128,2304]{1,0:T(8,128)(2,1)S(1)}, u32[]{:S(2)}, u32[]{:S(2)}) collective-permute-start(bf16[128,2304]{1,0:T(8,128)(2,1)S(1)} %shard_map.96), channel_id=1, source_target_pairs={{0,2},{1,3},{2,0},{3,1},{4,6},{5,7},{6,4},{7,5},{8,10},{9,11},{10,... | collective-permute-start | bytes 1769480 | tf_op jit(solution)/shard_map/ppermute | solution.py:163
  125.4 3.7 %copy-start.5 = (f32[32,2]{0,1:T(2,128)S(1)}, f32[32,2]{0,1:T(2,128)}, u32[]{:S(2)}) copy-start(f32[32,2]{0,1:T(2,128)} %param.17) | copy-start | bytes 772
  125.4 17.6 %all-to-all-start.2 = ((bf16[8,16,2304]{2,1,0:T(8,128)(2,1)}), bf16[8,16,2304]{2,1,0:T(8,128)(2,1)S(1)}, u32[]{:S(2)}, u32[]{:S(2)}) async-start(bf16[8,16,2304]{2,1,0:T(8,128)(2,1)} %bitcast.11), calls=%async_computation.2 | async-start | bytes 1179648 | tf_op jit(solution)/shard_map/all_to_all | solution.py:184
